TPU v7x, 256 devices: a whole 4x4x8 slice. The times are simulated.
256 devices in a mesh: fsdp: 16 (over y, z_lo, core), uly: 4 (over x), blk: 4 (over z_hi).
Axes of the slice: x: 4, y: 4, z: 8 (z_hi: 4, z_lo: 2; z = z_hi * 2 + z_lo), core: 2. Of those that a mesh axis runs over, the one named last changes fastest.
Arguments:
- latents: bfloat16 [16, 3072, 3072], P('fsdp', ('uly', 'blk')), may hold values from -40 to 40
- sampler_noise: bfloat16 [16, 3072, 3072], P('fsdp', ('uly', 'blk')), may hold values from -6 to 6
- query_key_value_weight: bfloat16 [3, 3072, 1536], P(None, 'fsdp', 'uly'), may hold values from -0.375 to 0.375
- output_weight: bfloat16 [3072, 1536], P('fsdp', 'uly'), may hold values from -0.15625 to 0.15625
- adapter_down_map: bfloat16 [64, 1536], P(None, 'uly'), may hold values from -0.15625 to 0.15625
- adapter_up_map: bfloat16 [64, 3072], replicated, may hold values from -0.75 to 0.75
- valid_token_count: int32 [16], P('fsdp'), may hold values from 1536 to 3072
- advantage: float32 [16], P('fsdp'), may hold values from -3 to 3
- timestep_index: int32 [1], replicated, may hold values from 1 to 15
Outputs:
- next_latents: bfloat16 [16, 3072, 3072], P('fsdp', ('uly', 'blk'))
- log_ratio: float32 [16], P('fsdp')
- grad_down: float32 [64, 1536], P(None, 'uly')
- grad_up: float32 [64, 3072], replicated
All inputs are finite; a program needn't handle non-finite values.
Results may differ from a plain program's by a relative error of at most 0.0055.
The roundings to bfloat16 on the way count: a program that leaves them out, or rounds other values in their place, can miss the bound.
Values may be sent and summed in bfloat16 or wider, within the bound.
No kernel may reach another device: no remote copies, remote signals or barrier semaphores. Data moves between devices by JAX's collectives and lax.ppermute only.
A program may use at most 128 MiB of HBM per device.

v0:
```python
import math

import jax
import jax.numpy as jnp
from jax import lax
from jax.experimental import pallas as pl
from jax.experimental.pallas import tpu as pltpu
from jax.sharding import PartitionSpec as P


HEAD_SIZE = 128
STEPS = 16

noise_level = 0.7
loss_scale = 4194304.0
rms_eps = 1e-06


smem = pl.BlockSpec(memory_space=pltpu.SMEM)
vmem = pl.BlockSpec(memory_space=pltpu.VMEM)
last_axis = (((1,), (1,)), ((), ()))
first_axis = (((0,), (0,)), ((), ()))


def shift(x, axis, step):
    n = lax.axis_size(axis)
    return lax.ppermute(x, axis, [(i, (i + step) % n) for i in range(n)])


def exchange(x, axis, mask):
    n = lax.axis_size(axis)
    return lax.ppermute(x, axis, [(i, i ^ mask) for i in range(n)])


def after(x, *earlier):
    return lax.optimization_barrier((x,) + earlier)[0]


def four_sum(parts):
    return (parts[0] + parts[1]) + (parts[2] + parts[3])


def project_body(ints_ref, own_ref, left_ref, right_ref, up_ref, down_ref, w_ref, out_ref, all_ref):
    rows = own_ref.shape[0]
    half = rows // 2

    @pl.when(pl.program_id(0) == 0)
    def _():
        odd = lax.rem(ints_ref[0], 2)
        left = pl.multiple_of((3 - 2 * odd) * rows, half)
        right = pl.multiple_of((1 + 2 * odd) * rows, half)
        all_ref[:rows] = own_ref[...]
        all_ref[pl.ds(left, half)] = left_ref[...]
        all_ref[pl.ds(left + half, half)] = up_ref[half:]
        all_ref[pl.ds(right, half)] = down_ref[half:]
        all_ref[pl.ds(right + half, half)] = right_ref[...]
        all_ref[2 * rows : 2 * rows + half] = up_ref[:half]
        all_ref[2 * rows + half : 3 * rows] = down_ref[:half]

    out_ref[...] = jnp.dot(
        all_ref[...], w_ref[...], preferred_element_type=jnp.float32
    ).astype(jnp.bfloat16)


def query_body(all_ref, w_ref, out_ref):
    out_ref[...] = jnp.dot(
        all_ref[...], w_ref[...], preferred_element_type=jnp.float32
    ).astype(jnp.bfloat16)


def attention_body(q_ref, bias_ref, *refs):
    blocks, outs, (pairs_ref, scores_ref, acc_ref) = refs[:-7], refs[-7:-3], refs[-3:]
    scale = math.log2(math.e) / math.sqrt(HEAD_SIZE)
    at = 0
    for ref in blocks:
        pairs_ref[at : at + ref.shape[0]] = ref[...]
        at += ref.shape[0]
    chunk = scores_ref.shape[2]
    count = scores_ref.shape[0]
    rows = q_ref.shape[0]

    def score(c, top):
        start = pl.multiple_of(c * chunk, chunk)
        s = lax.dot_general(
            q_ref[...],
            pairs_ref[pl.ds(start, chunk), :HEAD_SIZE],
            last_axis,
            preferred_element_type=jnp.float32,
        )
        s = s + bias_ref[:, pl.ds(start, chunk)]
        scores_ref[c] = s
        for col in range(0, chunk, 128):
            top = jnp.maximum(top, s[:, col : col + 128])
        return top

    top = lax.fori_loop(0, count, score, jnp.full((rows, 128), -jnp.inf, jnp.float32))
    top = jnp.max(top, -1, keepdims=True) * scale
    acc_ref[...] = jnp.zeros_like(acc_ref)

    def collect(c, total):
        start = pl.multiple_of(c * chunk, chunk)
        p = jnp.exp2(scores_ref[c] * scale - top)
        for col in range(0, chunk, 128):
            total = total + p[:, col : col + 128]
        acc_ref[...] += jnp.dot(
            p.astype(jnp.bfloat16),
            pairs_ref[pl.ds(start, chunk), HEAD_SIZE:],
            preferred_element_type=jnp.float32,
        )
        return total

    total = lax.fori_loop(0, count, collect, jnp.zeros((rows, 128), jnp.float32))
    out = (acc_ref[...] / jnp.sum(total, -1, keepdims=True)).astype(jnp.bfloat16)
    seg = rows // len(outs)
    for k, ref in enumerate(outs):
        ref[...] = out[k * seg : (k + 1) * seg]


def attend(query_rows, first_head, heads, blocks, bias):
    rows = query_rows.shape[0]
    keys = bias.shape[1]
    seg = rows // 4
    chunk = 256

    def spec(array, place):
        return pl.BlockSpec((None,) + array.shape[1:], lambda i: (i + place, 0, 0))

    return pl.pallas_call(
        attention_body,
        out_shape=[jax.ShapeDtypeStruct((seg, heads * HEAD_SIZE), jnp.bfloat16)] * 4,
        grid=(heads,),
        in_specs=[
            pl.BlockSpec((rows, HEAD_SIZE), lambda i: (0, i + first_head)),
            pl.BlockSpec(bias.shape, lambda i: (0, 0)),
        ]
        + [spec(array, place) for array, place in blocks],
        out_specs=[pl.BlockSpec((seg, HEAD_SIZE), lambda i: (0, i))] * 4,
        scratch_shapes=[
            pltpu.VMEM((keys, 2 * HEAD_SIZE), jnp.bfloat16),
            pltpu.VMEM((keys // chunk, rows, chunk), jnp.float32),
            pltpu.VMEM((rows, HEAD_SIZE), jnp.float32),
        ],
        name="attend",
    )(query_rows, bias, *[array for array, _ in blocks])


def standard_body(ints_ref, gain_ref, down_ref, up_ref, noise_ref, *refs):
    pieces, own_ref, narrow_ref, masked_ref, log_ref = refs[:-4], *refs[-4:]
    rows, width = noise_ref.shape
    at = 0
    for ref in pieces:
        own_ref[:, at : at + ref.shape[1]] = ref[...]
        at += ref.shape[1]
    narrow = lax.dot_general(
        own_ref[...], down_ref[...], last_axis, preferred_element_type=jnp.float32
    ).astype(jnp.bfloat16)
    narrow_ref[...] = narrow
    position = ints_ref[0] + lax.broadcasted_iota(jnp.int32, (rows, 1), 0)
    keep = position < ints_ref[1]
    chunk = 512

    def step(c, total):
        start = pl.multiple_of(c * chunk, chunk)
        change = jnp.dot(
            narrow_ref[...], up_ref[:, pl.ds(start, chunk)], preferred_element_type=jnp.float32
        )
        noise = noise_ref[:, pl.ds(start, chunk)].astype(jnp.float32)
        standard = noise + gain_ref[0] * change
        masked_ref[:, pl.ds(start, chunk)] = jnp.where(keep, standard, 0.0).astype(jnp.bfloat16)
        terms = jnp.where(keep, noise * noise - standard * standard, 0.0)
        for col in range(0, chunk, 128):
            total = total + terms[:, col : col + 128]
        return total

    total = lax.fori_loop(0, width // chunk, step, jnp.zeros((rows, 128), jnp.float32))
    log_ref[...] = jnp.full(log_ref.shape, jnp.sum(total))


def products_body(ints_ref, narrow_ref, masked_ref, up_ref, own_ref, log_ref, *outs):
    width = masked_ref.shape[1]
    count = len(outs)
    columns = width // count
    own_columns = own_ref.shape[1] // count
    low_grad = lax.dot_general(
        masked_ref[...], up_ref[...], last_axis, preferred_element_type=jnp.float32
    ).astype(jnp.bfloat16)
    down = lax.dot_general(
        low_grad, own_ref[...], first_axis, preferred_element_type=jnp.float32
    )
    for k, out in enumerate(outs):
        start = pl.multiple_of(jnp.bitwise_xor(ints_ref[0], k) * columns, 128)
        out[:, :columns] = lax.dot_general(
            narrow_ref[...],
            masked_ref[:, pl.ds(start, columns)],
            first_axis,
            preferred_element_type=jnp.float32,
        )
        out[:, columns : columns + own_columns] = down[:, k * own_columns : (k + 1) * own_columns]
        out[:, columns + own_columns :] = jnp.broadcast_to(
            log_ref[:1], (out.shape[0], log_ref.shape[1])
        )


def rows_body(ints_ref, *refs):
    parts, up_ref, down_ref = refs[:-2], *refs[-2:]
    rows = parts[0].shape[0]
    columns = up_ref.shape[1]
    for k, ref in enumerate(parts):
        start = pl.multiple_of(jnp.bitwise_xor(ints_ref[0], k) * rows, 8)
        up_ref[pl.ds(start, rows)] = ref[:, :columns]
        down_ref[pl.ds(start, rows)] = ref[:, columns:]


def columns_body(ints_ref, *refs):
    parts, out_ref = refs[:-1], refs[-1]
    columns = parts[0].shape[1]
    for k, ref in enumerate(parts):
        start = pl.multiple_of(jnp.bitwise_xor(ints_ref[0], k) * columns, 128)
        out_ref[:, pl.ds(start, columns)] = ref[...]


def move_body(scalars_ref, own_ref, w_ref, latents_ref, noise_ref, out_ref):
    velocity = lax.dot_general(
        own_ref[...], w_ref[...], last_axis, preferred_element_type=jnp.float32
    )
    current = latents_ref[...].astype(jnp.float32)
    moved = current - scalars_ref[0] * (
        scalars_ref[1] * velocity + noise_level**2 * current / scalars_ref[2]
    )
    out_ref[...] = (moved + scalars_ref[3] * noise_ref[...].astype(jnp.float32)).astype(
        jnp.bfloat16
    )


def shards(
    latents,
    sampler_noise,
    query_key_value_weight,
    output_weight,
    adapter_down_map,
    adapter_up_map,
    valid_token_count,
    advantage,
    timestep_index,
):
    uly_count = lax.axis_size("uly")
    blk_count = lax.axis_size("blk")
    fsdp_count = lax.axis_size("fsdp")
    uly_id = lax.axis_index("uly")
    blk_id = lax.axis_index("blk")
    uly_int = jnp.reshape(uly_id, (1,)).astype(jnp.int32)
    blk_int = jnp.reshape(blk_id, (1,)).astype(jnp.int32)
    limit = valid_token_count[0]
    rank = adapter_down_map.shape[0]

    current = latents[0].astype(jnp.float32)
    rows = current.shape[0]
    width = current.shape[1]
    normed = (current * lax.rsqrt(jnp.mean(current * current, -1, keepdims=True) + rms_eps)).astype(
        jnp.bfloat16
    )
    heads_here = query_key_value_weight.shape[2] // HEAD_SIZE
    local_columns = heads_here * HEAD_SIZE
    pair = 2 * HEAD_SIZE
    group_rows = uly_count * rows

    pieces = []
    for h in range(heads_here):
        cols = slice(h * HEAD_SIZE, (h + 1) * HEAD_SIZE)
        pieces += [query_key_value_weight[1][:, cols], query_key_value_weight[2][:, cols]]
    pieces.append(query_key_value_weight[0])
    weight_rows = lax.all_gather(jnp.concatenate(pieces, 1), "fsdp", axis=0, tiled=True)

    half = rows // 2
    left = shift(normed[:half], "uly", 1)
    right = shift(normed[half:], "uly", -1)
    second, first, _, _ = lax.optimization_barrier((normed[half:], normed[:half], left, right))
    up = shift(jnp.concatenate((left, second), 0), "uly", 1)
    down = shift(jnp.concatenate((right, first), 0), "uly", -1)

    maps = after(jnp.concatenate((output_weight, adapter_down_map), 0), up, down)
    maps = jnp.concatenate([maps] + [exchange(maps, "uly", k) for k in (1, 2, 3)], 1)
    output_columns, down_full = maps[: output_weight.shape[0]], maps[output_weight.shape[0] :]

    key_values, gathered = pl.pallas_call(
        project_body,
        out_shape=(
            jax.ShapeDtypeStruct((heads_here, group_rows, pair), jnp.bfloat16),
            jax.ShapeDtypeStruct((group_rows, width), jnp.bfloat16),
        ),
        grid=(heads_here,),
        in_specs=[smem] + [vmem] * 5 + [pl.BlockSpec((width, pair), lambda h: (0, h))],
        out_specs=(
            pl.BlockSpec((None, group_rows, pair), lambda h: (h, 0, 0)),
            pl.BlockSpec((group_rows, width), lambda h: (0, 0)),
        ),
        name="project",
    )(uly_int, normed, left, right, up, down, weight_rows)
    query_rows = pl.pallas_call(
        query_body,
        out_shape=jax.ShapeDtypeStruct((group_rows, local_columns), jnp.bfloat16),
        grid=(1,),
        in_specs=[
            pl.BlockSpec((group_rows, width), lambda i: (0, 0)),
            pl.BlockSpec((width, local_columns), lambda i: (0, 2)),
        ],
        out_specs=pl.BlockSpec((group_rows, local_columns), lambda i: (0, 0)),
        name="query",
    )(gathered, weight_rows)

    key_index = jnp.arange(blk_count * group_rows, dtype=jnp.int32)
    step = key_index // group_rows
    key_blk = (blk_id + jnp.where(step == 0, 0, jnp.where(step == 1, 3, step - 1))) % blk_count
    key_pos = (
        (uly_id ^ (key_index % group_rows // rows)) * blk_count + key_blk
    ) * rows + key_index % rows
    bias = jnp.where(key_pos < limit, 0.0, -1e30).astype(jnp.float32)[None]

    middle = group_rows // 2
    firsts, seconds = key_values[:, :middle], key_values[:, middle:]
    lead = heads_here - 1

    def wave(up_part, down_part):
        up_part, down_part = lax.optimization_barrier((up_part, down_part))
        up_part = shift(up_part, "blk", 1)
        down_part = shift(down_part, "blk", -1)
        return up_part, down_part

    def join(*parts):
        return jnp.concatenate(parts, 0)

    up_0, down_0 = wave(firsts[:lead], seconds[:lead])
    up_1, down_1 = wave(
        join(up_0, seconds[:lead], firsts[lead:]), join(down_0, firsts[:lead], seconds[lead:])
    )
    up_2, down_2 = wave(
        join(up_1[2 * lead :], seconds[lead:]), join(down_1[2 * lead :], firsts[lead:])
    )
    weight_full = lax.all_gather(after(output_columns, up_1, down_1), "fsdp", axis=0, tiled=True)

    def others(segs):
        return [segs[0]] + [exchange(segs[k], "uly", k) for k in (1, 2, 3)]

    segs = attend(
        query_rows,
        0,
        lead,
        (
            (key_values, 0),
            (up_0, 0),
            (up_1, lead),
            (down_1, lead),
            (down_0, 0),
            (up_1, 0),
            (down_1, 0),
        ),
        bias,
    )
    lead_pieces = others(segs)
    segs = attend(
        query_rows,
        lead,
        1,
        (
            (key_values, lead),
            (up_1, 2 * lead),
            (up_2, 1),
            (down_2, 1),
            (down_1, 2 * lead),
            (up_2, 0),
            (down_2, 0),
        ),
        bias,
    )
    last_pieces = others(segs)

    step_float = timestep_index[0].astype(jnp.float32)
    time_now = 1.0 - step_float / STEPS
    step_size = 1.0 / STEPS
    noise_std = noise_level * jnp.sqrt(time_now / (1.0 - time_now))
    drift_gain = 1.0 + noise_level**2 / 2.0
    ratio_gain = jnp.sqrt(step_size) * drift_gain / noise_std
    valid_len = limit.astype(jnp.float32)
    ints = jnp.stack([(uly_id * blk_count + blk_id) * rows, limit]).astype(jnp.int32)
    pieces = [p for both in zip(lead_pieces, last_pieces) for p in both]
    own_heads, narrow_projection, masked, log_tile = pl.pallas_call(
        standard_body,
        out_shape=(
            jax.ShapeDtypeStruct((rows, uly_count * local_columns), jnp.bfloat16),
            jax.ShapeDtypeStruct((rows, rank), jnp.bfloat16),
            jax.ShapeDtypeStruct((rows, width), jnp.bfloat16),
            jax.ShapeDtypeStruct((8, 128), jnp.float32),
        ),
        in_specs=[smem, smem] + [vmem] * (3 + len(pieces)),
        out_specs=(vmem,) * 4,
        name="standard",
    )(ints, jnp.reshape(ratio_gain, (1,)), down_full, adapter_up_map, sampler_noise[0], *pieces)

    up_columns = width // uly_count
    share_columns = up_columns + local_columns
    shares = pl.pallas_call(
        products_body,
        out_shape=[jax.ShapeDtypeStruct((rank, share_columns + 128), jnp.float32)] * uly_count,
        in_specs=[smem] + [vmem] * 5,
        out_specs=[vmem] * uly_count,
        name="products",
    )(uly_int, narrow_projection, masked, adapter_up_map, own_heads, log_tile)

    summed = four_sum([shares[0]] + [exchange(shares[k], "uly", k) for k in (1, 2, 3)])
    part = rank // blk_count

    def rows_of(k):
        return lax.dynamic_slice_in_dim(summed, (blk_id ^ k) * part, part, 0)

    summed = four_sum([rows_of(0)] + [exchange(rows_of(k), "blk", k) for k in (1, 2, 3)])
    log_ratio = summed[0, share_columns] / (2.0 * valid_len * width)
    coef = (
        loss_scale
        * advantage[0]
        * jnp.exp(log_ratio)
        * ratio_gain
        / (fsdp_count * valid_len * width)
    )
    summed = summed[:, :share_columns] * coef
    for unit in (4, 1):
        summed = four_sum([summed] + [exchange(summed, "fsdp", unit * k) for k in (1, 2, 3)])

    tile = 512
    scalars = jnp.stack(
        [
            jnp.float32(step_size),
            jnp.float32(drift_gain),
            2.0 * (1.0 - time_now),
            noise_std * jnp.sqrt(step_size),
        ]
    )
    token_tile = pl.BlockSpec((rows, tile), lambda i: (0, i))
    next_latents = pl.pallas_call(
        move_body,
        out_shape=jax.ShapeDtypeStruct((rows, width), jnp.bfloat16),
        grid=(width // tile,),
        in_specs=[
            smem,
            pl.BlockSpec(own_heads.shape, lambda i: (0, 0)),
            pl.BlockSpec((tile, own_heads.shape[1]), lambda i: (i, 0)),
            token_tile,
            token_tile,
        ],
        out_specs=token_tile,
        name="move",
    )(scalars, own_heads, weight_full, latents[0], sampler_noise[0])
    parts = [exchange(summed, "blk", k) for k in (1, 2, 3)]
    next_latents, *parts = lax.optimization_barrier((next_latents, *parts))
    up_mine, grad_down = pl.pallas_call(
        rows_body,
        out_shape=(
            jax.ShapeDtypeStruct((rank, up_columns), jnp.float32),
            jax.ShapeDtypeStruct((rank, local_columns), jnp.float32),
        ),
        in_specs=[smem] + [vmem] * 4,
        out_specs=(vmem,) * 2,
        name="rows",
    )(blk_int, summed, *parts)
    grad_up = pl.pallas_call(
        columns_body,
        out_shape=jax.ShapeDtypeStruct((rank, width), jnp.float32),
        in_specs=[smem] + [vmem] * 4,
        out_specs=vmem,
        name="columns",
    )(uly_int, up_mine, *[exchange(up_mine, "uly", k) for k in (1, 2, 3)])
    return (next_latents[None], jnp.reshape(log_ratio, (1,)), grad_down, grad_up)


def solution(mesh):
    placed = (
        P("fsdp", ("uly", "blk"), None),
        P("fsdp", ("uly", "blk"), None),
        P(None, "fsdp", "uly"),
        P("fsdp", "uly"),
        P(None, "uly"),
        P(),
        P("fsdp"),
        P("fsdp"),
        P(),
    )

    return jax.shard_map(
        shards,
        mesh=mesh,
        in_specs=placed,
        out_specs=(P("fsdp", ("uly", "blk"), None), P("fsdp"), P(None, "uly"), P()),
        check_vma=False,
    )
```

profile of v0, /device:TPU:1, one launch (start us, length us, event | category | flops | bytes accessed | tf_op | source)
XLA Modules:
  0.0 307.0 jit_solution(16622089320170303648)
XLA Ops:
  15.2 10.8 %collective-permute-done.left_ref = bf16[96,3072]{1,0:T(8,128)(2,1)S(1)} collective-permute-done((bf16[96,3072]{1,0:T(8,128)(2,1)S(1)}, bf16[96,3072]{1,0:T(8,128)(2,1)S(1)}, u32[]{:S(2)}, u32[]{:S(2)}) %collective-permute-start) | collective-permute-done | bytes 589856 | tf_op jit(solution)/shard_map/ppermute | solution.py:27
  31.8 22.9 %collective-permute-done.3.down_ref = bf16[192,3072]{1,0:T(8,128)(2,1)S(1)} collective-permute-done((bf16[192,3072]{1,0:T(8,128)(2,1)}, bf16[192,3072]{1,0:T(8,128)(2,1)S(1)}, u32[]{:S(2)}, u32[]{:S(2)}) %collective-permute-start.3) | collective-permute-done | bytes 1179680 | tf_op jit(solution)/shard_map/ppermute | solution.py:27
  54.7 3.0 collective-permute-done.2.up_ref
  57.7 5.3 %all-gather.3.cloned.1.call-done.w_ref = bf16[3072,1152]{1,0:T(8,128)(2,1)} async-done(((bf16[192,1152]{1,0:T(8,128)(2,1)}), bf16[3072,1152]{1,0:T(8,128)(2,1)}) %all-gather.3.cloned.1.call-update) | async-done | bytes 7077904 | tf_op jit(solution)/shard_map/all_gather | solution.py:272
  63.0 9.3 %project.1 = (bf16[3,768,256]{2,1,0:T(8,128)(2,1)}, bf16[768,3072]{1,0:T(8,128)(2,1)}) custom-call(s32[1]{0:T(128)} %bitcast.7.ints_ref, bf16[192,3072]{1,0:T(8,128)(2,1)} %copy-done, bf16[96,3072]{1,0:T(8,128)(2,1)} %copy-done.4, bf16[96,3072]{1,0:T(8,128)(2,1)} %copy-done.5, bf16[192,3072]{1,0:T(8,128)(2,1)} %copy-done.11, bf16[192,3072]{1,0:T(8,128)(2,1)} %copy-done.10, ...), custom_call_target="tpu_custom_call" | custom-call | tf_op jit(solution)/shard_map/project/pallas_call | solution.py:285
  73.5 3.8 %collective-permute-start.8 = (bf16[2,384,256]{2,1,0:T(8,128)(2,1)S(1)}, bf16[2,384,256]{2,1,0:T(8,128)(2,1)S(1)}, u32[]{:S(2)}, u32[]{:S(2)}) collective-permute-start(bf16[2,384,256]{2,1,0:T(8,128)(2,1)S(1)} %get-tuple-element.44), channel_id=1, source_target_pairs={{0,3},{1,0},{2,1},{3,2},{4,7},{5,4},{6,5},{7,6},{8,11},{9,8},{10,9... | collective-permute-start | bytes 1179656 | tf_op jit(solution)/shard_map/ppermute | solution.py:27
  78.4 14.7 %collective-permute-done.8.refs_4_ = bf16[2,384,256]{2,1,0:T(8,128)(2,1)S(1)} collective-permute-done((bf16[2,384,256]{2,1,0:T(8,128)(2,1)S(1)}, bf16[2,384,256]{2,1,0:T(8,128)(2,1)S(1)}, u32[]{:S(2)}, u32[]{:S(2)}) %collective-permute-start.8) | collective-permute-done | bytes 393248 | tf_op jit(solution)/shard_map/ppermute | solution.py:27
  95.4 3.2 %collective-permute-start.9 = (bf16[5,384,256]{2,1,0:T(8,128)(2,1)}, bf16[5,384,256]{2,1,0:T(8,128)(2,1)S(1)}, u32[]{:S(2)}, u32[]{:S(2)}) collective-permute-start(bf16[5,384,256]{2,1,0:T(8,128)(2,1)} %pad_maximum_fusion.2), channel_id=1, source_target_pairs={{0,1},{1,2},{2,3},{3,0},{4,5},{5,6},{6,7},{7,4},{8,9},{9,10},{10,1... | collective-permute-start | bytes 2949128 | tf_op jit(solution)/shard_map/ppermute | solution.py:27
  99.0 3.3 %collective-permute-start.4 = (bf16[256,384]{1,0:T(8,128)(2,1)S(1)}, bf16[256,384]{1,0:T(8,128)(2,1)S(1)}, u32[]{:S(2)}, u32[]{:S(2)}) collective-permute-start(bf16[256,384]{1,0:T(8,128)(2,1)S(1)} %pad_maximum_fusion.6), channel_id=1, source_target_pairs={{0,4},{4,0},{8,12},{12,8},{1,5},{5,1},{9,13},{13,9},{2,6},{6,2},{1... | collective-permute-start | bytes 589832 | tf_op jit(solution)/shard_map/ppermute | solution.py:32
  106.1 6.9 %collective-permute-done.5 = bf16[256,384]{1,0:T(8,128)(2,1)S(1)} collective-permute-done((bf16[256,384]{1,0:T(8,128)(2,1)S(1)}, bf16[256,384]{1,0:T(8,128)(2,1)S(1)}, u32[]{:S(2)}, u32[]{:S(2)}) %collective-permute-start.5) | collective-permute-done | bytes 196640 | tf_op jit(solution)/shard_map/ppermute | solution.py:32
  114.0 4.7 %collective-permute-done.9.refs_2_.refs_5_.refs_1_ = bf16[5,384,256]{2,1,0:T(8,128)(2,1)S(1)} collective-permute-done((bf16[5,384,256]{2,1,0:T(8,128)(2,1)}, bf16[5,384,256]{2,1,0:T(8,128)(2,1)S(1)}, u32[]{:S(2)}, u32[]{:S(2)}) %collective-permute-start.9) | collective-permute-done | bytes 983072 | tf_op jit(solution)/shard_map/ppermute | solution.py:27
  118.7 9.3 %collective-permute-done.10.refs_3_.refs_6_.refs_4_ = bf16[5,384,256]{2,1,0:T(8,128)(2,1)S(1)} collective-permute-done((bf16[5,384,256]{2,1,0:T(8,128)(2,1)}, bf16[5,384,256]{2,1,0:T(8,128)(2,1)S(1)}, u32[]{:S(2)}, u32[]{:S(2)}) %collective-permute-start.10) | collective-permute-done | bytes 983072 | tf_op jit(solution)/shard_map/ppermute | solution.py:27
  134.1 6.5 %query.1.q_ref = bf16[768,384]{1,0:T(8,128)(2,1)} custom-call(bf16[768,3072]{1,0:T(8,128)(2,1)} %get-tuple-element.41.all_ref, bf16[3072,1152]{1,0:T(8,128)(2,1)} %all-gather.3.cloned.1.call-done.w_ref), custom_call_target="tpu_custom_call" | custom-call | tf_op jit(solution)/shard_map/query/pallas_call | solution.py:299
  140.6 18.1 %attend.2 = (bf16[192,256]{1,0:T(8,128)(2,1)}, bf16[192,256]{1,0:T(8,128)(2,1)}, bf16[192,256]{1,0:T(8,128)(2,1)}, bf16[192,256]{1,0:T(8,128)(2,1)}) custom-call(bf16[768,384]{1,0:T(8,128)(2,1)} %query.1.q_ref, f32[1,3072]{1,0:T(1,128)} %compare_select_fusion.2.bias_ref, bf16[3,768,256]{2,1,0:T(8,128)(2,1)} %get-tuple-element.42.refs_0_, ...), custom_call_target="tpu_custom_call" | custom-call | tf_op jit(solution)/shard_map/attend/pallas_call | solution.py:128
  158.8 8.2 %collective-permute-start.13 = (bf16[192,256]{1,0:T(8,128)(2,1)}, bf16[192,256]{1,0:T(8,128)(2,1)S(1)}, u32[]{:S(2)}, u32[]{:S(2)}) collective-permute-start(bf16[192,256]{1,0:T(8,128)(2,1)} %get-tuple-element.51), channel_id=1, source_target_pairs={{0,4},{4,0},{8,12},{12,8},{1,5},{5,1},{9,13},{13,9},{2,6},{6,2},{1... | collective-permute-start | bytes 294920 | tf_op jit(solution)/shard_map/ppermute | solution.py:32
  171.0 10.2 %attend.3 = (bf16[192,128]{1,0:T(8,128)(2,1)}, bf16[192,128]{1,0:T(8,128)(2,1)}, bf16[192,128]{1,0:T(8,128)(2,1)}, bf16[192,128]{1,0:T(8,128)(2,1)}) custom-call(bf16[768,384]{1,0:T(8,128)(2,1)} %query.1.q_ref, f32[1,3072]{1,0:T(1,128)} %compare_select_fusion.2.bias_ref, bf16[3,768,256]{2,1,0:T(8,128)(2,1)} %get-tuple-element.42.refs_0_, ...), custom_call_target="tpu_custom_call" | custom-call | tf_op jit(solution)/shard_map/attend/pallas_call | solution.py:128
  181.3 3.6 %collective-permute-start.16 = (bf16[192,128]{1,0:T(8,128)(2,1)}, bf16[192,128]{1,0:T(8,128)(2,1)S(1)}, u32[]{:S(2)}, u32[]{:S(2)}) collective-permute-start(bf16[192,128]{1,0:T(8,128)(2,1)} %get-tuple-element.54), channel_id=1, source_target_pairs={{0,8},{4,12},{8,0},{12,4},{1,9},{5,13},{9,1},{13,5},{2,10},{6,14},... | collective-permute-start | bytes 147464 | tf_op jit(solution)/shard_map/ppermute | solution.py:32
  189.8 4.6 %standard.1 = (bf16[192,1536]{1,0:T(8,128)(2,1)}, bf16[192,64]{1,0:T(8,128)(2,1)}, bf16[192,3072]{1,0:T(8,128)(2,1)}, f32[8,128]{1,0:T(8,128)}) custom-call(s32[2]{0:T(128)} %pad_add_fusion.ints_ref, f32[1]{0:T(128)} %bitcast.4.gain_ref, bf16[64,1536]{1,0:T(8,128)(2,1)} %slice.102.down_ref, bf16[64,3072]{1,0:T(8,128)(2,1)} %up_ref.3, ...), custom_call_target="tpu_custom_call" | custom-call | tf_op jit(solution)/shard_map/standard/pallas_call | solution.py:386
  194.4 3.8 %products.1 = (f32[64,1280]{1,0:T(8,128)}, f32[64,1280]{1,0:T(8,128)}, f32[64,1280]{1,0:T(8,128)}, f32[64,1280]{1,0:T(8,128)}) custom-call(s32[1]{0:T(128)} %bitcast.7.ints_ref, bf16[192,64]{1,0:T(8,128)(2,1)} %get-tuple-element.59.narrow_ref, bf16[192,3072]{1,0:T(8,128)(2,1)} %get-tuple-element.60.masked_ref, bf16[64,3072]{1,0:T(8,128)(2,1)} %up_ref.3, ...), custom_call_target="tpu_custom_call" | custom-call | tf_op jit(solution)/shard_map/products/pallas_call | solution.py:401
  202.1 2.7 collective-permute-done.19
  204.7 3.5 %collective-permute-done.20 = f32[64,1280]{1,0:T(8,128)S(1)} collective-permute-done((f32[64,1280]{1,0:T(8,128)}, f32[64,1280]{1,0:T(8,128)S(1)}, u32[]{:S(2)}, u32[]{:S(2)}) %collective-permute-start.20) | collective-permute-done | bytes 327712 | tf_op jit(solution)/shard_map/ppermute | solution.py:32
  208.2 2.6 collective-permute-done.21
  211.9 2.7 collective-permute-start.22
  214.5 3.5 %collective-permute-start.24 = (f32[16,1280]{1,0:T(8,128)S(1)}, f32[16,1280]{1,0:T(8,128)S(1)}, u32[]{:S(2)}, u32[]{:S(2)}) collective-permute-start(f32[16,1280]{1,0:T(8,128)S(1)} %get-tuple-element.81), channel_id=1, source_target_pairs={{0,3},{1,2},{2,1},{3,0},{4,7},{5,6},{6,5},{7,4},{8,11},{9,10},{10,... | collective-permute-start | bytes 245768 | tf_op jit(solution)/shard_map/ppermute | solution.py:32
  220.2 5.9 %collective-permute-done.23 = f32[16,1280]{1,0:T(8,128)S(1)} collective-permute-done((f32[16,1280]{1,0:T(8,128)S(1)}, f32[16,1280]{1,0:T(8,128)S(1)}, u32[]{:S(2)}, u32[]{:S(2)}) %collective-permute-start.23) | collective-permute-done | bytes 81952 | tf_op jit(solution)/shard_map/ppermute | solution.py:32
  227.4 3.0 collective-permute-start.26
  230.5 8.8 %collective-permute-start.27 = (f32[16,1152]{1,0:T(8,128)S(1)}, f32[16,1152]{1,0:T(8,128)S(1)}, u32[]{:S(2)}, u32[]{:S(2)}) collective-permute-start(f32[16,1152]{1,0:T(8,128)S(1)} %slice_multiply_fusion), channel_id=1, source_target_pairs={{0,192},{16,208},{32,224},{48,240},{64,128},{80,144},{96,160},{112... | collective-permute-start | bytes 221192 | tf_op jit(solution)/shard_map/ppermute | solution.py:32
  242.5 20.9 %collective-permute-start.30 = (f32[16,1152]{1,0:T(8,128)S(1)}, f32[16,1152]{1,0:T(8,128)S(1)}, u32[]{:S(2)}, u32[]{:S(2)}) collective-permute-start(f32[16,1152]{1,0:T(8,128)S(1)} %add_add_fusion.3), channel_id=1, source_target_pairs={{0,48},{16,32},{32,16},{48,0},{64,112},{80,96},{96,80},{112,64},{1... | collective-permute-start | bytes 221192 | tf_op jit(solution)/shard_map/ppermute | solution.py:32
  269.9 2.9 collective-permute-start.31
  273.5 8.7 %move.1 = bf16[192,3072]{1,0:T(8,128)(2,1)} custom-call(f32[4]{0:T(128)} %pad_maximum_fusion.7.scalars_ref, bf16[192,1536]{1,0:T(8,128)(2,1)} %get-tuple-element.57.own_ref, bf16[3072,1536]{1,0:T(8,128)(2,1)} %all-gather.5.cloned.1.call-done.w_ref, bf16[192,3072]{1,0:T(8,128)(2,1)} %bitcast.24, bf16[192,3072]{1,0:T(8,128)(2,1)} %bitcast.26), custom_call_target="tpu_custom_call" | custom-call | tf_op jit(solution)/shard_map/move/pallas_call | solution.py:438
  284.6 2.4 collective-permute-start.36
  287.9 7.6 %collective-permute-done.36.refs_3_ = f32[64,768]{1,0:T(8,128)S(1)} collective-permute-done((f32[64,768]{1,0:T(8,128)}, f32[64,768]{1,0:T(8,128)S(1)}, u32[]{:S(2)}, u32[]{:S(2)}) %collective-permute-start.36) | collective-permute-done | bytes 196640 | tf_op jit(solution)/shard_map/ppermute | solution.py:32
  (152 shorter events, 60.9 us)
Async XLA Ops:
  7.2 55.8 %all-gather.3.cloned.1.call-start = ((), (), s32[]{:S(2)}) async-start(), calls=%async_computation | async-start | bytes 7520256 | tf_op jit(solution)/shard_map/all_gather | solution.py:272
  10.2 263.3 %all-gather.5.cloned.1.call-start = ((), (), s32[]{:S(2)}) async-start(), calls=%async_computation.1 | async-start | bytes 10027008 | tf_op jit(solution)/shard_map/all_gather | solution.py:339
  11.9 14.1 %collective-permute-start = (bf16[96,3072]{1,0:T(8,128)(2,1)S(1)}, bf16[96,3072]{1,0:T(8,128)(2,1)S(1)}, u32[]{:S(2)}, u32[]{:S(2)}) collective-permute-start(bf16[96,3072]{1,0:T(8,128)(2,1)S(1)} %get-tuple-element.39), channel_id=1, source_target_pairs={{0,4},{4,8},{8,12},{12,0},{1,5},{5,9},{9,13},{13,1},{2,6},{6,10},{... | collective-permute-start | bytes 1769480 | tf_op jit(solution)/shard_map/ppermute | solution.py:27
  13.9 13.7 %collective-permute-start.1 = (bf16[96,3072]{1,0:T(8,128)(2,1)S(1)}, bf16[96,3072]{1,0:T(8,128)(2,1)S(1)}, u32[]{:S(2)}, u32[]{:S(2)}) collective-permute-start(bf16[96,3072]{1,0:T(8,128)(2,1)S(1)} %get-tuple-element.38), channel_id=1, source_target_pairs={{0,12},{4,0},{8,4},{12,8},{1,13},{5,1},{9,5},{13,9},{2,14},{6,2},{... | collective-permute-start | bytes 1769480 | tf_op jit(solution)/shard_map/ppermute | solution.py:27
  28.8 25.8 %collective-permute-start.3 = (bf16[192,3072]{1,0:T(8,128)(2,1)}, bf16[192,3072]{1,0:T(8,128)(2,1)S(1)}, u32[]{:S(2)}, u32[]{:S(2)}) collective-permute-start(bf16[192,3072]{1,0:T(8,128)(2,1)} %pad_maximum_fusion.1), channel_id=1, source_target_pairs={{0,12},{4,0},{8,4},{12,8},{1,13},{5,1},{9,5},{13,9},{2,14},{6,2},{... | collective-permute-start | bytes 3538952 | tf_op jit(solution)/shard_map/ppermute | solution.py:27
  31.7 25.9 %collective-permute-start.2 = (bf16[192,3072]{1,0:T(8,128)(2,1)}, bf16[192,3072]{1,0:T(8,128)(2,1)S(1)}, u32[]{:S(2)}, u32[]{:S(2)}) collective-permute-start(bf16[192,3072]{1,0:T(8,128)(2,1)} %pad_maximum_fusion), channel_id=1, source_target_pairs={{0,4},{4,8},{8,12},{12,0},{1,5},{5,9},{9,13},{13,1},{2,6},{6,10},{... | collective-permute-start | bytes 3538952 | tf_op jit(solution)/shard_map/ppermute | solution.py:27
  73.5 19.6 %collective-permute-start.8 = (bf16[2,384,256]{2,1,0:T(8,128)(2,1)S(1)}, bf16[2,384,256]{2,1,0:T(8,128)(2,1)S(1)}, u32[]{:S(2)}, u32[]{:S(2)}) collective-permute-start(bf16[2,384,256]{2,1,0:T(8,128)(2,1)S(1)} %get-tuple-element.44), channel_id=1, source_target_pairs={{0,3},{1,0},{2,1},{3,2},{4,7},{5,4},{6,5},{7,6},{8,11},{9,8},{10,9... | collective-permute-start | bytes 1179656 | tf_op jit(solution)/shard_map/ppermute | solution.py:27
  77.3 17.0 %collective-permute-start.7 = (bf16[2,384,256]{2,1,0:T(8,128)(2,1)S(1)}, bf16[2,384,256]{2,1,0:T(8,128)(2,1)S(1)}, u32[]{:S(2)}, u32[]{:S(2)}) collective-permute-start(bf16[2,384,256]{2,1,0:T(8,128)(2,1)S(1)} %get-tuple-element.43), channel_id=1, source_target_pairs={{0,1},{1,2},{2,3},{3,0},{4,5},{5,6},{6,7},{7,4},{8,9},{9,10},{10,1... | collective-permute-start | bytes 1179656 | tf_op jit(solution)/shard_map/ppermute | solution.py:27
  95.4 23.4 %collective-permute-start.9 = (bf16[5,384,256]{2,1,0:T(8,128)(2,1)}, bf16[5,384,256]{2,1,0:T(8,128)(2,1)S(1)}, u32[]{:S(2)}, u32[]{:S(2)}) collective-permute-start(bf16[5,384,256]{2,1,0:T(8,128)(2,1)} %pad_maximum_fusion.2), channel_id=1, source_target_pairs={{0,1},{1,2},{2,3},{3,0},{4,5},{5,6},{6,7},{7,4},{8,9},{9,10},{10,1... | collective-permute-start | bytes 2949128 | tf_op jit(solution)/shard_map/ppermute | solution.py:27
  98.6 29.5 %collective-permute-start.10 = (bf16[5,384,256]{2,1,0:T(8,128)(2,1)}, bf16[5,384,256]{2,1,0:T(8,128)(2,1)S(1)}, u32[]{:S(2)}, u32[]{:S(2)}) collective-permute-start(bf16[5,384,256]{2,1,0:T(8,128)(2,1)} %pad_maximum_fusion.3), channel_id=1, source_target_pairs={{0,3},{1,0},{2,1},{3,2},{4,7},{5,4},{6,5},{7,6},{8,11},{9,8},{10,9... | collective-permute-start | bytes 2949128 | tf_op jit(solution)/shard_map/ppermute | solution.py:27
  99.0 7.1 %collective-permute-start.4 = (bf16[256,384]{1,0:T(8,128)(2,1)S(1)}, bf16[256,384]{1,0:T(8,128)(2,1)S(1)}, u32[]{:S(2)}, u32[]{:S(2)}) collective-permute-start(bf16[256,384]{1,0:T(8,128)(2,1)S(1)} %pad_maximum_fusion.6), channel_id=1, source_target_pairs={{0,4},{4,0},{8,12},{12,8},{1,5},{5,1},{9,13},{13,9},{2,6},{6,2},{1... | collective-permute-start | bytes 589832 | tf_op jit(solution)/shard_map/ppermute | solution.py:32
  102.3 10.8 %collective-permute-start.6 = (bf16[256,384]{1,0:T(8,128)(2,1)S(1)}, bf16[256,384]{1,0:T(8,128)(2,1)S(1)}, u32[]{:S(2)}, u32[]{:S(2)}) collective-permute-start(bf16[256,384]{1,0:T(8,128)(2,1)S(1)} %pad_maximum_fusion.6), channel_id=1, source_target_pairs={{0,12},{4,8},{8,4},{12,0},{1,13},{5,9},{9,5},{13,1},{2,14},{6,10},... | collective-permute-start | bytes 589832 | tf_op jit(solution)/shard_map/ppermute | solution.py:32
  104.1 8.9 %collective-permute-start.5 = (bf16[256,384]{1,0:T(8,128)(2,1)S(1)}, bf16[256,384]{1,0:T(8,128)(2,1)S(1)}, u32[]{:S(2)}, u32[]{:S(2)}) collective-permute-start(bf16[256,384]{1,0:T(8,128)(2,1)S(1)} %pad_maximum_fusion.6), channel_id=1, source_target_pairs={{0,8},{4,12},{8,0},{12,4},{1,9},{5,13},{9,1},{13,5},{2,10},{6,14},... | collective-permute-start | bytes 589832 | tf_op jit(solution)/shard_map/ppermute | solution.py:32
  129.7 39.8 %collective-permute-start.11 = (bf16[2,384,256]{2,1,0:T(8,128)(2,1)}, bf16[2,384,256]{2,1,0:T(8,128)(2,1)S(1)}, u32[]{:S(2)}, u32[]{:S(2)}) collective-permute-start(bf16[2,384,256]{2,1,0:T(8,128)(2,1)} %pad_maximum_fusion.4), channel_id=1, source_target_pairs={{0,1},{1,2},{2,3},{3,0},{4,5},{5,6},{6,7},{7,4},{8,9},{9,10},{10,1... | collective-permute-start | bytes 1179656 | tf_op jit(solution)/shard_map/ppermute | solution.py:27
  132.0 37.5 %collective-permute-start.12 = (bf16[2,384,256]{2,1,0:T(8,128)(2,1)S(1)}, bf16[2,384,256]{2,1,0:T(8,128)(2,1)S(1)}, u32[]{:S(2)}, u32[]{:S(2)}) collective-permute-start(bf16[2,384,256]{2,1,0:T(8,128)(2,1)S(1)} %pad_maximum_fusion.5), channel_id=1, source_target_pairs={{0,3},{1,0},{2,1},{3,2},{4,7},{5,4},{6,5},{7,6},{8,11},{9,8},{10,9... | collective-permute-start | bytes 1179656 | tf_op jit(solution)/shard_map/ppermute | solution.py:27
  158.8 26.1 %collective-permute-start.13 = (bf16[192,256]{1,0:T(8,128)(2,1)}, bf16[192,256]{1,0:T(8,128)(2,1)S(1)}, u32[]{:S(2)}, u32[]{:S(2)}) collective-permute-start(bf16[192,256]{1,0:T(8,128)(2,1)} %get-tuple-element.51), channel_id=1, source_target_pairs={{0,4},{4,0},{8,12},{12,8},{1,5},{5,1},{9,13},{13,9},{2,6},{6,2},{1... | collective-permute-start | bytes 294920 | tf_op jit(solution)/shard_map/ppermute | solution.py:32
  167.0 20.2 %collective-permute-start.15 = (bf16[192,256]{1,0:T(8,128)(2,1)}, bf16[192,256]{1,0:T(8,128)(2,1)S(1)}, u32[]{:S(2)}, u32[]{:S(2)}) collective-permute-start(bf16[192,256]{1,0:T(8,128)(2,1)} %get-tuple-element.53), channel_id=1, source_target_pairs={{0,8},{4,12},{8,0},{12,4},{1,9},{5,13},{9,1},{13,5},{2,10},{6,14},... | collective-permute-start | bytes 294920 | tf_op jit(solution)/shard_map/ppermute | solution.py:32
  169.3 17.9 %collective-permute-start.17 = (bf16[192,256]{1,0:T(8,128)(2,1)}, bf16[192,256]{1,0:T(8,128)(2,1)S(1)}, u32[]{:S(2)}, u32[]{:S(2)}) collective-permute-start(bf16[192,256]{1,0:T(8,128)(2,1)} %get-tuple-element.55), channel_id=1, source_target_pairs={{0,12},{4,8},{8,4},{12,0},{1,13},{5,9},{9,5},{13,1},{2,14},{6,10},... | collective-permute-start | bytes 294920 | tf_op jit(solution)/shard_map/ppermute | solution.py:32
  198.2 6.5 %collective-permute-start.19 = (f32[64,1280]{1,0:T(8,128)}, f32[64,1280]{1,0:T(8,128)S(1)}, u32[]{:S(2)}, u32[]{:S(2)}) collective-permute-start(f32[64,1280]{1,0:T(8,128)} %get-tuple-element.63), channel_id=1, source_target_pairs={{0,4},{4,0},{8,12},{12,8},{1,5},{5,1},{9,13},{13,9},{2,6},{6,2},{1... | collective-permute-start | bytes 983048 | tf_op jit(solution)/shard_map/ppermute | solution.py:32
  198.2 10.0 %collective-permute-start.20 = (f32[64,1280]{1,0:T(8,128)}, f32[64,1280]{1,0:T(8,128)S(1)}, u32[]{:S(2)}, u32[]{:S(2)}) collective-permute-start(f32[64,1280]{1,0:T(8,128)} %get-tuple-element.64), channel_id=1, source_target_pairs={{0,8},{4,12},{8,0},{12,4},{1,9},{5,13},{9,1},{13,5},{2,10},{6,14},... | collective-permute-start | bytes 983048 | tf_op jit(solution)/shard_map/ppermute | solution.py:32
  199.9 10.9 %collective-permute-start.21 = (f32[64,1280]{1,0:T(8,128)}, f32[64,1280]{1,0:T(8,128)S(1)}, u32[]{:S(2)}, u32[]{:S(2)}) collective-permute-start(f32[64,1280]{1,0:T(8,128)} %get-tuple-element.65), channel_id=1, source_target_pairs={{0,12},{4,8},{8,4},{12,0},{1,13},{5,9},{9,5},{13,1},{2,14},{6,10},... | collective-permute-start | bytes 983048 | tf_op jit(solution)/shard_map/ppermute | solution.py:32
  211.9 6.9 %collective-permute-start.22 = (f32[16,1280]{1,0:T(8,128)S(1)}, f32[16,1280]{1,0:T(8,128)S(1)}, u32[]{:S(2)}, u32[]{:S(2)}) collective-permute-start(f32[16,1280]{1,0:T(8,128)S(1)} %get-tuple-element.80), channel_id=1, source_target_pairs={{0,1},{1,0},{2,3},{3,2},{4,5},{5,4},{6,7},{7,6},{8,9},{9,8},{10,11... | collective-permute-start | bytes 245768 | tf_op jit(solution)/shard_map/ppermute | solution.py:32
  218.1 8.1 %collective-permute-start.23 = (f32[16,1280]{1,0:T(8,128)S(1)}, f32[16,1280]{1,0:T(8,128)S(1)}, u32[]{:S(2)}, u32[]{:S(2)}) collective-permute-start(f32[16,1280]{1,0:T(8,128)S(1)} %get-tuple-element.82), channel_id=1, source_target_pairs={{0,2},{1,3},{2,0},{3,1},{4,6},{5,7},{6,4},{7,5},{8,10},{9,11},{10,... | collective-permute-start | bytes 245768 | tf_op jit(solution)/shard_map/ppermute | solution.py:32
  227.4 12.3 %collective-permute-start.26 = (f32[16,1152]{1,0:T(8,128)S(1)}, f32[16,1152]{1,0:T(8,128)S(1)}, u32[]{:S(2)}, u32[]{:S(2)}) collective-permute-start(f32[16,1152]{1,0:T(8,128)S(1)} %slice_multiply_fusion), channel_id=1, source_target_pairs={{0,128},{16,144},{32,160},{48,176},{64,192},{80,208},{96,224},{112... | collective-permute-start | bytes 221192 | tf_op jit(solution)/shard_map/ppermute | solution.py:32
  230.5 10.9 %collective-permute-start.27 = (f32[16,1152]{1,0:T(8,128)S(1)}, f32[16,1152]{1,0:T(8,128)S(1)}, u32[]{:S(2)}, u32[]{:S(2)}) collective-permute-start(f32[16,1152]{1,0:T(8,128)S(1)} %slice_multiply_fusion), channel_id=1, source_target_pairs={{0,192},{16,208},{32,224},{48,240},{64,128},{80,144},{96,160},{112... | collective-permute-start | bytes 221192 | tf_op jit(solution)/shard_map/ppermute | solution.py:32
  242.5 22.9 %collective-permute-start.30 = (f32[16,1152]{1,0:T(8,128)S(1)}, f32[16,1152]{1,0:T(8,128)S(1)}, u32[]{:S(2)}, u32[]{:S(2)}) collective-permute-start(f32[16,1152]{1,0:T(8,128)S(1)} %add_add_fusion.3), channel_id=1, source_target_pairs={{0,48},{16,32},{32,16},{48,0},{64,112},{80,96},{96,80},{112,64},{1... | collective-permute-start | bytes 221192 | tf_op jit(solution)/shard_map/ppermute | solution.py:32
  267.1 15.1 %collective-permute-start.33 = (f32[16,1152]{1,0:T(8,128)S(1)}, f32[16,1152]{1,0:T(8,128)S(1)}, u32[]{:S(2)}, u32[]{:S(2)}) collective-permute-start(f32[16,1152]{1,0:T(8,128)S(1)} %add_add_fusion.2.refs_0_), channel_id=1, source_target_pairs={{0,3},{1,2},{2,1},{3,0},{4,7},{5,6},{6,5},{7,4},{8,11},{9,10},{10,... | collective-permute-start | bytes 221192 | tf_op jit(solution)/shard_map/ppermute | solution.py:32
  268.8 13.5 %collective-permute-start.32 = (f32[16,1152]{1,0:T(8,128)S(1)}, f32[16,1152]{1,0:T(8,128)S(1)}, u32[]{:S(2)}, u32[]{:S(2)}) collective-permute-start(f32[16,1152]{1,0:T(8,128)S(1)} %add_add_fusion.2.refs_0_), channel_id=1, source_target_pairs={{0,2},{1,3},{2,0},{3,1},{4,6},{5,7},{6,4},{7,5},{8,10},{9,11},{10,... | collective-permute-start | bytes 221192 | tf_op jit(solution)/shard_map/ppermute | solution.py:32
  269.9 12.3 %collective-permute-start.31 = (f32[16,1152]{1,0:T(8,128)S(1)}, f32[16,1152]{1,0:T(8,128)S(1)}, u32[]{:S(2)}, u32[]{:S(2)}) collective-permute-start(f32[16,1152]{1,0:T(8,128)S(1)} %add_add_fusion.2.refs_0_), channel_id=1, source_target_pairs={{0,1},{1,0},{2,3},{3,2},{4,5},{5,4},{6,7},{7,6},{8,9},{9,8},{10,11... | collective-permute-start | bytes 221192 | tf_op jit(solution)/shard_map/ppermute | solution.py:32
  284.6 10.8 %collective-permute-start.36 = (f32[64,768]{1,0:T(8,128)}, f32[64,768]{1,0:T(8,128)S(1)}, u32[]{:S(2)}, u32[]{:S(2)}) collective-permute-start(f32[64,768]{1,0:T(8,128)} %get-tuple-element.71.refs_0_), channel_id=1, source_target_pairs={{0,12},{4,8},{8,4},{12,0},{1,13},{5,9},{9,5},{13,1},{2,14},{6,10},... | collective-permute-start | bytes 589832 | tf_op jit(solution)/shard_map/ppermute | solution.py:32
  287.0 8.4 %collective-permute-start.35 = (f32[64,768]{1,0:T(8,128)}, f32[64,768]{1,0:T(8,128)S(1)}, u32[]{:S(2)}, u32[]{:S(2)}) collective-permute-start(f32[64,768]{1,0:T(8,128)} %get-tuple-element.71.refs_0_), channel_id=1, source_target_pairs={{0,8},{4,12},{8,0},{12,4},{1,9},{5,13},{9,1},{13,5},{2,10},{6,14},... | collective-permute-start | bytes 589832 | tf_op jit(solution)/shard_map/ppermute | solution.py:32
  287.0 8.9 %collective-permute-start.34 = (f32[64,768]{1,0:T(8,128)}, f32[64,768]{1,0:T(8,128)S(1)}, u32[]{:S(2)}, u32[]{:S(2)}) collective-permute-start(f32[64,768]{1,0:T(8,128)} %get-tuple-element.71.refs_0_), channel_id=1, source_target_pairs={{0,4},{4,0},{8,12},{12,8},{1,5},{5,1},{9,13},{13,9},{2,6},{6,2},{1... | collective-permute-start | bytes 589832 | tf_op jit(solution)/shard_map/ppermute | solution.py:32
  (35 other events, 123.3 us)
Sparse Core Ops, SparseCore 0:
  10.3 52.6 all-gather.2
  128.2 85.6 all-gather.4
where the time goes:
time: 308 us; the launch traced here: 307 us
  waiting for transfers between devices  113 us (37%)
  starting transfers between devices  89.2 us (29%)
  Pallas kernels  65.2 us (21%)
  between operations  18.4 us (6%)
  local copies, waits for them, and re-layouts  12.1 us (4%)
  other arithmetic  9.23 us (3%)
    ppermute x27, starting transfers between devices, exchange(): return lax.ppermute(x, axis, [(i, i ^ mask) for i in range(n)])  73 us
    ppermute x10, waiting for transfers between devices, shift(): return lax.ppermute(x, axis, [(i, (i + step) % n) for i in range(n)])  67.2 us
    ppermute x27, waiting for transfers between devices, exchange(): return lax.ppermute(x, axis, [(i, i ^ mask) for i in range(n)])  40.2 us
    pallas_call x2, Pallas kernels, attend(): pl.pallas_call(attention_body, out_shape=[jax.ShapeDtypeStruct((seg, head...  28.3 us
    ppermute x10, starting transfers between devices, shift(): return lax.ppermute(x, axis, [(i, (i + step) % n) for i in range(n)])  16.1 us
    pallas_call x1, Pallas kernels, shards(): pl.pallas_call(project_body, out_shape=(jax.ShapeDtypeStruct((heads_here,...  9.33 us
    pallas_call x1, Pallas kernels, shards(): pl.pallas_call(move_body, out_shape=jax.ShapeDtypeStruct((rows, width), j...  8.74 us
    pallas_call x1, Pallas kernels, shards(): pl.pallas_call(query_body, out_shape=jax.ShapeDtypeStruct((group_rows, lo...  6.5 us
  transfers between devices with their start and end apart: 39, of which 22 were waited for; matrix products, arithmetic and copies ran while one was open for 4% of the time, Pallas kernels for 17%

commit v1 on v0

--- a/solution.py
+++ b/solution.py
@@ -22,6 +22,40 @@
 first_axis = (((0,), (0,)), ((), ()))
 
 
+PLACE = (0, 2, 1, 3)
+SLOT = ((0, 2, 3, 1), (2, 0, 1, 3), (0, 2, 3, 1), (2, 0, 1, 3))
+VIDEO = [PLACE.index(p) for p in range(4)]
+BLOCK = [[SLOT[VIDEO[p]].index(q) for q in range(4)] for p in range(4)]
+
+
+def worker(f, b):
+    w = f % 4
+    return f - w + SLOT[w][b], PLACE[w]
+
+
+def gather_tokens(x):
+    count = lax.axis_size("blk")
+    pairs = []
+    for f in range(lax.axis_size("fsdp")):
+        for b in range(count):
+            to_f, to_b = worker(f, b)
+            pairs.append((f * count + b, to_f * count + to_b))
+    return lax.ppermute(x, ("fsdp", "blk"), pairs)
+
+
+def return_tokens(x, mask):
+    blks, ulys = lax.axis_size("blk"), lax.axis_size("uly")
+    pairs = []
+    for f in range(lax.axis_size("fsdp")):
+        for b in range(blks):
+            to_f, to_b = worker(f, b)
+            for u in range(ulys):
+                pairs.append(
+                    ((to_f * ulys + u) * blks + to_b, (f * ulys + (u ^ mask)) * blks + b)
+                )
+    return lax.ppermute(x, ("fsdp", "uly", "blk"), pairs)
+
+
 def shift(x, axis, step):
     n = lax.axis_size(axis)
     return lax.ppermute(x, axis, [(i, (i + step) % n) for i in range(n)])
@@ -40,32 +74,42 @@
     return (parts[0] + parts[1]) + (parts[2] + parts[3])
 
 
-def project_body(ints_ref, own_ref, left_ref, right_ref, up_ref, down_ref, w_ref, out_ref, all_ref):
-    rows = own_ref.shape[0]
-    half = rows // 2
+def project_body(
+    ints_ref, a_ref, b_ref, left_a_ref, right_a_ref, up_ref, right_b_ref, far_b_ref, w_ref,
+    pairs_ref, query_ref, all_ref, acc_ref,
+):
+    half = a_ref.shape[0]
+    rows = 2 * half
 
     @pl.when(pl.program_id(0) == 0)
     def _():
         odd = lax.rem(ints_ref[0], 2)
         left = pl.multiple_of((3 - 2 * odd) * rows, half)
         right = pl.multiple_of((1 + 2 * odd) * rows, half)
-        all_ref[:rows] = own_ref[...]
-        all_ref[pl.ds(left, half)] = left_ref[...]
+        all_ref[:half] = a_ref[...]
+        all_ref[half:rows] = b_ref[...]
+        all_ref[pl.ds(left, half)] = left_a_ref[...]
         all_ref[pl.ds(left + half, half)] = up_ref[half:]
-        all_ref[pl.ds(right, half)] = down_ref[half:]
-        all_ref[pl.ds(right + half, half)] = right_ref[...]
+        all_ref[pl.ds(right, half)] = right_a_ref[...]
+        all_ref[pl.ds(right + half, half)] = right_b_ref[...]
         all_ref[2 * rows : 2 * rows + half] = up_ref[:half]
-        all_ref[2 * rows + half : 3 * rows] = down_ref[:half]
-
-    out_ref[...] = jnp.dot(
-        all_ref[...], w_ref[...], preferred_element_type=jnp.float32
-    ).astype(jnp.bfloat16)
-
-
-def query_body(all_ref, w_ref, out_ref):
-    out_ref[...] = jnp.dot(
-        all_ref[...], w_ref[...], preferred_element_type=jnp.float32
-    ).astype(jnp.bfloat16)
+        all_ref[2 * rows + half : 3 * rows] = far_b_ref[...]
+
+    acc_ref[...] = jnp.zeros_like(acc_ref)
+    depth = 512
+
+    def step(c, carry):
+        start = pl.multiple_of(c * depth, depth)
+        acc_ref[...] += jnp.dot(
+            all_ref[:, pl.ds(start, depth)],
+            w_ref[pl.ds(start, depth)],
+            preferred_element_type=jnp.float32,
+        )
+        return carry
+
+    lax.fori_loop(0, all_ref.shape[1] // depth, step, 0)
+    query_ref[...] = acc_ref[:, :HEAD_SIZE].astype(jnp.bfloat16)
+    pairs_ref[...] = acc_ref[:, HEAD_SIZE:].astype(jnp.bfloat16)
 
 
 def attention_body(q_ref, bias_ref, *refs):
@@ -117,10 +161,10 @@
 
 
 def attend(query_rows, first_head, heads, blocks, bias):
-    rows = query_rows.shape[0]
+    rows = query_rows.shape[1]
     keys = bias.shape[1]
     seg = rows // 4
-    chunk = 256
+    chunk = 512
 
     def spec(array, place):
         return pl.BlockSpec((None,) + array.shape[1:], lambda i: (i + place, 0, 0))
@@ -130,7 +174,7 @@
         out_shape=[jax.ShapeDtypeStruct((seg, heads * HEAD_SIZE), jnp.bfloat16)] * 4,
         grid=(heads,),
         in_specs=[
-            pl.BlockSpec((rows, HEAD_SIZE), lambda i: (0, i + first_head)),
+            pl.BlockSpec((None, rows, HEAD_SIZE), lambda i: (i + first_head, 0, 0)),
             pl.BlockSpec(bias.shape, lambda i: (0, 0)),
         ]
         + [spec(array, place) for array, place in blocks],
@@ -253,123 +297,92 @@
     limit = valid_token_count[0]
     rank = adapter_down_map.shape[0]
 
-    current = latents[0].astype(jnp.float32)
-    rows = current.shape[0]
-    width = current.shape[1]
-    normed = (current * lax.rsqrt(jnp.mean(current * current, -1, keepdims=True) + rms_eps)).astype(
-        jnp.bfloat16
-    )
+    rows, width = latents.shape[1:]
+    half = rows // 2
+    video_slot = lax.axis_index("fsdp") % 4
+    moved_a = gather_tokens(latents[0, :half])
+    moved_b = gather_tokens(after(latents[0, half:], moved_a))
+    work_limit = gather_tokens(jnp.full((8, 128), limit, jnp.int32))[0, 0]
+
+    def norm(x):
+        x = x.astype(jnp.float32)
+        return (x * lax.rsqrt(jnp.mean(x * x, -1, keepdims=True) + rms_eps)).astype(jnp.bfloat16)
+
+    normed_a, normed_b = norm(moved_a), norm(moved_b)
     heads_here = query_key_value_weight.shape[2] // HEAD_SIZE
     local_columns = heads_here * HEAD_SIZE
     pair = 2 * HEAD_SIZE
     group_rows = uly_count * rows
 
-    pieces = []
-    for h in range(heads_here):
-        cols = slice(h * HEAD_SIZE, (h + 1) * HEAD_SIZE)
-        pieces += [query_key_value_weight[1][:, cols], query_key_value_weight[2][:, cols]]
-    pieces.append(query_key_value_weight[0])
-    weight_rows = lax.all_gather(jnp.concatenate(pieces, 1), "fsdp", axis=0, tiled=True)
-
-    half = rows // 2
-    left = shift(normed[:half], "uly", 1)
-    right = shift(normed[half:], "uly", -1)
-    second, first, _, _ = lax.optimization_barrier((normed[half:], normed[:half], left, right))
-    up = shift(jnp.concatenate((left, second), 0), "uly", 1)
-    down = shift(jnp.concatenate((right, first), 0), "uly", -1)
-
-    maps = after(jnp.concatenate((output_weight, adapter_down_map), 0), up, down)
+    weight = jnp.concatenate(
+        [
+            query_key_value_weight[j, :, h * HEAD_SIZE : (h + 1) * HEAD_SIZE]
+            for h in range(heads_here)
+            for j in range(3)
+        ],
+        1,
+    )
+    weight_rows = lax.all_gather(weight, "fsdp", axis=0, tiled=True)
+
+    left_a = shift(normed_a, "uly", 1)
+    right_a = shift(normed_a, "uly", -1)
+    normed_b, relay, _ = lax.optimization_barrier((normed_b, left_a, right_a))
+    up = shift(jnp.concatenate((relay, normed_b), 0), "uly", 1)
+    right_b = shift(normed_b, "uly", -1)
+    far_b = shift(right_b, "uly", -1)
+
+    maps = after(jnp.concatenate((output_weight, adapter_down_map), 0), up, far_b)
     maps = jnp.concatenate([maps] + [exchange(maps, "uly", k) for k in (1, 2, 3)], 1)
     output_columns, down_full = maps[: output_weight.shape[0]], maps[output_weight.shape[0] :]
 
-    key_values, gathered = pl.pallas_call(
+    key_values, query_rows = pl.pallas_call(
         project_body,
         out_shape=(
             jax.ShapeDtypeStruct((heads_here, group_rows, pair), jnp.bfloat16),
-            jax.ShapeDtypeStruct((group_rows, width), jnp.bfloat16),
+            jax.ShapeDtypeStruct((heads_here, group_rows, HEAD_SIZE), jnp.bfloat16),
         ),
         grid=(heads_here,),
-        in_specs=[smem] + [vmem] * 5 + [pl.BlockSpec((width, pair), lambda h: (0, h))],
+        in_specs=[smem] + [vmem] * 7 + [pl.BlockSpec((width, local_columns), lambda h: (0, h))],
         out_specs=(
             pl.BlockSpec((None, group_rows, pair), lambda h: (h, 0, 0)),
-            pl.BlockSpec((group_rows, width), lambda h: (0, 0)),
+            pl.BlockSpec((None, group_rows, HEAD_SIZE), lambda h: (h, 0, 0)),
         ),
+        scratch_shapes=[
+            pltpu.VMEM((group_rows, width), jnp.bfloat16),
+            pltpu.VMEM((group_rows, local_columns), jnp.float32),
+        ],
         name="project",
-    )(uly_int, normed, left, right, up, down, weight_rows)
-    query_rows = pl.pallas_call(
-        query_body,
-        out_shape=jax.ShapeDtypeStruct((group_rows, local_columns), jnp.bfloat16),
-        grid=(1,),
-        in_specs=[
-            pl.BlockSpec((group_rows, width), lambda i: (0, 0)),
-            pl.BlockSpec((width, local_columns), lambda i: (0, 2)),
-        ],
-        out_specs=pl.BlockSpec((group_rows, local_columns), lambda i: (0, 0)),
-        name="query",
-    )(gathered, weight_rows)
+    )(uly_int, normed_a, normed_b, left_a, right_a, up, right_b, far_b, weight_rows)
 
     key_index = jnp.arange(blk_count * group_rows, dtype=jnp.int32)
-    step = key_index // group_rows
-    key_blk = (blk_id + jnp.where(step == 0, 0, jnp.where(step == 1, 3, step - 1))) % blk_count
+    key_blk = jnp.array(BLOCK, jnp.int32)[blk_id]
+    key_blk = jnp.stack([key_blk[video_slot ^ k] for k in range(4)])
     key_pos = (
-        (uly_id ^ (key_index % group_rows // rows)) * blk_count + key_blk
+        (uly_id ^ (key_index % group_rows // rows)) * blk_count
+        + jnp.repeat(key_blk, group_rows)
     ) * rows + key_index % rows
-    bias = jnp.where(key_pos < limit, 0.0, -1e30).astype(jnp.float32)[None]
-
-    middle = group_rows // 2
-    firsts, seconds = key_values[:, :middle], key_values[:, middle:]
+    bias = jnp.where(key_pos < work_limit, 0.0, -1e30).astype(jnp.float32)[None]
+
     lead = heads_here - 1
-
-    def wave(up_part, down_part):
-        up_part, down_part = lax.optimization_barrier((up_part, down_part))
-        up_part = shift(up_part, "blk", 1)
-        down_part = shift(down_part, "blk", -1)
-        return up_part, down_part
-
-    def join(*parts):
-        return jnp.concatenate(parts, 0)
-
-    up_0, down_0 = wave(firsts[:lead], seconds[:lead])
-    up_1, down_1 = wave(
-        join(up_0, seconds[:lead], firsts[lead:]), join(down_0, firsts[:lead], seconds[lead:])
-    )
-    up_2, down_2 = wave(
-        join(up_1[2 * lead :], seconds[lead:]), join(down_1[2 * lead :], firsts[lead:])
-    )
-    weight_full = lax.all_gather(after(output_columns, up_1, down_1), "fsdp", axis=0, tiled=True)
+    core = exchange(key_values, "fsdp", 1)
+    chip_lead = exchange(key_values[:lead], "fsdp", 2)
+    chip_last = exchange(after(key_values[lead:], chip_lead), "fsdp", 2)
+    far_lead = exchange(chip_lead, "fsdp", 1)
+    far_last = exchange(chip_last, "fsdp", 1)
+    weight_full = lax.all_gather(after(output_columns, chip_last), "fsdp", axis=0, tiled=True)
 
     def others(segs):
-        return [segs[0]] + [exchange(segs[k], "uly", k) for k in (1, 2, 3)]
+        return [return_tokens(segs[k], k) for k in range(4)]
 
     segs = attend(
-        query_rows,
-        0,
-        lead,
-        (
-            (key_values, 0),
-            (up_0, 0),
-            (up_1, lead),
-            (down_1, lead),
-            (down_0, 0),
-            (up_1, 0),
-            (down_1, 0),
-        ),
-        bias,
+        query_rows, 0, lead, ((key_values, 0), (core, 0), (chip_lead, 0), (far_lead, 0)), bias
     )
     lead_pieces = others(segs)
     segs = attend(
         query_rows,
         lead,
         1,
-        (
-            (key_values, lead),
-            (up_1, 2 * lead),
-            (up_2, 1),
-            (down_2, 1),
-            (down_1, 2 * lead),
-            (up_2, 0),
-            (down_2, 0),
-        ),
+        ((key_values, lead), (core, lead), (chip_last, 0), (far_last, 0)),
         bias,
     )
     last_pieces = others(segs)

time: 308 us -> 297 us (0.964)
  waiting for transfers between devices: 113 us -> 93.1 us
  starting transfers between devices: 89.2 us -> 103 us
  Pallas kernels: 65.2 us -> 57 us
  local copies, waits for them, and re-layouts: 12.1 us -> 15.8 us
    ppermute x0 -> x11, starting transfers between devices: none -> 53.1 us  [the longest x8 27.2 us: return_tokens(): return lax.ppermute(x, ('fsdp', 'uly', 'blk'), pairs)]
    ppermute x10 -> x5, waiting for transfers between devices: 67.2 us -> 14.5 us  [shift(): return lax.ppermute(x, axis, [(i, (i + step) % n) for i in range(n)])]
    ppermute x0 -> x11, waiting for transfers between devices: none -> 31.9 us  [the longest x3 26.8 us: gather_tokens(): return lax.ppermute(x, ('fsdp', 'blk'), pairs)]
    ppermute x27 -> x26, starting transfers between devices: 73 us -> 42.3 us  [exchange(): return lax.ppermute(x, axis, [(i, i ^ mask) for i in range(n)])]
    ppermute x10 -> x5, starting transfers between devices: 16.1 us -> 7.73 us  [shift(): return lax.ppermute(x, axis, [(i, (i + step) % n) for i in range(n)])]
    pallas_call x2, Pallas kernels: 28.3 us -> 21.1 us  [attend(): pl.pallas_call(attention_body, out_shape=[jax.ShapeDtypeStruct((seg, head...]
    pallas_call x1 -> x0, Pallas kernels: 6.5 us -> none  [shards(): pl.pallas_call(query_body, out_shape=jax.ShapeDtypeStruct((group_rows, lo...]
    ppermute x27 -> x26, waiting for transfers between devices: 40.2 us -> 46.7 us  [exchange(): return lax.ppermute(x, axis, [(i, i ^ mask) for i in range(n)])]
  transfers between devices with their start and end apart: 39 -> 44, of which waited for: 22 -> 21; matrix products, arithmetic and copies ran while one was open for 4% -> 4% of each run, Pallas kernels for 17% -> 13%
where the time goes in v1:
time: 297 us; the launch traced here: 296 us
  starting transfers between devices  103 us (35%)
  waiting for transfers between devices  93.1 us (31%)
  Pallas kernels  57 us (19%)
  between operations  18.6 us (6%)
  local copies, waits for them, and re-layouts  15.8 us (5%)
  other arithmetic  8.55 us (3%)
    ppermute x26, waiting for transfers between devices, exchange(): return lax.ppermute(x, axis, [(i, i ^ mask) for i in range(n)])  46.7 us
    ppermute x26, starting transfers between devices, exchange(): return lax.ppermute(x, axis, [(i, i ^ mask) for i in range(n)])  42.3 us
    ppermute x8, starting transfers between devices, return_tokens(): return lax.ppermute(x, ('fsdp', 'uly', 'blk'), pairs)  27.2 us
    ppermute x3, waiting for transfers between devices, gather_tokens(): return lax.ppermute(x, ('fsdp', 'blk'), pairs)  26.8 us
    ppermute x3, starting transfers between devices, gather_tokens(): return lax.ppermute(x, ('fsdp', 'blk'), pairs)  26 us
    pallas_call x2, Pallas kernels, attend(): pl.pallas_call(attention_body, out_shape=[jax.ShapeDtypeStruct((seg, head...  21.1 us
    pallas_call x1, Pallas kernels, shards(): pl.pallas_call(project_body, out_shape=(jax.ShapeDtypeStruct((heads_here,...  15.1 us
    ppermute x5, waiting for transfers between devices, shift(): return lax.ppermute(x, axis, [(i, (i + step) % n) for i in range(n)])  14.5 us
  transfers between devices with their start and end apart: 44, of which 21 were waited for; matrix products, arithmetic and copies ran while one was open for 4% of the time, Pallas kernels for 13%

profile of v1, /device:TPU:1, one launch (start us, length us, event | category | flops | bytes accessed | tf_op | source)
XLA Modules:
  0.0 296.4 jit_solution(13178598909949312685)
XLA Ops:
  15.6 9.8 %collective-permute-start = (bf16[96,3072]{1,0:T(8,128)(2,1)S(1)}, bf16[96,3072]{1,0:T(8,128)(2,1)S(1)}, u32[]{:S(2)}, u32[]{:S(2)}) collective-permute-start(bf16[96,3072]{1,0:T(8,128)(2,1)S(1)} %get-tuple-element.64), channel_id=1, source_target_pairs={{0,0},{1,32},{2,48},{3,16},{16,34},{17,2},{18,18},{19,50},{32,1},{... | collective-permute-start | bytes 1769480 | tf_op jit(solution)/shard_map/ppermute | solution.py:43
  25.4 13.2 %collective-permute-done = bf16[96,3072]{1,0:T(8,128)(2,1)S(1)} collective-permute-done((bf16[96,3072]{1,0:T(8,128)(2,1)S(1)}, bf16[96,3072]{1,0:T(8,128)(2,1)S(1)}, u32[]{:S(2)}, u32[]{:S(2)}) %collective-permute-start) | collective-permute-done | bytes 589856 | tf_op jit(solution)/shard_map/ppermute | solution.py:43
  38.6 7.5 %collective-permute-start.1 = (bf16[96,3072]{1,0:T(8,128)(2,1)S(1)}, bf16[96,3072]{1,0:T(8,128)(2,1)S(1)}, u32[]{:S(2)}, u32[]{:S(2)}) collective-permute-start(bf16[96,3072]{1,0:T(8,128)(2,1)S(1)} %get-tuple-element.34), channel_id=1, source_target_pairs={{0,0},{1,32},{2,48},{3,16},{16,34},{17,2},{18,18},{19,50},{32,1},{... | collective-permute-start | bytes 1769480 | tf_op jit(solution)/shard_map/ppermute | solution.py:43
  49.3 13.6 %collective-permute-done.1 = bf16[96,3072]{1,0:T(8,128)(2,1)S(1)} collective-permute-done((bf16[96,3072]{1,0:T(8,128)(2,1)S(1)}, bf16[96,3072]{1,0:T(8,128)(2,1)S(1)}, u32[]{:S(2)}, u32[]{:S(2)}) %collective-permute-start.1) | collective-permute-done | bytes 589856 | tf_op jit(solution)/shard_map/ppermute | solution.py:43
  67.2 7.6 %collective-permute-done.5.right_b_ref = bf16[96,3072]{1,0:T(8,128)(2,1)S(1)} collective-permute-done((bf16[96,3072]{1,0:T(8,128)(2,1)S(1)}, bf16[96,3072]{1,0:T(8,128)(2,1)S(1)}, u32[]{:S(2)}, u32[]{:S(2)}) %collective-permute-start.5) | collective-permute-done | bytes 589856 | tf_op jit(solution)/shard_map/ppermute | solution.py:61
  77.1 3.8 %collective-permute-done.4.up_ref = bf16[192,3072]{1,0:T(8,128)(2,1)S(1)} collective-permute-done((bf16[192,3072]{1,0:T(8,128)(2,1)}, bf16[192,3072]{1,0:T(8,128)(2,1)S(1)}, u32[]{:S(2)}, u32[]{:S(2)}) %collective-permute-start.4) | collective-permute-done | bytes 1179680 | tf_op jit(solution)/shard_map/ppermute | solution.py:61
  81.0 3.0 %collective-permute-done.6.far_b_ref = bf16[96,3072]{1,0:T(8,128)(2,1)} collective-permute-done((bf16[96,3072]{1,0:T(8,128)(2,1)S(1)}, bf16[96,3072]{1,0:T(8,128)(2,1)}, u32[]{:S(2)}, u32[]{:S(2)}) %collective-permute-start.6) | collective-permute-done | bytes 589856 | tf_op jit(solution)/shard_map/ppermute | solution.py:61
  84.0 15.1 %project.1 = (bf16[3,768,256]{2,1,0:T(8,128)(2,1)}, bf16[3,768,128]{2,1,0:T(8,128)(2,1)}) custom-call(s32[1]{0:T(128)} %bitcast.8.ints_ref, bf16[96,3072]{1,0:T(8,128)(2,1)} %copy-done.4, bf16[96,3072]{1,0:T(8,128)(2,1)} %copy-done.1, bf16[96,3072]{1,0:T(8,128)(2,1)} %copy-done.5, bf16[96,3072]{1,0:T(8,128)(2,1)} %copy-done.8, bf16[192,3072]{1,0:T(8,128)(2,1)} %copy-done.6, ...), custom_call_target="tpu_custom_call" | custom-call | tf_op jit(solution)/shard_map/project/pallas_call | solution.py:338
  103.0 4.4 %collective-permute-start.8 = (bf16[256,384]{1,0:T(8,128)(2,1)S(1)}, bf16[256,384]{1,0:T(8,128)(2,1)S(1)}, u32[]{:S(2)}, u32[]{:S(2)}) collective-permute-start(bf16[256,384]{1,0:T(8,128)(2,1)S(1)} %pad_maximum_fusion.1), channel_id=1, source_target_pairs={{0,8},{4,12},{8,0},{12,4},{1,9},{5,13},{9,1},{13,5},{2,10},{6,14},... | collective-permute-start | bytes 589832 | tf_op jit(solution)/shard_map/ppermute | solution.py:66
  107.4 9.7 %collective-permute-done.12.refs_2_ = bf16[2,768,256]{2,1,0:T(8,128)(2,1)S(1)} collective-permute-done((bf16[2,768,256]{2,1,0:T(8,128)(2,1)S(1)}, bf16[2,768,256]{2,1,0:T(8,128)(2,1)S(1)}, u32[]{:S(2)}, u32[]{:S(2)}) %collective-permute-start.12) | collective-permute-done | bytes 786464 | tf_op jit(solution)/shard_map/ppermute | solution.py:66
  118.9 3.3 %collective-permute-start.9 = (bf16[256,384]{1,0:T(8,128)(2,1)S(1)}, bf16[256,384]{1,0:T(8,128)(2,1)S(1)}, u32[]{:S(2)}, u32[]{:S(2)}) collective-permute-start(bf16[256,384]{1,0:T(8,128)(2,1)S(1)} %pad_maximum_fusion.1), channel_id=1, source_target_pairs={{0,12},{4,8},{8,4},{12,0},{1,13},{5,9},{9,5},{13,1},{2,14},{6,10},... | collective-permute-start | bytes 589832 | tf_op jit(solution)/shard_map/ppermute | solution.py:66
  122.3 2.9 collective-permute-done.9
  127.0 8.7 %collective-permute-start.10 = (s32[8,128]{1,0:T(8,128)S(1)}, s32[8,128]{1,0:T(8,128)S(1)}, u32[]{:S(2)}, u32[]{:S(2)}) collective-permute-start(s32[8,128]{1,0:T(8,128)S(1)} %broadcast_in_dim.21), channel_id=1, source_target_pairs={{0,0},{1,32},{2,48},{3,16},{16,34},{17,2},{18,18},{19,50},{32,1},{... | collective-permute-start | bytes 12296 | tf_op jit(solution)/shard_map/ppermute | solution.py:43
  143.0 7.7 %attend.3 = (bf16[192,128]{1,0:T(8,128)(2,1)}, bf16[192,128]{1,0:T(8,128)(2,1)}, bf16[192,128]{1,0:T(8,128)(2,1)}, bf16[192,128]{1,0:T(8,128)(2,1)}) custom-call(bf16[3,768,128]{2,1,0:T(8,128)(2,1)} %get-tuple-element.38.q_ref, f32[1,3072]{1,0:T(1,128)} %compare_select_fusion.bias_ref, bf16[3,768,256]{2,1,0:T(8,128)(2,1)} %get-tuple-element.39.refs_0_, ...), custom_call_target="tpu_custom_call" | custom-call | tf_op jit(solution)/shard_map/attend/pallas_call | solution.py:172
  150.7 3.2 %collective-permute-start.17 = (bf16[192,128]{1,0:T(8,128)(2,1)}, bf16[192,128]{1,0:T(8,128)(2,1)S(1)}, u32[]{:S(2)}, u32[]{:S(2)}) collective-permute-start(bf16[192,128]{1,0:T(8,128)(2,1)} %get-tuple-element.42), channel_id=1, source_target_pairs={{0,0},{4,4},{8,8},{12,12},{32,1},{36,5},{40,9},{44,13},{48,2},{52,... | collective-permute-start | bytes 147464 | tf_op jit(solution)/shard_map/ppermute | solution.py:56
  156.6 5.0 %collective-permute-start.21 = (bf16[192,128]{1,0:T(8,128)(2,1)}, bf16[192,128]{1,0:T(8,128)(2,1)S(1)}, u32[]{:S(2)}, u32[]{:S(2)}) collective-permute-start(bf16[192,128]{1,0:T(8,128)(2,1)} %get-tuple-element.46), channel_id=1, source_target_pairs={{0,8},{4,12},{8,0},{12,4},{32,9},{36,13},{40,1},{44,5},{48,10},{52... | collective-permute-start | bytes 147464 | tf_op jit(solution)/shard_map/ppermute | solution.py:56
  164.3 13.4 %attend.2 = (bf16[192,256]{1,0:T(8,128)(2,1)}, bf16[192,256]{1,0:T(8,128)(2,1)}, bf16[192,256]{1,0:T(8,128)(2,1)}, bf16[192,256]{1,0:T(8,128)(2,1)}) custom-call(bf16[3,768,128]{2,1,0:T(8,128)(2,1)} %get-tuple-element.38.q_ref, f32[1,3072]{1,0:T(1,128)} %compare_select_fusion.bias_ref, bf16[3,768,256]{2,1,0:T(8,128)(2,1)} %get-tuple-element.39.refs_0_, ...), custom_call_target="tpu_custom_call" | custom-call | tf_op jit(solution)/shard_map/attend/pallas_call | solution.py:172
  177.7 3.2 %collective-permute-start.14 = (bf16[192,256]{1,0:T(8,128)(2,1)}, bf16[192,256]{1,0:T(8,128)(2,1)S(1)}, u32[]{:S(2)}, u32[]{:S(2)}) collective-permute-start(bf16[192,256]{1,0:T(8,128)(2,1)} %get-tuple-element.40), channel_id=1, source_target_pairs={{0,0},{4,4},{8,8},{12,12},{32,1},{36,5},{40,9},{44,13},{48,2},{52,... | collective-permute-start | bytes 294920 | tf_op jit(solution)/shard_map/ppermute | solution.py:56
  182.4 6.3 %collective-permute-start.20 = (bf16[192,256]{1,0:T(8,128)(2,1)}, bf16[192,256]{1,0:T(8,128)(2,1)S(1)}, u32[]{:S(2)}, u32[]{:S(2)}) collective-permute-start(bf16[192,256]{1,0:T(8,128)(2,1)} %get-tuple-element.45), channel_id=1, source_target_pairs={{0,8},{4,12},{8,0},{12,4},{32,9},{36,13},{40,1},{44,5},{48,10},{52... | collective-permute-start | bytes 294920 | tf_op jit(solution)/shard_map/ppermute | solution.py:56
  193.6 5.1 %collective-permute-done.22.refs_6_ = bf16[192,256]{1,0:T(8,128)(2,1)S(1)} collective-permute-done((bf16[192,256]{1,0:T(8,128)(2,1)}, bf16[192,256]{1,0:T(8,128)(2,1)S(1)}, u32[]{:S(2)}, u32[]{:S(2)}) %collective-permute-start.22) | collective-permute-done | bytes 98336 | tf_op jit(solution)/shard_map/ppermute | solution.py:56
  199.3 4.5 %standard.1 = (bf16[192,1536]{1,0:T(8,128)(2,1)}, bf16[192,64]{1,0:T(8,128)(2,1)}, bf16[192,3072]{1,0:T(8,128)(2,1)}, f32[8,128]{1,0:T(8,128)}) custom-call(s32[2]{0:T(128)} %pad_add_fusion.ints_ref, f32[1]{0:T(128)} %bitcast.4.gain_ref, bf16[64,1536]{1,0:T(8,128)(2,1)} %slice.72.down_ref, bf16[64,3072]{1,0:T(8,128)(2,1)} %up_ref.3, ...), custom_call_target="tpu_custom_call" | custom-call | tf_op jit(solution)/shard_map/standard/pallas_call | solution.py:399
  203.8 3.8 %products.1 = (f32[64,1280]{1,0:T(8,128)}, f32[64,1280]{1,0:T(8,128)}, f32[64,1280]{1,0:T(8,128)}, f32[64,1280]{1,0:T(8,128)}) custom-call(s32[1]{0:T(128)} %bitcast.8.ints_ref, bf16[192,64]{1,0:T(8,128)(2,1)} %get-tuple-element.51.narrow_ref, bf16[192,3072]{1,0:T(8,128)(2,1)} %get-tuple-element.52.masked_ref, bf16[64,3072]{1,0:T(8,128)(2,1)} %up_ref.3, ...), custom_call_target="tpu_custom_call" | custom-call | tf_op jit(solution)/shard_map/products/pallas_call | solution.py:414
  208.1 3.3 %collective-permute-start.26 = (f32[64,1280]{1,0:T(8,128)}, f32[64,1280]{1,0:T(8,128)S(1)}, u32[]{:S(2)}, u32[]{:S(2)}) collective-permute-start(f32[64,1280]{1,0:T(8,128)} %get-tuple-element.57), channel_id=1, source_target_pairs={{0,12},{4,8},{8,4},{12,0},{1,13},{5,9},{9,5},{13,1},{2,14},{6,10},... | collective-permute-start | bytes 983048 | tf_op jit(solution)/shard_map/ppermute | solution.py:66
  216.4 3.2 %collective-permute-done.26 = f32[64,1280]{1,0:T(8,128)S(1)} collective-permute-done((f32[64,1280]{1,0:T(8,128)}, f32[64,1280]{1,0:T(8,128)S(1)}, u32[]{:S(2)}, u32[]{:S(2)}) %collective-permute-start.26) | collective-permute-done | bytes 327712 | tf_op jit(solution)/shard_map/ppermute | solution.py:66
  223.0 3.4 %collective-permute-start.29 = (f32[16,1280]{1,0:T(8,128)S(1)}, f32[16,1280]{1,0:T(8,128)S(1)}, u32[]{:S(2)}, u32[]{:S(2)}) collective-permute-start(f32[16,1280]{1,0:T(8,128)S(1)} %get-tuple-element.67), channel_id=1, source_target_pairs={{0,3},{1,2},{2,1},{3,0},{4,7},{5,6},{6,5},{7,4},{8,11},{9,10},{10,... | collective-permute-start | bytes 245768 | tf_op jit(solution)/shard_map/ppermute | solution.py:66
  227.1 5.2 %collective-permute-done.28 = f32[16,1280]{1,0:T(8,128)S(1)} collective-permute-done((f32[16,1280]{1,0:T(8,128)S(1)}, f32[16,1280]{1,0:T(8,128)S(1)}, u32[]{:S(2)}, u32[]{:S(2)}) %collective-permute-start.28) | collective-permute-done | bytes 81952 | tf_op jit(solution)/shard_map/ppermute | solution.py:66
  234.3 3.9 %collective-permute-start.31 = (f32[16,1152]{1,0:T(8,128)S(1)}, f32[16,1152]{1,0:T(8,128)S(1)}, u32[]{:S(2)}, u32[]{:S(2)}) collective-permute-start(f32[16,1152]{1,0:T(8,128)S(1)} %slice_multiply_fusion), channel_id=1, source_target_pairs={{0,128},{16,144},{32,160},{48,176},{64,192},{80,208},{96,224},{112... | collective-permute-start | bytes 221192 | tf_op jit(solution)/shard_map/ppermute | solution.py:66
  242.6 4.1 %collective-permute-start.33 = (f32[16,1152]{1,0:T(8,128)S(1)}, f32[16,1152]{1,0:T(8,128)S(1)}, u32[]{:S(2)}, u32[]{:S(2)}) collective-permute-start(f32[16,1152]{1,0:T(8,128)S(1)} %add_add_fusion.3), channel_id=1, source_target_pairs={{0,16},{16,0},{32,48},{48,32},{64,80},{80,64},{96,112},{112,96},{1... | collective-permute-start | bytes 221192 | tf_op jit(solution)/shard_map/ppermute | solution.py:66
  259.4 8.7 %move.1 = bf16[192,3072]{1,0:T(8,128)(2,1)} custom-call(f32[4]{0:T(128)} %pad_maximum_fusion.2.scalars_ref, bf16[192,1536]{1,0:T(8,128)(2,1)} %get-tuple-element.49.own_ref, bf16[3072,1536]{1,0:T(8,128)(2,1)} %all-gather.5.cloned.1.call-done.w_ref, bf16[192,3072]{1,0:T(8,128)(2,1)} %bitcast.49, bf16[192,3072]{1,0:T(8,128)(2,1)} %bitcast.48), custom_call_target="tpu_custom_call" | custom-call | tf_op jit(solution)/shard_map/move/pallas_call | solution.py:451
  270.5 3.7 %collective-permute-start.40 = (f32[64,768]{1,0:T(8,128)}, f32[64,768]{1,0:T(8,128)S(1)}, u32[]{:S(2)}, u32[]{:S(2)}) collective-permute-start(f32[64,768]{1,0:T(8,128)} %get-tuple-element.63.refs_0_), channel_id=1, source_target_pairs={{0,8},{4,12},{8,0},{12,4},{1,9},{5,13},{9,1},{13,5},{2,10},{6,14},... | collective-permute-start | bytes 589832 | tf_op jit(solution)/shard_map/ppermute | solution.py:66
  276.0 6.4 %collective-permute-done.40.refs_2_ = f32[64,768]{1,0:T(8,128)S(1)} collective-permute-done((f32[64,768]{1,0:T(8,128)}, f32[64,768]{1,0:T(8,128)S(1)}, u32[]{:S(2)}, u32[]{:S(2)}) %collective-permute-start.40) | collective-permute-done | bytes 196640 | tf_op jit(solution)/shard_map/ppermute | solution.py:66
  282.4 3.2 %collective-permute-done.41.refs_3_ = f32[64,768]{1,0:T(8,128)S(1)} collective-permute-done((f32[64,768]{1,0:T(8,128)}, f32[64,768]{1,0:T(8,128)S(1)}, u32[]{:S(2)}, u32[]{:S(2)}) %collective-permute-start.41) | collective-permute-done | bytes 196640 | tf_op jit(solution)/shard_map/ppermute | solution.py:66
  (170 shorter events, 77.8 us)
Async XLA Ops:
  7.2 76.8 %all-gather.3.cloned.1.call-start = ((), (), s32[]{:S(2)}) async-start(), calls=%async_computation | async-start | bytes 7520256 | tf_op jit(solution)/shard_map/all_gather | solution.py:325
  15.5 243.9 %all-gather.5.cloned.1.call-start = ((), (), s32[]{:S(2)}) async-start(), calls=%async_computation.1 | async-start | bytes 10027008 | tf_op jit(solution)/shard_map/all_gather | solution.py:372
  15.6 23.0 %collective-permute-start = (bf16[96,3072]{1,0:T(8,128)(2,1)S(1)}, bf16[96,3072]{1,0:T(8,128)(2,1)S(1)}, u32[]{:S(2)}, u32[]{:S(2)}) collective-permute-start(bf16[96,3072]{1,0:T(8,128)(2,1)S(1)} %get-tuple-element.64), channel_id=1, source_target_pairs={{0,0},{1,32},{2,48},{3,16},{16,34},{17,2},{18,18},{19,50},{32,1},{... | collective-permute-start | bytes 1769480 | tf_op jit(solution)/shard_map/ppermute | solution.py:43
  38.6 24.2 %collective-permute-start.1 = (bf16[96,3072]{1,0:T(8,128)(2,1)S(1)}, bf16[96,3072]{1,0:T(8,128)(2,1)S(1)}, u32[]{:S(2)}, u32[]{:S(2)}) collective-permute-start(bf16[96,3072]{1,0:T(8,128)(2,1)S(1)} %get-tuple-element.34), channel_id=1, source_target_pairs={{0,0},{1,32},{2,48},{3,16},{16,34},{17,2},{18,18},{19,50},{32,1},{... | collective-permute-start | bytes 1769480 | tf_op jit(solution)/shard_map/ppermute | solution.py:43
  46.5 16.7 %collective-permute-start.2 = (bf16[96,3072]{1,0:T(8,128)(2,1)S(1)}, bf16[96,3072]{1,0:T(8,128)(2,1)S(1)}, u32[]{:S(2)}, u32[]{:S(2)}) collective-permute-start(bf16[96,3072]{1,0:T(8,128)(2,1)S(1)} %fusion.3.a_ref), channel_id=1, source_target_pairs={{0,4},{4,8},{8,12},{12,0},{1,5},{5,9},{9,13},{13,1},{2,6},{6,10},{... | collective-permute-start | bytes 1769480 | tf_op jit(solution)/shard_map/ppermute | solution.py:61
  47.8 15.5 %collective-permute-start.3 = (bf16[96,3072]{1,0:T(8,128)(2,1)S(1)}, bf16[96,3072]{1,0:T(8,128)(2,1)S(1)}, u32[]{:S(2)}, u32[]{:S(2)}) collective-permute-start(bf16[96,3072]{1,0:T(8,128)(2,1)S(1)} %fusion.3.a_ref), channel_id=1, source_target_pairs={{0,12},{4,0},{8,4},{12,8},{1,13},{5,1},{9,5},{13,9},{2,14},{6,2},{... | collective-permute-start | bytes 1769480 | tf_op jit(solution)/shard_map/ppermute | solution.py:61
  64.5 16.5 %collective-permute-start.4 = (bf16[192,3072]{1,0:T(8,128)(2,1)}, bf16[192,3072]{1,0:T(8,128)(2,1)S(1)}, u32[]{:S(2)}, u32[]{:S(2)}) collective-permute-start(bf16[192,3072]{1,0:T(8,128)(2,1)} %pad_maximum_fusion), channel_id=1, source_target_pairs={{0,4},{4,8},{8,12},{12,0},{1,5},{5,9},{9,13},{13,1},{2,6},{6,10},{... | collective-permute-start | bytes 3538952 | tf_op jit(solution)/shard_map/ppermute | solution.py:61
  65.7 9.1 %collective-permute-start.5 = (bf16[96,3072]{1,0:T(8,128)(2,1)S(1)}, bf16[96,3072]{1,0:T(8,128)(2,1)S(1)}, u32[]{:S(2)}, u32[]{:S(2)}) collective-permute-start(bf16[96,3072]{1,0:T(8,128)(2,1)S(1)} %fusion.1.b_ref), channel_id=1, source_target_pairs={{0,12},{4,0},{8,4},{12,8},{1,13},{5,1},{9,5},{13,9},{2,14},{6,2},{... | collective-permute-start | bytes 1769480 | tf_op jit(solution)/shard_map/ppermute | solution.py:61
  74.8 9.1 %collective-permute-start.6 = (bf16[96,3072]{1,0:T(8,128)(2,1)S(1)}, bf16[96,3072]{1,0:T(8,128)(2,1)}, u32[]{:S(2)}, u32[]{:S(2)}) collective-permute-start(bf16[96,3072]{1,0:T(8,128)(2,1)S(1)} %collective-permute-done.5.right_b_ref), channel_id=1, source_target_pairs={{0,12},{4,0},{8,4},{12,8},{1,13},{5,1},{9,5},{13,9},{2,14},{6,2},{... | collective-permute-start | bytes 1769480 | tf_op jit(solution)/shard_map/ppermute | solution.py:61
  100.3 16.8 %collective-permute-start.12 = (bf16[2,768,256]{2,1,0:T(8,128)(2,1)S(1)}, bf16[2,768,256]{2,1,0:T(8,128)(2,1)S(1)}, u32[]{:S(2)}, u32[]{:S(2)}) collective-permute-start(bf16[2,768,256]{2,1,0:T(8,128)(2,1)S(1)} %slice.67), channel_id=1, source_target_pairs={{0,32},{16,48},{32,0},{48,16},{64,96},{80,112},{96,64},{112,80},{1... | collective-permute-start | bytes 2359304 | tf_op jit(solution)/shard_map/ppermute | solution.py:66
  102.9 19.3 %collective-permute-start.7 = (bf16[256,384]{1,0:T(8,128)(2,1)S(1)}, bf16[256,384]{1,0:T(8,128)(2,1)S(1)}, u32[]{:S(2)}, u32[]{:S(2)}) collective-permute-start(bf16[256,384]{1,0:T(8,128)(2,1)S(1)} %pad_maximum_fusion.1), channel_id=1, source_target_pairs={{0,4},{4,0},{8,12},{12,8},{1,5},{5,1},{9,13},{13,9},{2,6},{6,2},{1... | collective-permute-start | bytes 589832 | tf_op jit(solution)/shard_map/ppermute | solution.py:66
  103.0 19.2 %collective-permute-start.8 = (bf16[256,384]{1,0:T(8,128)(2,1)S(1)}, bf16[256,384]{1,0:T(8,128)(2,1)S(1)}, u32[]{:S(2)}, u32[]{:S(2)}) collective-permute-start(bf16[256,384]{1,0:T(8,128)(2,1)S(1)} %pad_maximum_fusion.1), channel_id=1, source_target_pairs={{0,8},{4,12},{8,0},{12,4},{1,9},{5,13},{9,1},{13,5},{2,10},{6,14},... | collective-permute-start | bytes 589832 | tf_op jit(solution)/shard_map/ppermute | solution.py:66
  117.1 9.0 %collective-permute-start.15 = (bf16[1,768,256]{2,1,0:T(8,128)(2,1)S(1)}, bf16[1,768,256]{2,1,0:T(8,128)(2,1)S(1)}, u32[]{:S(2)}, u32[]{:S(2)}) collective-permute-start(bf16[1,768,256]{2,1,0:T(8,128)(2,1)S(1)} %slice.68), channel_id=1, source_target_pairs={{0,32},{16,48},{32,0},{48,16},{64,96},{80,112},{96,64},{112,80},{1... | collective-permute-start | bytes 1179656 | tf_op jit(solution)/shard_map/ppermute | solution.py:66
  126.2 15.5 %collective-permute-start.11 = (bf16[3,768,256]{2,1,0:T(8,128)(2,1)S(1)}, bf16[3,768,256]{2,1,0:T(8,128)(2,1)S(1)}, u32[]{:S(2)}, u32[]{:S(2)}) collective-permute-start(bf16[3,768,256]{2,1,0:T(8,128)(2,1)S(1)} %copy-done), channel_id=1, source_target_pairs={{0,16},{16,0},{32,48},{48,32},{64,80},{80,64},{96,112},{112,96},{1... | collective-permute-start | bytes 3538952 | tf_op jit(solution)/shard_map/ppermute | solution.py:66
  127.0 12.3 %collective-permute-start.10 = (s32[8,128]{1,0:T(8,128)S(1)}, s32[8,128]{1,0:T(8,128)S(1)}, u32[]{:S(2)}, u32[]{:S(2)}) collective-permute-start(s32[8,128]{1,0:T(8,128)S(1)} %broadcast_in_dim.21), channel_id=1, source_target_pairs={{0,0},{1,32},{2,48},{3,16},{16,34},{17,2},{18,18},{19,50},{32,1},{... | collective-permute-start | bytes 12296 | tf_op jit(solution)/shard_map/ppermute | solution.py:43
  139.2 25.1 %collective-permute-start.13 = (bf16[2,768,256]{2,1,0:T(8,128)(2,1)}, bf16[2,768,256]{2,1,0:T(8,128)(2,1)}, u32[]{:S(2)}, u32[]{:S(2)}) collective-permute-start(bf16[2,768,256]{2,1,0:T(8,128)(2,1)} %copy-done.7), channel_id=1, source_target_pairs={{0,16},{16,0},{32,48},{48,32},{64,80},{80,64},{96,112},{112,96},{1... | collective-permute-start | bytes 2359304 | tf_op jit(solution)/shard_map/ppermute | solution.py:66
  150.7 30.2 %collective-permute-start.17 = (bf16[192,128]{1,0:T(8,128)(2,1)}, bf16[192,128]{1,0:T(8,128)(2,1)S(1)}, u32[]{:S(2)}, u32[]{:S(2)}) collective-permute-start(bf16[192,128]{1,0:T(8,128)(2,1)} %get-tuple-element.42), channel_id=1, source_target_pairs={{0,0},{4,4},{8,8},{12,12},{32,1},{36,5},{40,9},{44,13},{48,2},{52,... | collective-permute-start | bytes 147464 | tf_op jit(solution)/shard_map/ppermute | solution.py:56
  153.9 28.5 %collective-permute-start.19 = (bf16[192,128]{1,0:T(8,128)(2,1)}, bf16[192,128]{1,0:T(8,128)(2,1)S(1)}, u32[]{:S(2)}, u32[]{:S(2)}) collective-permute-start(bf16[192,128]{1,0:T(8,128)(2,1)} %get-tuple-element.44), channel_id=1, source_target_pairs={{0,4},{4,0},{8,12},{12,8},{32,5},{36,1},{40,13},{44,9},{48,6},{52,... | collective-permute-start | bytes 147464 | tf_op jit(solution)/shard_map/ppermute | solution.py:56
  156.6 32.2 %collective-permute-start.21 = (bf16[192,128]{1,0:T(8,128)(2,1)}, bf16[192,128]{1,0:T(8,128)(2,1)S(1)}, u32[]{:S(2)}, u32[]{:S(2)}) collective-permute-start(bf16[192,128]{1,0:T(8,128)(2,1)} %get-tuple-element.46), channel_id=1, source_target_pairs={{0,8},{4,12},{8,0},{12,4},{32,9},{36,13},{40,1},{44,5},{48,10},{52... | collective-permute-start | bytes 147464 | tf_op jit(solution)/shard_map/ppermute | solution.py:56
  161.6 31.9 %collective-permute-start.23 = (bf16[192,128]{1,0:T(8,128)(2,1)}, bf16[192,128]{1,0:T(8,128)(2,1)S(1)}, u32[]{:S(2)}, u32[]{:S(2)}) collective-permute-start(bf16[192,128]{1,0:T(8,128)(2,1)} %get-tuple-element.48), channel_id=1, source_target_pairs={{0,12},{4,8},{8,4},{12,0},{32,13},{36,9},{40,5},{44,1},{48,14},{52... | collective-permute-start | bytes 147464 | tf_op jit(solution)/shard_map/ppermute | solution.py:56
  177.7 15.8 %collective-permute-start.14 = (bf16[192,256]{1,0:T(8,128)(2,1)}, bf16[192,256]{1,0:T(8,128)(2,1)S(1)}, u32[]{:S(2)}, u32[]{:S(2)}) collective-permute-start(bf16[192,256]{1,0:T(8,128)(2,1)} %get-tuple-element.40), channel_id=1, source_target_pairs={{0,0},{4,4},{8,8},{12,12},{32,1},{36,5},{40,9},{44,13},{48,2},{52,... | collective-permute-start | bytes 294920 | tf_op jit(solution)/shard_map/ppermute | solution.py:56
  181.0 12.5 %collective-permute-start.18 = (bf16[192,256]{1,0:T(8,128)(2,1)}, bf16[192,256]{1,0:T(8,128)(2,1)S(1)}, u32[]{:S(2)}, u32[]{:S(2)}) collective-permute-start(bf16[192,256]{1,0:T(8,128)(2,1)} %get-tuple-element.43), channel_id=1, source_target_pairs={{0,4},{4,0},{8,12},{12,8},{32,5},{36,1},{40,13},{44,9},{48,6},{52,... | collective-permute-start | bytes 294920 | tf_op jit(solution)/shard_map/ppermute | solution.py:56
  182.4 11.1 %collective-permute-start.20 = (bf16[192,256]{1,0:T(8,128)(2,1)}, bf16[192,256]{1,0:T(8,128)(2,1)S(1)}, u32[]{:S(2)}, u32[]{:S(2)}) collective-permute-start(bf16[192,256]{1,0:T(8,128)(2,1)} %get-tuple-element.45), channel_id=1, source_target_pairs={{0,8},{4,12},{8,0},{12,4},{32,9},{36,13},{40,1},{44,5},{48,10},{52... | collective-permute-start | bytes 294920 | tf_op jit(solution)/shard_map/ppermute | solution.py:56
  188.7 10.0 %collective-permute-start.22 = (bf16[192,256]{1,0:T(8,128)(2,1)}, bf16[192,256]{1,0:T(8,128)(2,1)S(1)}, u32[]{:S(2)}, u32[]{:S(2)}) collective-permute-start(bf16[192,256]{1,0:T(8,128)(2,1)} %get-tuple-element.47), channel_id=1, source_target_pairs={{0,12},{4,8},{8,4},{12,0},{32,13},{36,9},{40,5},{44,1},{48,14},{52... | collective-permute-start | bytes 294920 | tf_op jit(solution)/shard_map/ppermute | solution.py:56
  208.1 11.4 %collective-permute-start.26 = (f32[64,1280]{1,0:T(8,128)}, f32[64,1280]{1,0:T(8,128)S(1)}, u32[]{:S(2)}, u32[]{:S(2)}) collective-permute-start(f32[64,1280]{1,0:T(8,128)} %get-tuple-element.57), channel_id=1, source_target_pairs={{0,12},{4,8},{8,4},{12,0},{1,13},{5,9},{9,5},{13,1},{2,14},{6,10},... | collective-permute-start | bytes 983048 | tf_op jit(solution)/shard_map/ppermute | solution.py:66
  223.0 9.3 %collective-permute-start.28 = (f32[16,1280]{1,0:T(8,128)S(1)}, f32[16,1280]{1,0:T(8,128)S(1)}, u32[]{:S(2)}, u32[]{:S(2)}) collective-permute-start(f32[16,1280]{1,0:T(8,128)S(1)} %get-tuple-element.68), channel_id=1, source_target_pairs={{0,2},{1,3},{2,0},{3,1},{4,6},{5,7},{6,4},{7,5},{8,10},{9,11},{10,... | collective-permute-start | bytes 245768 | tf_op jit(solution)/shard_map/ppermute | solution.py:66
  223.0 9.7 %collective-permute-start.29 = (f32[16,1280]{1,0:T(8,128)S(1)}, f32[16,1280]{1,0:T(8,128)S(1)}, u32[]{:S(2)}, u32[]{:S(2)}) collective-permute-start(f32[16,1280]{1,0:T(8,128)S(1)} %get-tuple-element.67), channel_id=1, source_target_pairs={{0,3},{1,2},{2,1},{3,0},{4,7},{5,6},{6,5},{7,4},{8,11},{9,10},{10,... | collective-permute-start | bytes 245768 | tf_op jit(solution)/shard_map/ppermute | solution.py:66
  253.0 15.2 %collective-permute-start.36 = (f32[16,1152]{1,0:T(8,128)S(1)}, f32[16,1152]{1,0:T(8,128)S(1)}, u32[]{:S(2)}, u32[]{:S(2)}) collective-permute-start(f32[16,1152]{1,0:T(8,128)S(1)} %add_add_fusion.2.refs_0_), channel_id=1, source_target_pairs={{0,1},{1,0},{2,3},{3,2},{4,5},{5,4},{6,7},{7,6},{8,9},{9,8},{10,11... | collective-permute-start | bytes 221192 | tf_op jit(solution)/shard_map/ppermute | solution.py:66
  254.6 13.6 %collective-permute-start.37 = (f32[16,1152]{1,0:T(8,128)S(1)}, f32[16,1152]{1,0:T(8,128)S(1)}, u32[]{:S(2)}, u32[]{:S(2)}) collective-permute-start(f32[16,1152]{1,0:T(8,128)S(1)} %add_add_fusion.2.refs_0_), channel_id=1, source_target_pairs={{0,2},{1,3},{2,0},{3,1},{4,6},{5,7},{6,4},{7,5},{8,10},{9,11},{10,... | collective-permute-start | bytes 221192 | tf_op jit(solution)/shard_map/ppermute | solution.py:66
  257.0 11.2 %collective-permute-start.38 = (f32[16,1152]{1,0:T(8,128)S(1)}, f32[16,1152]{1,0:T(8,128)S(1)}, u32[]{:S(2)}, u32[]{:S(2)}) collective-permute-start(f32[16,1152]{1,0:T(8,128)S(1)} %add_add_fusion.2.refs_0_), channel_id=1, source_target_pairs={{0,3},{1,2},{2,1},{3,0},{4,7},{5,6},{6,5},{7,4},{8,11},{9,10},{10,... | collective-permute-start | bytes 221192 | tf_op jit(solution)/shard_map/ppermute | solution.py:66
  270.5 11.9 %collective-permute-start.40 = (f32[64,768]{1,0:T(8,128)}, f32[64,768]{1,0:T(8,128)S(1)}, u32[]{:S(2)}, u32[]{:S(2)}) collective-permute-start(f32[64,768]{1,0:T(8,128)} %get-tuple-element.63.refs_0_), channel_id=1, source_target_pairs={{0,8},{4,12},{8,0},{12,4},{1,9},{5,13},{9,1},{13,5},{2,10},{6,14},... | collective-permute-start | bytes 589832 | tf_op jit(solution)/shard_map/ppermute | solution.py:66
  274.2 11.4 %collective-permute-start.41 = (f32[64,768]{1,0:T(8,128)}, f32[64,768]{1,0:T(8,128)S(1)}, u32[]{:S(2)}, u32[]{:S(2)}) collective-permute-start(f32[64,768]{1,0:T(8,128)} %get-tuple-element.63.refs_0_), channel_id=1, source_target_pairs={{0,12},{4,8},{8,4},{12,0},{1,13},{5,9},{9,5},{13,1},{2,14},{6,10},... | collective-permute-start | bytes 589832 | tf_op jit(solution)/shard_map/ppermute | solution.py:66
  (43 other events, 296.1 us)
Sparse Core Ops, SparseCore 0:
  15.6 62.3 all-gather.2
  126.3 68.5 all-gather.4

commit v2 on v1

--- a/solution.py
+++ b/solution.py
@@ -74,9 +74,17 @@
     return (parts[0] + parts[1]) + (parts[2] + parts[3])
 
 
+def arrange_body(w_ref, out_ref):
+    at = 0
+    for start in range(0, w_ref.shape[2], HEAD_SIZE):
+        for j in range(3):
+            out_ref[:, at : at + HEAD_SIZE] = w_ref[j, :, start : start + HEAD_SIZE]
+            at += HEAD_SIZE
+
+
 def project_body(
     ints_ref, a_ref, b_ref, left_a_ref, right_a_ref, up_ref, right_b_ref, far_b_ref, w_ref,
-    pairs_ref, query_ref, all_ref, acc_ref,
+    pairs_ref, query_ref, all_ref,
 ):
     half = a_ref.shape[0]
     rows = 2 * half
@@ -95,21 +103,18 @@
         all_ref[2 * rows : 2 * rows + half] = up_ref[:half]
         all_ref[2 * rows + half : 3 * rows] = far_b_ref[...]
 
-    acc_ref[...] = jnp.zeros_like(acc_ref)
-    depth = 512
-
-    def step(c, carry):
-        start = pl.multiple_of(c * depth, depth)
-        acc_ref[...] += jnp.dot(
-            all_ref[:, pl.ds(start, depth)],
-            w_ref[pl.ds(start, depth)],
-            preferred_element_type=jnp.float32,
-        )
+    tile = 384
+
+    def step(r, carry):
+        start = pl.multiple_of(r * tile, tile)
+        out = jnp.dot(
+            all_ref[pl.ds(start, tile)], w_ref[...], preferred_element_type=jnp.float32
+        ).astype(jnp.bfloat16)
+        query_ref[pl.ds(start, tile)] = out[:, :HEAD_SIZE]
+        pairs_ref[pl.ds(start, tile)] = out[:, HEAD_SIZE:]
         return carry
 
-    lax.fori_loop(0, all_ref.shape[1] // depth, step, 0)
-    query_ref[...] = acc_ref[:, :HEAD_SIZE].astype(jnp.bfloat16)
-    pairs_ref[...] = acc_ref[:, HEAD_SIZE:].astype(jnp.bfloat16)
+    lax.fori_loop(0, all_ref.shape[0] // tile, step, 0)
 
 
 def attention_body(q_ref, bias_ref, *refs):
@@ -314,14 +319,15 @@
     pair = 2 * HEAD_SIZE
     group_rows = uly_count * rows
 
-    weight = jnp.concatenate(
-        [
-            query_key_value_weight[j, :, h * HEAD_SIZE : (h + 1) * HEAD_SIZE]
-            for h in range(heads_here)
-            for j in range(3)
-        ],
-        1,
-    )
+    weight = pl.pallas_call(
+        arrange_body,
+        out_shape=jax.ShapeDtypeStruct(
+            (query_key_value_weight.shape[1], 3 * local_columns), jnp.bfloat16
+        ),
+        in_specs=[vmem],
+        out_specs=vmem,
+        name="arrange",
+    )(query_key_value_weight)
     weight_rows = lax.all_gather(weight, "fsdp", axis=0, tiled=True)
 
     left_a = shift(normed_a, "uly", 1)
@@ -347,19 +353,19 @@
             pl.BlockSpec((None, group_rows, pair), lambda h: (h, 0, 0)),
             pl.BlockSpec((None, group_rows, HEAD_SIZE), lambda h: (h, 0, 0)),
         ),
-        scratch_shapes=[
-            pltpu.VMEM((group_rows, width), jnp.bfloat16),
-            pltpu.VMEM((group_rows, local_columns), jnp.float32),
-        ],
+        scratch_shapes=[pltpu.VMEM((group_rows, width), jnp.bfloat16)],
         name="project",
     )(uly_int, normed_a, normed_b, left_a, right_a, up, right_b, far_b, weight_rows)
 
     key_index = jnp.arange(blk_count * group_rows, dtype=jnp.int32)
-    key_blk = jnp.array(BLOCK, jnp.int32)[blk_id]
-    key_blk = jnp.stack([key_blk[video_slot ^ k] for k in range(4)])
+    slot = video_slot ^ (key_index // group_rows)
+    key_blk = jnp.zeros_like(slot)
+    for p in range(blk_count):
+        for q in range(4):
+            key_blk = jnp.where((blk_id == p) & (slot == q), BLOCK[p][q], key_blk)
     key_pos = (
         (uly_id ^ (key_index % group_rows // rows)) * blk_count
-        + jnp.repeat(key_blk, group_rows)
+        + key_blk
     ) * rows + key_index % rows
     bias = jnp.where(key_pos < work_limit, 0.0, -1e30).astype(jnp.float32)[None]
 
@@ -369,7 +375,7 @@
     chip_last = exchange(after(key_values[lead:], chip_lead), "fsdp", 2)
     far_lead = exchange(chip_lead, "fsdp", 1)
     far_last = exchange(chip_last, "fsdp", 1)
-    weight_full = lax.all_gather(after(output_columns, chip_last), "fsdp", axis=0, tiled=True)
+    weight_full = lax.all_gather(after(output_columns, chip_lead), "fsdp", axis=0, tiled=True)
 
     def others(segs):
         return [return_tokens(segs[k], k) for k in range(4)]
@@ -419,25 +425,7 @@
         name="products",
     )(uly_int, narrow_projection, masked, adapter_up_map, own_heads, log_tile)
 
-    summed = four_sum([shares[0]] + [exchange(shares[k], "uly", k) for k in (1, 2, 3)])
-    part = rank // blk_count
-
-    def rows_of(k):
-        return lax.dynamic_slice_in_dim(summed, (blk_id ^ k) * part, part, 0)
-
-    summed = four_sum([rows_of(0)] + [exchange(rows_of(k), "blk", k) for k in (1, 2, 3)])
-    log_ratio = summed[0, share_columns] / (2.0 * valid_len * width)
-    coef = (
-        loss_scale
-        * advantage[0]
-        * jnp.exp(log_ratio)
-        * ratio_gain
-        / (fsdp_count * valid_len * width)
-    )
-    summed = summed[:, :share_columns] * coef
-    for unit in (4, 1):
-        summed = four_sum([summed] + [exchange(summed, "fsdp", unit * k) for k in (1, 2, 3)])
-
+    parts = [exchange(shares[k], "uly", k) for k in (1, 2, 3)]
     tile = 512
     scalars = jnp.stack(
         [
@@ -462,8 +450,27 @@
         out_specs=token_tile,
         name="move",
     )(scalars, own_heads, weight_full, latents[0], sampler_noise[0])
+    next_latents, *parts = lax.optimization_barrier((next_latents, *parts))
+    summed = four_sum([shares[0]] + parts)
+    part = rank // blk_count
+
+    def rows_of(k):
+        return lax.dynamic_slice_in_dim(summed, (blk_id ^ k) * part, part, 0)
+
+    summed = four_sum([rows_of(0)] + [exchange(rows_of(k), "blk", k) for k in (1, 2, 3)])
+    log_ratio = summed[0, share_columns] / (2.0 * valid_len * width)
+    coef = (
+        loss_scale
+        * advantage[0]
+        * jnp.exp(log_ratio)
+        * ratio_gain
+        / (fsdp_count * valid_len * width)
+    )
+    summed = summed[:, :share_columns] * coef
+    for unit in (4, 1):
+        summed = four_sum([summed] + [exchange(summed, "fsdp", unit * k) for k in (1, 2, 3)])
+
     parts = [exchange(summed, "blk", k) for k in (1, 2, 3)]
-    next_latents, *parts = lax.optimization_barrier((next_latents, *parts))
     up_mine, grad_down = pl.pallas_call(
         rows_body,
         out_shape=(

time: 297 us -> 283 us (0.953)
  local copies, waits for them, and re-layouts: 15.8 us -> 7.93 us
  other arithmetic: 8.55 us -> 5.06 us
  starting transfers between devices: 103 us -> 100 us
    unnamed x75 -> x61, local copies, waits for them, and re-layouts: 10.3 us -> 3.94 us
  transfers between devices with their start and end apart: 44 -> 44, of which waited for: 21 -> 25; matrix products, arithmetic and copies ran while one was open for 4% -> 3% of each run, Pallas kernels for 13% -> 14%
where the time goes in v2:
time: 283 us; the launch traced here: 281 us
  starting transfers between devices  100 us (35%)
  waiting for transfers between devices  93.3 us (33%)
  Pallas kernels  56.5 us (20%)
  between operations  18.5 us (7%)
  local copies, waits for them, and re-layouts  7.93 us (3%)
  other arithmetic  5.06 us (2%)
    ppermute x26, waiting for transfers between devices, exchange(): return lax.ppermute(x, axis, [(i, i ^ mask) for i in range(n)])  45.6 us
    ppermute x26, starting transfers between devices, exchange(): return lax.ppermute(x, axis, [(i, i ^ mask) for i in range(n)])  39.4 us
    ppermute x8, starting transfers between devices, return_tokens(): return lax.ppermute(x, ('fsdp', 'uly', 'blk'), pairs)  27.7 us
    ppermute x3, waiting for transfers between devices, gather_tokens(): return lax.ppermute(x, ('fsdp', 'blk'), pairs)  27 us
    ppermute x3, starting transfers between devices, gather_tokens(): return lax.ppermute(x, ('fsdp', 'blk'), pairs)  25.3 us
    pallas_call x2, Pallas kernels, attend(): pl.pallas_call(attention_body, out_shape=[jax.ShapeDtypeStruct((seg, head...  21.1 us
    ppermute x5, waiting for transfers between devices, shift(): return lax.ppermute(x, axis, [(i, (i + step) % n) for i in range(n)])  14.6 us
    pallas_call x1, Pallas kernels, shards(): pl.pallas_call(project_body, out_shape=(jax.ShapeDtypeStruct((heads_here,...  12.6 us
  transfers between devices with their start and end apart: 44, of which 25 were waited for; matrix products, arithmetic and copies ran while one was open for 3% of the time, Pallas kernels for 14%

profile of v2, /device:TPU:1, one launch (start us, length us, event | category | flops | bytes accessed | tf_op | source)
XLA Modules:
  0.0 281.3 jit_solution(9623630548763557945)
XLA Ops:
  9.3 9.8 %collective-permute-start = (bf16[96,3072]{1,0:T(8,128)(2,1)S(1)}, bf16[96,3072]{1,0:T(8,128)(2,1)S(1)}, u32[]{:S(2)}, u32[]{:S(2)}) collective-permute-start(bf16[96,3072]{1,0:T(8,128)(2,1)S(1)} %get-tuple-element.64), channel_id=1, source_target_pairs={{0,0},{1,32},{2,48},{3,16},{16,34},{17,2},{18,18},{19,50},{32,1},{... | collective-permute-start | bytes 1769480 | tf_op jit(solution)/shard_map/ppermute | solution.py:43
  19.1 13.2 %collective-permute-done = bf16[96,3072]{1,0:T(8,128)(2,1)S(1)} collective-permute-done((bf16[96,3072]{1,0:T(8,128)(2,1)S(1)}, bf16[96,3072]{1,0:T(8,128)(2,1)S(1)}, u32[]{:S(2)}, u32[]{:S(2)}) %collective-permute-start) | collective-permute-done | bytes 589856 | tf_op jit(solution)/shard_map/ppermute | solution.py:43
  32.3 7.5 %collective-permute-start.1 = (bf16[96,3072]{1,0:T(8,128)(2,1)S(1)}, bf16[96,3072]{1,0:T(8,128)(2,1)S(1)}, u32[]{:S(2)}, u32[]{:S(2)}) collective-permute-start(bf16[96,3072]{1,0:T(8,128)(2,1)S(1)} %get-tuple-element.34), channel_id=1, source_target_pairs={{0,0},{1,32},{2,48},{3,16},{16,34},{17,2},{18,18},{19,50},{32,1},{... | collective-permute-start | bytes 1769480 | tf_op jit(solution)/shard_map/ppermute | solution.py:43
  43.0 13.0 %collective-permute-done.1 = bf16[96,3072]{1,0:T(8,128)(2,1)S(1)} collective-permute-done((bf16[96,3072]{1,0:T(8,128)(2,1)S(1)}, bf16[96,3072]{1,0:T(8,128)(2,1)S(1)}, u32[]{:S(2)}, u32[]{:S(2)}) %collective-permute-start.1) | collective-permute-done | bytes 589856 | tf_op jit(solution)/shard_map/ppermute | solution.py:43
  60.3 7.8 %collective-permute-done.5.right_b_ref = bf16[96,3072]{1,0:T(8,128)(2,1)S(1)} collective-permute-done((bf16[96,3072]{1,0:T(8,128)(2,1)S(1)}, bf16[96,3072]{1,0:T(8,128)(2,1)S(1)}, u32[]{:S(2)}, u32[]{:S(2)}) %collective-permute-start.5) | collective-permute-done | bytes 589856 | tf_op jit(solution)/shard_map/ppermute | solution.py:61
  70.3 3.8 %collective-permute-done.4.up_ref = bf16[192,3072]{1,0:T(8,128)(2,1)S(1)} collective-permute-done((bf16[192,3072]{1,0:T(8,128)(2,1)}, bf16[192,3072]{1,0:T(8,128)(2,1)S(1)}, u32[]{:S(2)}, u32[]{:S(2)}) %collective-permute-start.4) | collective-permute-done | bytes 1179680 | tf_op jit(solution)/shard_map/ppermute | solution.py:61
  74.1 3.0 %collective-permute-done.6.far_b_ref = bf16[96,3072]{1,0:T(8,128)(2,1)} collective-permute-done((bf16[96,3072]{1,0:T(8,128)(2,1)S(1)}, bf16[96,3072]{1,0:T(8,128)(2,1)}, u32[]{:S(2)}, u32[]{:S(2)}) %collective-permute-start.6) | collective-permute-done | bytes 589856 | tf_op jit(solution)/shard_map/ppermute | solution.py:61
  77.1 12.6 %project.1 = (bf16[3,768,256]{2,1,0:T(8,128)(2,1)}, bf16[3,768,128]{2,1,0:T(8,128)(2,1)}) custom-call(s32[1]{0:T(128)} %bitcast.8.ints_ref, bf16[96,3072]{1,0:T(8,128)(2,1)} %copy-done.4, bf16[96,3072]{1,0:T(8,128)(2,1)} %copy-done.1, bf16[96,3072]{1,0:T(8,128)(2,1)} %copy-done.5, bf16[96,3072]{1,0:T(8,128)(2,1)} %copy-done.8, bf16[192,3072]{1,0:T(8,128)(2,1)} %copy-done.6, ...), custom_call_target="tpu_custom_call" | custom-call | tf_op jit(solution)/shard_map/project/pallas_call | solution.py:344
  90.9 3.0 %collective-permute-start.12 = (bf16[2,768,256]{2,1,0:T(8,128)(2,1)S(1)}, bf16[2,768,256]{2,1,0:T(8,128)(2,1)S(1)}, u32[]{:S(2)}, u32[]{:S(2)}) collective-permute-start(bf16[2,768,256]{2,1,0:T(8,128)(2,1)S(1)} %slice.31), channel_id=1, source_target_pairs={{0,32},{16,48},{32,0},{48,16},{64,96},{80,112},{96,64},{112,80},{1... | collective-permute-start | bytes 2359304 | tf_op jit(solution)/shard_map/ppermute | solution.py:66
  94.0 4.4 %collective-permute-start.8 = (bf16[256,384]{1,0:T(8,128)(2,1)S(1)}, bf16[256,384]{1,0:T(8,128)(2,1)S(1)}, u32[]{:S(2)}, u32[]{:S(2)}) collective-permute-start(bf16[256,384]{1,0:T(8,128)(2,1)S(1)} %pad_maximum_fusion.1), channel_id=1, source_target_pairs={{0,8},{4,12},{8,0},{12,4},{1,9},{5,13},{9,1},{13,5},{2,10},{6,14},... | collective-permute-start | bytes 589832 | tf_op jit(solution)/shard_map/ppermute | solution.py:66
  99.1 4.5 %collective-permute-done.8 = bf16[256,384]{1,0:T(8,128)(2,1)S(1)} collective-permute-done((bf16[256,384]{1,0:T(8,128)(2,1)S(1)}, bf16[256,384]{1,0:T(8,128)(2,1)S(1)}, u32[]{:S(2)}, u32[]{:S(2)}) %collective-permute-start.8) | collective-permute-done | bytes 196640 | tf_op jit(solution)/shard_map/ppermute | solution.py:66
  110.4 8.2 %collective-permute-done.15.refs_2_ = bf16[1,768,256]{2,1,0:T(8,128)(2,1)S(1)} collective-permute-done((bf16[1,768,256]{2,1,0:T(8,128)(2,1)S(1)}, bf16[1,768,256]{2,1,0:T(8,128)(2,1)S(1)}, u32[]{:S(2)}, u32[]{:S(2)}) %collective-permute-start.15) | collective-permute-done | bytes 393248 | tf_op jit(solution)/shard_map/ppermute | solution.py:66
  120.3 8.0 %collective-permute-start.10 = (s32[8,128]{1,0:T(8,128)S(1)}, s32[8,128]{1,0:T(8,128)S(1)}, u32[]{:S(2)}, u32[]{:S(2)}) collective-permute-start(s32[8,128]{1,0:T(8,128)S(1)} %broadcast_in_dim.34), channel_id=1, source_target_pairs={{0,0},{1,32},{2,48},{3,16},{16,34},{17,2},{18,18},{19,50},{32,1},{... | collective-permute-start | bytes 12296 | tf_op jit(solution)/shard_map/ppermute | solution.py:43
  132.2 7.7 %attend.3 = (bf16[192,128]{1,0:T(8,128)(2,1)}, bf16[192,128]{1,0:T(8,128)(2,1)}, bf16[192,128]{1,0:T(8,128)(2,1)}, bf16[192,128]{1,0:T(8,128)(2,1)}) custom-call(bf16[3,768,128]{2,1,0:T(8,128)(2,1)} %get-tuple-element.38.q_ref, f32[1,3072]{1,0:T(1,128)} %compare_select_fusion.bias_ref, bf16[3,768,256]{2,1,0:T(8,128)(2,1)} %get-tuple-element.39.refs_0_, ...), custom_call_target="tpu_custom_call" | custom-call | tf_op jit(solution)/shard_map/attend/pallas_call | solution.py:177
  140.0 6.6 %collective-permute-start.17 = (bf16[192,128]{1,0:T(8,128)(2,1)}, bf16[192,128]{1,0:T(8,128)(2,1)S(1)}, u32[]{:S(2)}, u32[]{:S(2)}) collective-permute-start(bf16[192,128]{1,0:T(8,128)(2,1)} %get-tuple-element.42), channel_id=1, source_target_pairs={{0,0},{4,4},{8,8},{12,12},{32,1},{36,5},{40,9},{44,13},{48,2},{52,... | collective-permute-start | bytes 147464 | tf_op jit(solution)/shard_map/ppermute | solution.py:56
  146.7 6.3 %collective-permute-start.21 = (bf16[192,128]{1,0:T(8,128)(2,1)}, bf16[192,128]{1,0:T(8,128)(2,1)S(1)}, u32[]{:S(2)}, u32[]{:S(2)}) collective-permute-start(bf16[192,128]{1,0:T(8,128)(2,1)} %get-tuple-element.46), channel_id=1, source_target_pairs={{0,8},{4,12},{8,0},{12,4},{32,9},{36,13},{40,1},{44,5},{48,10},{52... | collective-permute-start | bytes 147464 | tf_op jit(solution)/shard_map/ppermute | solution.py:56
  154.1 13.4 %attend.2 = (bf16[192,256]{1,0:T(8,128)(2,1)}, bf16[192,256]{1,0:T(8,128)(2,1)}, bf16[192,256]{1,0:T(8,128)(2,1)}, bf16[192,256]{1,0:T(8,128)(2,1)}) custom-call(bf16[3,768,128]{2,1,0:T(8,128)(2,1)} %get-tuple-element.38.q_ref, f32[1,3072]{1,0:T(1,128)} %compare_select_fusion.bias_ref, bf16[3,768,256]{2,1,0:T(8,128)(2,1)} %get-tuple-element.39.refs_0_, ...), custom_call_target="tpu_custom_call" | custom-call | tf_op jit(solution)/shard_map/attend/pallas_call | solution.py:177
  167.4 6.1 %collective-permute-start.14 = (bf16[192,256]{1,0:T(8,128)(2,1)}, bf16[192,256]{1,0:T(8,128)(2,1)S(1)}, u32[]{:S(2)}, u32[]{:S(2)}) collective-permute-start(bf16[192,256]{1,0:T(8,128)(2,1)} %get-tuple-element.40), channel_id=1, source_target_pairs={{0,0},{4,4},{8,8},{12,12},{32,1},{36,5},{40,9},{44,13},{48,2},{52,... | collective-permute-start | bytes 294920 | tf_op jit(solution)/shard_map/ppermute | solution.py:56
  173.7 6.4 %collective-permute-start.20 = (bf16[192,256]{1,0:T(8,128)(2,1)}, bf16[192,256]{1,0:T(8,128)(2,1)S(1)}, u32[]{:S(2)}, u32[]{:S(2)}) collective-permute-start(bf16[192,256]{1,0:T(8,128)(2,1)} %get-tuple-element.45), channel_id=1, source_target_pairs={{0,8},{4,12},{8,0},{12,4},{32,9},{36,13},{40,1},{44,5},{48,10},{52... | collective-permute-start | bytes 294920 | tf_op jit(solution)/shard_map/ppermute | solution.py:56
  184.3 5.1 %collective-permute-done.22.refs_6_ = bf16[192,256]{1,0:T(8,128)(2,1)S(1)} collective-permute-done((bf16[192,256]{1,0:T(8,128)(2,1)}, bf16[192,256]{1,0:T(8,128)(2,1)S(1)}, u32[]{:S(2)}, u32[]{:S(2)}) %collective-permute-start.22) | collective-permute-done | bytes 98336 | tf_op jit(solution)/shard_map/ppermute | solution.py:56
  190.1 4.5 %standard.1 = (bf16[192,1536]{1,0:T(8,128)(2,1)}, bf16[192,64]{1,0:T(8,128)(2,1)}, bf16[192,3072]{1,0:T(8,128)(2,1)}, f32[8,128]{1,0:T(8,128)}) custom-call(s32[2]{0:T(128)} %pad_add_fusion.ints_ref, f32[1]{0:T(128)} %bitcast.4.gain_ref, bf16[64,1536]{1,0:T(8,128)(2,1)} %slice.36.down_ref, bf16[64,3072]{1,0:T(8,128)(2,1)} %up_ref.3, ...), custom_call_target="tpu_custom_call" | custom-call | tf_op jit(solution)/shard_map/standard/pallas_call | solution.py:405
  194.6 3.7 %products.1 = (f32[64,1280]{1,0:T(8,128)}, f32[64,1280]{1,0:T(8,128)}, f32[64,1280]{1,0:T(8,128)}, f32[64,1280]{1,0:T(8,128)}) custom-call(s32[1]{0:T(128)} %bitcast.8.ints_ref, bf16[192,64]{1,0:T(8,128)(2,1)} %get-tuple-element.51.narrow_ref, bf16[192,3072]{1,0:T(8,128)(2,1)} %get-tuple-element.52.masked_ref, bf16[64,3072]{1,0:T(8,128)(2,1)} %up_ref.3, ...), custom_call_target="tpu_custom_call" | custom-call | tf_op jit(solution)/shard_map/products/pallas_call | solution.py:420
  202.8 8.8 %move.1 = bf16[192,3072]{1,0:T(8,128)(2,1)} custom-call(f32[4]{0:T(128)} %pad_maximum_fusion.2.scalars_ref, bf16[192,1536]{1,0:T(8,128)(2,1)} %get-tuple-element.49.own_ref, bf16[3072,1536]{1,0:T(8,128)(2,1)} %all-gather.5.cloned.1.call-done.w_ref, bf16[192,3072]{1,0:T(8,128)(2,1)} %bitcast.23, bf16[192,3072]{1,0:T(8,128)(2,1)} %bitcast.22), custom_call_target="tpu_custom_call" | custom-call | tf_op jit(solution)/shard_map/move/pallas_call | solution.py:439
  213.6 4.0 %collective-permute-start.29 = (f32[16,1280]{1,0:T(8,128)S(1)}, f32[16,1280]{1,0:T(8,128)S(1)}, u32[]{:S(2)}, u32[]{:S(2)}) collective-permute-start(f32[16,1280]{1,0:T(8,128)S(1)} %get-tuple-element.67), channel_id=1, source_target_pairs={{0,3},{1,2},{2,1},{3,0},{4,7},{5,6},{6,5},{7,4},{8,11},{9,10},{10,... | collective-permute-start | bytes 245768 | tf_op jit(solution)/shard_map/ppermute | solution.py:66
  218.2 3.7 %collective-permute-done.28 = f32[16,1280]{1,0:T(8,128)S(1)} collective-permute-done((f32[16,1280]{1,0:T(8,128)S(1)}, f32[16,1280]{1,0:T(8,128)S(1)}, u32[]{:S(2)}, u32[]{:S(2)}) %collective-permute-start.28) | collective-permute-done | bytes 81952 | tf_op jit(solution)/shard_map/ppermute | solution.py:66
  224.4 4.1 %collective-permute-start.31 = (f32[16,1152]{1,0:T(8,128)S(1)}, f32[16,1152]{1,0:T(8,128)S(1)}, u32[]{:S(2)}, u32[]{:S(2)}) collective-permute-start(f32[16,1152]{1,0:T(8,128)S(1)} %slice_multiply_fusion), channel_id=1, source_target_pairs={{0,128},{16,144},{32,160},{48,176},{64,192},{80,208},{96,224},{112... | collective-permute-start | bytes 221192 | tf_op jit(solution)/shard_map/ppermute | solution.py:66
  228.4 2.7 collective-permute-done.31
  244.2 3.0 %collective-permute-start.37 = (f32[16,1152]{1,0:T(8,128)S(1)}, f32[16,1152]{1,0:T(8,128)S(1)}, u32[]{:S(2)}, u32[]{:S(2)}) collective-permute-start(f32[16,1152]{1,0:T(8,128)S(1)} %add_add_fusion.2.refs_0_), channel_id=1, source_target_pairs={{0,2},{1,3},{2,0},{3,1},{4,6},{5,7},{6,4},{7,5},{8,10},{9,11},{10,... | collective-permute-start | bytes 221192 | tf_op jit(solution)/shard_map/ppermute | solution.py:66
  248.2 3.2 %collective-permute-done.37.refs_2_ = f32[16,1152]{1,0:T(8,128)S(1)} collective-permute-done((f32[16,1152]{1,0:T(8,128)S(1)}, f32[16,1152]{1,0:T(8,128)S(1)}, u32[]{:S(2)}, u32[]{:S(2)}) %collective-permute-start.37) | collective-permute-done | bytes 73760 | tf_op jit(solution)/shard_map/ppermute | solution.py:66
  251.3 2.8 collective-permute-done.38.refs_3_
  262.1 5.4 %collective-permute-done.40.refs_2_ = f32[64,768]{1,0:T(8,128)S(1)} collective-permute-done((f32[64,768]{1,0:T(8,128)}, f32[64,768]{1,0:T(8,128)S(1)}, u32[]{:S(2)}, u32[]{:S(2)}) %collective-permute-start.40) | collective-permute-done | bytes 196640 | tf_op jit(solution)/shard_map/ppermute | solution.py:66
  267.4 3.1 %collective-permute-done.41.refs_3_ = f32[64,768]{1,0:T(8,128)S(1)} collective-permute-done((f32[64,768]{1,0:T(8,128)}, f32[64,768]{1,0:T(8,128)S(1)}, u32[]{:S(2)}, u32[]{:S(2)}) %collective-permute-start.41) | collective-permute-done | bytes 196640 | tf_op jit(solution)/shard_map/ppermute | solution.py:66
  (154 shorter events, 63.7 us)
Async XLA Ops:
  7.2 69.9 %all-gather.3.cloned.1.call-start = ((), (), s32[]{:S(2)}) async-start(), calls=%async_computation | async-start | bytes 7520256 | tf_op jit(solution)/shard_map/all_gather | solution.py:331
  9.2 193.6 %all-gather.5.cloned.1.call-start = ((), (), s32[]{:S(2)}) async-start(), calls=%async_computation.1 | async-start | bytes 10027008 | tf_op jit(solution)/shard_map/all_gather | solution.py:378
  9.3 22.9 %collective-permute-start = (bf16[96,3072]{1,0:T(8,128)(2,1)S(1)}, bf16[96,3072]{1,0:T(8,128)(2,1)S(1)}, u32[]{:S(2)}, u32[]{:S(2)}) collective-permute-start(bf16[96,3072]{1,0:T(8,128)(2,1)S(1)} %get-tuple-element.64), channel_id=1, source_target_pairs={{0,0},{1,32},{2,48},{3,16},{16,34},{17,2},{18,18},{19,50},{32,1},{... | collective-permute-start | bytes 1769480 | tf_op jit(solution)/shard_map/ppermute | solution.py:43
  32.3 23.7 %collective-permute-start.1 = (bf16[96,3072]{1,0:T(8,128)(2,1)S(1)}, bf16[96,3072]{1,0:T(8,128)(2,1)S(1)}, u32[]{:S(2)}, u32[]{:S(2)}) collective-permute-start(bf16[96,3072]{1,0:T(8,128)(2,1)S(1)} %get-tuple-element.34), channel_id=1, source_target_pairs={{0,0},{1,32},{2,48},{3,16},{16,34},{17,2},{18,18},{19,50},{32,1},{... | collective-permute-start | bytes 1769480 | tf_op jit(solution)/shard_map/ppermute | solution.py:43
  40.2 16.2 %collective-permute-start.2 = (bf16[96,3072]{1,0:T(8,128)(2,1)S(1)}, bf16[96,3072]{1,0:T(8,128)(2,1)S(1)}, u32[]{:S(2)}, u32[]{:S(2)}) collective-permute-start(bf16[96,3072]{1,0:T(8,128)(2,1)S(1)} %fusion.3.a_ref), channel_id=1, source_target_pairs={{0,4},{4,8},{8,12},{12,0},{1,5},{5,9},{9,13},{13,1},{2,6},{6,10},{... | collective-permute-start | bytes 1769480 | tf_op jit(solution)/shard_map/ppermute | solution.py:61
  41.5 14.9 %collective-permute-start.3 = (bf16[96,3072]{1,0:T(8,128)(2,1)S(1)}, bf16[96,3072]{1,0:T(8,128)(2,1)S(1)}, u32[]{:S(2)}, u32[]{:S(2)}) collective-permute-start(bf16[96,3072]{1,0:T(8,128)(2,1)S(1)} %fusion.3.a_ref), channel_id=1, source_target_pairs={{0,12},{4,0},{8,4},{12,8},{1,13},{5,1},{9,5},{13,9},{2,14},{6,2},{... | collective-permute-start | bytes 1769480 | tf_op jit(solution)/shard_map/ppermute | solution.py:61
  57.7 16.5 %collective-permute-start.4 = (bf16[192,3072]{1,0:T(8,128)(2,1)}, bf16[192,3072]{1,0:T(8,128)(2,1)S(1)}, u32[]{:S(2)}, u32[]{:S(2)}) collective-permute-start(bf16[192,3072]{1,0:T(8,128)(2,1)} %pad_maximum_fusion), channel_id=1, source_target_pairs={{0,4},{4,8},{8,12},{12,0},{1,5},{5,9},{9,13},{13,1},{2,6},{6,10},{... | collective-permute-start | bytes 3538952 | tf_op jit(solution)/shard_map/ppermute | solution.py:61
  59.0 9.1 %collective-permute-start.5 = (bf16[96,3072]{1,0:T(8,128)(2,1)S(1)}, bf16[96,3072]{1,0:T(8,128)(2,1)S(1)}, u32[]{:S(2)}, u32[]{:S(2)}) collective-permute-start(bf16[96,3072]{1,0:T(8,128)(2,1)S(1)} %fusion.1.b_ref), channel_id=1, source_target_pairs={{0,12},{4,0},{8,4},{12,8},{1,13},{5,1},{9,5},{13,9},{2,14},{6,2},{... | collective-permute-start | bytes 1769480 | tf_op jit(solution)/shard_map/ppermute | solution.py:61
  68.2 9.0 %collective-permute-start.6 = (bf16[96,3072]{1,0:T(8,128)(2,1)S(1)}, bf16[96,3072]{1,0:T(8,128)(2,1)}, u32[]{:S(2)}, u32[]{:S(2)}) collective-permute-start(bf16[96,3072]{1,0:T(8,128)(2,1)S(1)} %collective-permute-done.5.right_b_ref), channel_id=1, source_target_pairs={{0,12},{4,0},{8,4},{12,8},{1,13},{5,1},{9,5},{13,9},{2,14},{6,2},{... | collective-permute-start | bytes 1769480 | tf_op jit(solution)/shard_map/ppermute | solution.py:61
  90.9 15.8 %collective-permute-start.12 = (bf16[2,768,256]{2,1,0:T(8,128)(2,1)S(1)}, bf16[2,768,256]{2,1,0:T(8,128)(2,1)S(1)}, u32[]{:S(2)}, u32[]{:S(2)}) collective-permute-start(bf16[2,768,256]{2,1,0:T(8,128)(2,1)S(1)} %slice.31), channel_id=1, source_target_pairs={{0,32},{16,48},{32,0},{48,16},{64,96},{80,112},{96,64},{112,80},{1... | collective-permute-start | bytes 2359304 | tf_op jit(solution)/shard_map/ppermute | solution.py:66
  94.0 9.7 %collective-permute-start.8 = (bf16[256,384]{1,0:T(8,128)(2,1)S(1)}, bf16[256,384]{1,0:T(8,128)(2,1)S(1)}, u32[]{:S(2)}, u32[]{:S(2)}) collective-permute-start(bf16[256,384]{1,0:T(8,128)(2,1)S(1)} %pad_maximum_fusion.1), channel_id=1, source_target_pairs={{0,8},{4,12},{8,0},{12,4},{1,9},{5,13},{9,1},{13,5},{2,10},{6,14},... | collective-permute-start | bytes 589832 | tf_op jit(solution)/shard_map/ppermute | solution.py:66
  98.4 7.3 %collective-permute-start.9 = (bf16[256,384]{1,0:T(8,128)(2,1)S(1)}, bf16[256,384]{1,0:T(8,128)(2,1)S(1)}, u32[]{:S(2)}, u32[]{:S(2)}) collective-permute-start(bf16[256,384]{1,0:T(8,128)(2,1)S(1)} %pad_maximum_fusion.1), channel_id=1, source_target_pairs={{0,12},{4,8},{8,4},{12,0},{1,13},{5,9},{9,5},{13,1},{2,14},{6,10},... | collective-permute-start | bytes 589832 | tf_op jit(solution)/shard_map/ppermute | solution.py:66
  107.6 23.6 %collective-permute-start.11 = (bf16[3,768,256]{2,1,0:T(8,128)(2,1)S(1)}, bf16[3,768,256]{2,1,0:T(8,128)(2,1)S(1)}, u32[]{:S(2)}, u32[]{:S(2)}) collective-permute-start(bf16[3,768,256]{2,1,0:T(8,128)(2,1)S(1)} %copy-done), channel_id=1, source_target_pairs={{0,16},{16,0},{32,48},{48,32},{64,80},{80,64},{96,112},{112,96},{1... | collective-permute-start | bytes 3538952 | tf_op jit(solution)/shard_map/ppermute | solution.py:66
  107.8 10.8 %collective-permute-start.15 = (bf16[1,768,256]{2,1,0:T(8,128)(2,1)S(1)}, bf16[1,768,256]{2,1,0:T(8,128)(2,1)S(1)}, u32[]{:S(2)}, u32[]{:S(2)}) collective-permute-start(bf16[1,768,256]{2,1,0:T(8,128)(2,1)S(1)} %slice.32), channel_id=1, source_target_pairs={{0,32},{16,48},{32,0},{48,16},{64,96},{80,112},{96,64},{112,80},{1... | collective-permute-start | bytes 1179656 | tf_op jit(solution)/shard_map/ppermute | solution.py:66
  109.6 44.5 %collective-permute-start.13 = (bf16[2,768,256]{2,1,0:T(8,128)(2,1)}, bf16[2,768,256]{2,1,0:T(8,128)(2,1)}, u32[]{:S(2)}, u32[]{:S(2)}) collective-permute-start(bf16[2,768,256]{2,1,0:T(8,128)(2,1)} %copy-done.7), channel_id=1, source_target_pairs={{0,16},{16,0},{32,48},{48,32},{64,80},{80,64},{96,112},{112,96},{1... | collective-permute-start | bytes 2359304 | tf_op jit(solution)/shard_map/ppermute | solution.py:66
  118.6 12.6 %collective-permute-start.16 = (bf16[1,768,256]{2,1,0:T(8,128)(2,1)S(1)}, bf16[1,768,256]{2,1,0:T(8,128)(2,1)}, u32[]{:S(2)}, u32[]{:S(2)}) collective-permute-start(bf16[1,768,256]{2,1,0:T(8,128)(2,1)S(1)} %collective-permute-done.15.refs_2_), channel_id=1, source_target_pairs={{0,16},{16,0},{32,48},{48,32},{64,80},{80,64},{96,112},{112,96},{1... | collective-permute-start | bytes 1179656 | tf_op jit(solution)/shard_map/ppermute | solution.py:66
  120.3 8.8 %collective-permute-start.10 = (s32[8,128]{1,0:T(8,128)S(1)}, s32[8,128]{1,0:T(8,128)S(1)}, u32[]{:S(2)}, u32[]{:S(2)}) collective-permute-start(s32[8,128]{1,0:T(8,128)S(1)} %broadcast_in_dim.34), channel_id=1, source_target_pairs={{0,0},{1,32},{2,48},{3,16},{16,34},{17,2},{18,18},{19,50},{32,1},{... | collective-permute-start | bytes 12296 | tf_op jit(solution)/shard_map/ppermute | solution.py:43
  140.0 33.6 %collective-permute-start.17 = (bf16[192,128]{1,0:T(8,128)(2,1)}, bf16[192,128]{1,0:T(8,128)(2,1)S(1)}, u32[]{:S(2)}, u32[]{:S(2)}) collective-permute-start(bf16[192,128]{1,0:T(8,128)(2,1)} %get-tuple-element.42), channel_id=1, source_target_pairs={{0,0},{4,4},{8,8},{12,12},{32,1},{36,5},{40,9},{44,13},{48,2},{52,... | collective-permute-start | bytes 147464 | tf_op jit(solution)/shard_map/ppermute | solution.py:56
  146.5 27.1 %collective-permute-start.19 = (bf16[192,128]{1,0:T(8,128)(2,1)}, bf16[192,128]{1,0:T(8,128)(2,1)S(1)}, u32[]{:S(2)}, u32[]{:S(2)}) collective-permute-start(bf16[192,128]{1,0:T(8,128)(2,1)} %get-tuple-element.44), channel_id=1, source_target_pairs={{0,4},{4,0},{8,12},{12,8},{32,5},{36,1},{40,13},{44,9},{48,6},{52,... | collective-permute-start | bytes 147464 | tf_op jit(solution)/shard_map/ppermute | solution.py:56
  146.7 33.4 %collective-permute-start.21 = (bf16[192,128]{1,0:T(8,128)(2,1)}, bf16[192,128]{1,0:T(8,128)(2,1)S(1)}, u32[]{:S(2)}, u32[]{:S(2)}) collective-permute-start(bf16[192,128]{1,0:T(8,128)(2,1)} %get-tuple-element.46), channel_id=1, source_target_pairs={{0,8},{4,12},{8,0},{12,4},{32,9},{36,13},{40,1},{44,5},{48,10},{52... | collective-permute-start | bytes 147464 | tf_op jit(solution)/shard_map/ppermute | solution.py:56
  153.0 30.3 %collective-permute-start.23 = (bf16[192,128]{1,0:T(8,128)(2,1)}, bf16[192,128]{1,0:T(8,128)(2,1)S(1)}, u32[]{:S(2)}, u32[]{:S(2)}) collective-permute-start(bf16[192,128]{1,0:T(8,128)(2,1)} %get-tuple-element.48), channel_id=1, source_target_pairs={{0,12},{4,8},{8,4},{12,0},{32,13},{36,9},{40,5},{44,1},{48,14},{52... | collective-permute-start | bytes 147464 | tf_op jit(solution)/shard_map/ppermute | solution.py:56
  167.4 15.8 %collective-permute-start.14 = (bf16[192,256]{1,0:T(8,128)(2,1)}, bf16[192,256]{1,0:T(8,128)(2,1)S(1)}, u32[]{:S(2)}, u32[]{:S(2)}) collective-permute-start(bf16[192,256]{1,0:T(8,128)(2,1)} %get-tuple-element.40), channel_id=1, source_target_pairs={{0,0},{4,4},{8,8},{12,12},{32,1},{36,5},{40,9},{44,13},{48,2},{52,... | collective-permute-start | bytes 294920 | tf_op jit(solution)/shard_map/ppermute | solution.py:56
  173.5 9.8 %collective-permute-start.18 = (bf16[192,256]{1,0:T(8,128)(2,1)}, bf16[192,256]{1,0:T(8,128)(2,1)S(1)}, u32[]{:S(2)}, u32[]{:S(2)}) collective-permute-start(bf16[192,256]{1,0:T(8,128)(2,1)} %get-tuple-element.43), channel_id=1, source_target_pairs={{0,4},{4,0},{8,12},{12,8},{32,5},{36,1},{40,13},{44,9},{48,6},{52,... | collective-permute-start | bytes 294920 | tf_op jit(solution)/shard_map/ppermute | solution.py:56
  173.7 10.7 %collective-permute-start.20 = (bf16[192,256]{1,0:T(8,128)(2,1)}, bf16[192,256]{1,0:T(8,128)(2,1)S(1)}, u32[]{:S(2)}, u32[]{:S(2)}) collective-permute-start(bf16[192,256]{1,0:T(8,128)(2,1)} %get-tuple-element.45), channel_id=1, source_target_pairs={{0,8},{4,12},{8,0},{12,4},{32,9},{36,13},{40,1},{44,5},{48,10},{52... | collective-permute-start | bytes 294920 | tf_op jit(solution)/shard_map/ppermute | solution.py:56
  180.1 9.4 %collective-permute-start.22 = (bf16[192,256]{1,0:T(8,128)(2,1)}, bf16[192,256]{1,0:T(8,128)(2,1)S(1)}, u32[]{:S(2)}, u32[]{:S(2)}) collective-permute-start(bf16[192,256]{1,0:T(8,128)(2,1)} %get-tuple-element.47), channel_id=1, source_target_pairs={{0,12},{4,8},{8,4},{12,0},{32,13},{36,9},{40,5},{44,1},{48,14},{52... | collective-permute-start | bytes 294920 | tf_op jit(solution)/shard_map/ppermute | solution.py:56
  198.3 13.3 %collective-permute-start.24 = (f32[64,1280]{1,0:T(8,128)}, f32[64,1280]{1,0:T(8,128)S(1)}, u32[]{:S(2)}, u32[]{:S(2)}) collective-permute-start(f32[64,1280]{1,0:T(8,128)} %get-tuple-element.54), channel_id=1, source_target_pairs={{0,4},{4,0},{8,12},{12,8},{1,5},{5,1},{9,13},{13,9},{2,6},{6,2},{1... | collective-permute-start | bytes 983048 | tf_op jit(solution)/shard_map/ppermute | solution.py:66
  198.3 13.3 %collective-permute-start.25 = (f32[64,1280]{1,0:T(8,128)}, f32[64,1280]{1,0:T(8,128)S(1)}, u32[]{:S(2)}, u32[]{:S(2)}) collective-permute-start(f32[64,1280]{1,0:T(8,128)} %get-tuple-element.55), channel_id=1, source_target_pairs={{0,8},{4,12},{8,0},{12,4},{1,9},{5,13},{9,1},{13,5},{2,10},{6,14},... | collective-permute-start | bytes 983048 | tf_op jit(solution)/shard_map/ppermute | solution.py:66
  200.8 10.9 %collective-permute-start.26 = (f32[64,1280]{1,0:T(8,128)}, f32[64,1280]{1,0:T(8,128)S(1)}, u32[]{:S(2)}, u32[]{:S(2)}) collective-permute-start(f32[64,1280]{1,0:T(8,128)} %get-tuple-element.56), channel_id=1, source_target_pairs={{0,12},{4,8},{8,4},{12,0},{1,13},{5,9},{9,5},{13,1},{2,14},{6,10},... | collective-permute-start | bytes 983048 | tf_op jit(solution)/shard_map/ppermute | solution.py:66
  213.6 8.3 %collective-permute-start.28 = (f32[16,1280]{1,0:T(8,128)S(1)}, f32[16,1280]{1,0:T(8,128)S(1)}, u32[]{:S(2)}, u32[]{:S(2)}) collective-permute-start(f32[16,1280]{1,0:T(8,128)S(1)} %get-tuple-element.68), channel_id=1, source_target_pairs={{0,2},{1,3},{2,0},{3,1},{4,6},{5,7},{6,4},{7,5},{8,10},{9,11},{10,... | collective-permute-start | bytes 245768 | tf_op jit(solution)/shard_map/ppermute | solution.py:66
  213.6 9.4 %collective-permute-start.29 = (f32[16,1280]{1,0:T(8,128)S(1)}, f32[16,1280]{1,0:T(8,128)S(1)}, u32[]{:S(2)}, u32[]{:S(2)}) collective-permute-start(f32[16,1280]{1,0:T(8,128)S(1)} %get-tuple-element.67), channel_id=1, source_target_pairs={{0,3},{1,2},{2,1},{3,0},{4,7},{5,6},{6,5},{7,4},{8,11},{9,10},{10,... | collective-permute-start | bytes 245768 | tf_op jit(solution)/shard_map/ppermute | solution.py:66
  256.4 11.0 %collective-permute-start.40 = (f32[64,768]{1,0:T(8,128)}, f32[64,768]{1,0:T(8,128)S(1)}, u32[]{:S(2)}, u32[]{:S(2)}) collective-permute-start(f32[64,768]{1,0:T(8,128)} %get-tuple-element.63.refs_0_), channel_id=1, source_target_pairs={{0,8},{4,12},{8,0},{12,4},{1,9},{5,13},{9,1},{13,5},{2,10},{6,14},... | collective-permute-start | bytes 589832 | tf_op jit(solution)/shard_map/ppermute | solution.py:66
  259.0 11.5 %collective-permute-start.41 = (f32[64,768]{1,0:T(8,128)}, f32[64,768]{1,0:T(8,128)S(1)}, u32[]{:S(2)}, u32[]{:S(2)}) collective-permute-start(f32[64,768]{1,0:T(8,128)} %get-tuple-element.63.refs_0_), channel_id=1, source_target_pairs={{0,12},{4,8},{8,4},{12,0},{1,13},{5,9},{9,5},{13,1},{2,14},{6,10},... | collective-permute-start | bytes 589832 | tf_op jit(solution)/shard_map/ppermute | solution.py:66
  (41 other events, 274.6 us)
Sparse Core Ops, SparseCore 0:
  9.8 61.8 all-gather.2
  107.7 62.7 all-gather.4

commit v3 on v2

--- a/solution.py
+++ b/solution.py
@@ -118,7 +118,8 @@
 
 
 def attention_body(q_ref, bias_ref, *refs):
-    blocks, outs, (pairs_ref, scores_ref, acc_ref) = refs[:-7], refs[-7:-3], refs[-3:]
+    blocks, earlier = refs[:4], refs[4:-7]
+    outs, (pairs_ref, scores_ref, acc_ref) = refs[-7:-3], refs[-3:]
     scale = math.log2(math.e) / math.sqrt(HEAD_SIZE)
     at = 0
     for ref in blocks:
@@ -162,35 +163,39 @@
     out = (acc_ref[...] / jnp.sum(total, -1, keepdims=True)).astype(jnp.bfloat16)
     seg = rows // len(outs)
     for k, ref in enumerate(outs):
-        ref[...] = out[k * seg : (k + 1) * seg]
-
-
-def attend(query_rows, first_head, heads, blocks, bias):
+        ref[:, -HEAD_SIZE:] = out[k * seg : (k + 1) * seg]
+    for ref, before in zip(outs, earlier):
+        ref[:, :-HEAD_SIZE] = before[...]
+
+
+def attend(query_rows, first_head, heads, blocks, bias, earlier=()):
     rows = query_rows.shape[1]
     keys = bias.shape[1]
     seg = rows // 4
-    chunk = 512
+    columns = heads * HEAD_SIZE + sum(array.shape[1] for array in earlier[:1])
+    chunk = 1024
 
     def spec(array, place):
         return pl.BlockSpec((None,) + array.shape[1:], lambda i: (i + place, 0, 0))
 
     return pl.pallas_call(
         attention_body,
-        out_shape=[jax.ShapeDtypeStruct((seg, heads * HEAD_SIZE), jnp.bfloat16)] * 4,
+        out_shape=[jax.ShapeDtypeStruct((seg, columns), jnp.bfloat16)] * 4,
         grid=(heads,),
         in_specs=[
             pl.BlockSpec((None, rows, HEAD_SIZE), lambda i: (i + first_head, 0, 0)),
             pl.BlockSpec(bias.shape, lambda i: (0, 0)),
         ]
-        + [spec(array, place) for array, place in blocks],
-        out_specs=[pl.BlockSpec((seg, HEAD_SIZE), lambda i: (0, i))] * 4,
+        + [spec(array, place) for array, place in blocks]
+        + [pl.BlockSpec(array.shape, lambda i: (0, 0)) for array in earlier],
+        out_specs=[pl.BlockSpec((seg, columns // heads), lambda i: (0, i))] * 4,
         scratch_shapes=[
             pltpu.VMEM((keys, 2 * HEAD_SIZE), jnp.bfloat16),
             pltpu.VMEM((keys // chunk, rows, chunk), jnp.float32),
             pltpu.VMEM((rows, HEAD_SIZE), jnp.float32),
         ],
         name="attend",
-    )(query_rows, bias, *[array for array, _ in blocks])
+    )(query_rows, bias, *[array for array, _ in blocks], *earlier)
 
 
 def standard_body(ints_ref, gain_ref, down_ref, up_ref, noise_ref, *refs):
@@ -255,9 +260,9 @@
     rows = parts[0].shape[0]
     columns = up_ref.shape[1]
     for k, ref in enumerate(parts):
-        start = pl.multiple_of(jnp.bitwise_xor(ints_ref[0], k) * rows, 8)
+        start = pl.multiple_of(jnp.bitwise_xor(ints_ref[0], k) * rows, 16)
         up_ref[pl.ds(start, rows)] = ref[:, :columns]
-        down_ref[pl.ds(start, rows)] = ref[:, columns:]
+        down_ref[pl.ds(start, rows)] = ref[:, columns:].astype(jnp.float32)
 
 
 def columns_body(ints_ref, *refs):
@@ -265,7 +270,7 @@
     columns = parts[0].shape[1]
     for k, ref in enumerate(parts):
         start = pl.multiple_of(jnp.bitwise_xor(ints_ref[0], k) * columns, 128)
-        out_ref[:, pl.ds(start, columns)] = ref[...]
+        out_ref[:, pl.ds(start, columns)] = ref[...].astype(jnp.float32)
 
 
 def move_body(scalars_ref, own_ref, w_ref, latents_ref, noise_ref, out_ref):
@@ -377,21 +382,18 @@
     far_last = exchange(chip_last, "fsdp", 1)
     weight_full = lax.all_gather(after(output_columns, chip_lead), "fsdp", axis=0, tiled=True)
 
-    def others(segs):
-        return [return_tokens(segs[k], k) for k in range(4)]
-
     segs = attend(
         query_rows, 0, lead, ((key_values, 0), (core, 0), (chip_lead, 0), (far_lead, 0)), bias
     )
-    lead_pieces = others(segs)
     segs = attend(
         query_rows,
         lead,
         1,
         ((key_values, lead), (core, lead), (chip_last, 0), (far_last, 0)),
         bias,
-    )
-    last_pieces = others(segs)
+        segs,
+    )
+    pieces = [return_tokens(segs[k], k) for k in range(uly_count)]
 
     step_float = timestep_index[0].astype(jnp.float32)
     time_now = 1.0 - step_float / STEPS
@@ -401,7 +403,6 @@
     ratio_gain = jnp.sqrt(step_size) * drift_gain / noise_std
     valid_len = limit.astype(jnp.float32)
     ints = jnp.stack([(uly_id * blk_count + blk_id) * rows, limit]).astype(jnp.int32)
-    pieces = [p for both in zip(lead_pieces, last_pieces) for p in both]
     own_heads, narrow_projection, masked, log_tile = pl.pallas_call(
         standard_body,
         out_shape=(
@@ -470,11 +471,12 @@
     for unit in (4, 1):
         summed = four_sum([summed] + [exchange(summed, "fsdp", unit * k) for k in (1, 2, 3)])
 
+    summed = summed.astype(jnp.bfloat16)
     parts = [exchange(summed, "blk", k) for k in (1, 2, 3)]
     up_mine, grad_down = pl.pallas_call(
         rows_body,
         out_shape=(
-            jax.ShapeDtypeStruct((rank, up_columns), jnp.float32),
+            jax.ShapeDtypeStruct((rank, up_columns), jnp.bfloat16),
             jax.ShapeDtypeStruct((rank, local_columns), jnp.float32),
         ),
         in_specs=[smem] + [vmem] * 4,

time: 283 us -> 260 us (0.919)
  starting transfers between devices: 100 us -> 85.7 us
  waiting for transfers between devices: 93.3 us -> 88.8 us
  Pallas kernels: 56.5 us -> 53.2 us
    ppermute x8 -> x4, starting transfers between devices: 27.7 us -> 14.1 us  [return_tokens(): return lax.ppermute(x, ('fsdp', 'uly', 'blk'), pairs)]
    ppermute x26, waiting for transfers between devices: 45.6 us -> 39.5 us  [exchange(): return lax.ppermute(x, axis, [(i, i ^ mask) for i in range(n)])]
    pallas_call x2, Pallas kernels: 21.1 us -> 18.3 us  [attend(): pl.pallas_call(attention_body, out_shape=[jax.ShapeDtypeStruct((seg, colu...]
    ppermute x8 -> x4, waiting for transfers between devices: 6.12 us -> 7.76 us  [return_tokens(): return lax.ppermute(x, ('fsdp', 'uly', 'blk'), pairs)]
  transfers between devices with their start and end apart: 44 -> 40, of which waited for: 25 -> 24; matrix products, arithmetic and copies ran while one was open for 3% -> 3% of each run, Pallas kernels for 14% -> 14%
where the time goes in v3:
time: 260 us; the launch traced here: 259 us
  waiting for transfers between devices  88.8 us (34%)
  starting transfers between devices  85.7 us (33%)
  Pallas kernels  53.2 us (20%)
  between operations  18.4 us (7%)
  local copies, waits for them, and re-layouts  7.95 us (3%)
  other arithmetic  5.06 us (2%)
    ppermute x26, waiting for transfers between devices, exchange(): return lax.ppermute(x, axis, [(i, i ^ mask) for i in range(n)])  39.5 us
    ppermute x26, starting transfers between devices, exchange(): return lax.ppermute(x, axis, [(i, i ^ mask) for i in range(n)])  39 us
    ppermute x3, waiting for transfers between devices, gather_tokens(): return lax.ppermute(x, ('fsdp', 'blk'), pairs)  27 us
    ppermute x3, starting transfers between devices, gather_tokens(): return lax.ppermute(x, ('fsdp', 'blk'), pairs)  24.9 us
    pallas_call x2, Pallas kernels, attend(): pl.pallas_call(attention_body, out_shape=[jax.ShapeDtypeStruct((seg, colu...  18.3 us
    ppermute x5, waiting for transfers between devices, shift(): return lax.ppermute(x, axis, [(i, (i + step) % n) for i in range(n)])  14.6 us
    ppermute x4, starting transfers between devices, return_tokens(): return lax.ppermute(x, ('fsdp', 'uly', 'blk'), pairs)  14.1 us
    pallas_call x1, Pallas kernels, shards(): pl.pallas_call(project_body, out_shape=(jax.ShapeDtypeStruct((heads_here,...  12.6 us
  transfers between devices with their start and end apart: 40, of which 24 were waited for; matrix products, arithmetic and copies ran while one was open for 3% of the time, Pallas kernels for 14%

profile of v3, /device:TPU:1, one launch (start us, length us, event | category | flops | bytes accessed | tf_op | source)
XLA Modules:
  0.0 259.1 jit_solution(13970785925820974744)
XLA Ops:
  9.3 9.8 %collective-permute-start = (bf16[96,3072]{1,0:T(8,128)(2,1)S(1)}, bf16[96,3072]{1,0:T(8,128)(2,1)S(1)}, u32[]{:S(2)}, u32[]{:S(2)}) collective-permute-start(bf16[96,3072]{1,0:T(8,128)(2,1)S(1)} %get-tuple-element.64), channel_id=1, source_target_pairs={{0,0},{1,32},{2,48},{3,16},{16,34},{17,2},{18,18},{19,50},{32,1},{... | collective-permute-start | bytes 1769480 | tf_op jit(solution)/shard_map/ppermute | solution.py:43
  19.1 13.2 %collective-permute-done = bf16[96,3072]{1,0:T(8,128)(2,1)S(1)} collective-permute-done((bf16[96,3072]{1,0:T(8,128)(2,1)S(1)}, bf16[96,3072]{1,0:T(8,128)(2,1)S(1)}, u32[]{:S(2)}, u32[]{:S(2)}) %collective-permute-start) | collective-permute-done | bytes 589856 | tf_op jit(solution)/shard_map/ppermute | solution.py:43
  32.3 7.5 %collective-permute-start.1 = (bf16[96,3072]{1,0:T(8,128)(2,1)S(1)}, bf16[96,3072]{1,0:T(8,128)(2,1)S(1)}, u32[]{:S(2)}, u32[]{:S(2)}) collective-permute-start(bf16[96,3072]{1,0:T(8,128)(2,1)S(1)} %get-tuple-element.34), channel_id=1, source_target_pairs={{0,0},{1,32},{2,48},{3,16},{16,34},{17,2},{18,18},{19,50},{32,1},{... | collective-permute-start | bytes 1769480 | tf_op jit(solution)/shard_map/ppermute | solution.py:43
  43.0 13.0 %collective-permute-done.1 = bf16[96,3072]{1,0:T(8,128)(2,1)S(1)} collective-permute-done((bf16[96,3072]{1,0:T(8,128)(2,1)S(1)}, bf16[96,3072]{1,0:T(8,128)(2,1)S(1)}, u32[]{:S(2)}, u32[]{:S(2)}) %collective-permute-start.1) | collective-permute-done | bytes 589856 | tf_op jit(solution)/shard_map/ppermute | solution.py:43
  60.3 7.8 %collective-permute-done.5.right_b_ref = bf16[96,3072]{1,0:T(8,128)(2,1)S(1)} collective-permute-done((bf16[96,3072]{1,0:T(8,128)(2,1)S(1)}, bf16[96,3072]{1,0:T(8,128)(2,1)S(1)}, u32[]{:S(2)}, u32[]{:S(2)}) %collective-permute-start.5) | collective-permute-done | bytes 589856 | tf_op jit(solution)/shard_map/ppermute | solution.py:61
  70.3 3.8 %collective-permute-done.4.up_ref = bf16[192,3072]{1,0:T(8,128)(2,1)S(1)} collective-permute-done((bf16[192,3072]{1,0:T(8,128)(2,1)}, bf16[192,3072]{1,0:T(8,128)(2,1)S(1)}, u32[]{:S(2)}, u32[]{:S(2)}) %collective-permute-start.4) | collective-permute-done | bytes 1179680 | tf_op jit(solution)/shard_map/ppermute | solution.py:61
  74.1 3.0 %collective-permute-done.6.far_b_ref = bf16[96,3072]{1,0:T(8,128)(2,1)} collective-permute-done((bf16[96,3072]{1,0:T(8,128)(2,1)S(1)}, bf16[96,3072]{1,0:T(8,128)(2,1)}, u32[]{:S(2)}, u32[]{:S(2)}) %collective-permute-start.6) | collective-permute-done | bytes 589856 | tf_op jit(solution)/shard_map/ppermute | solution.py:61
  77.1 12.6 %project.1 = (bf16[3,768,256]{2,1,0:T(8,128)(2,1)}, bf16[3,768,128]{2,1,0:T(8,128)(2,1)}) custom-call(s32[1]{0:T(128)} %bitcast.8.ints_ref, bf16[96,3072]{1,0:T(8,128)(2,1)} %copy-done.4, bf16[96,3072]{1,0:T(8,128)(2,1)} %copy-done.1, bf16[96,3072]{1,0:T(8,128)(2,1)} %copy-done.5, bf16[96,3072]{1,0:T(8,128)(2,1)} %copy-done.8, bf16[192,3072]{1,0:T(8,128)(2,1)} %copy-done.6, ...), custom_call_target="tpu_custom_call" | custom-call | tf_op jit(solution)/shard_map/project/pallas_call | solution.py:349
  90.9 3.0 %collective-permute-start.12 = (bf16[2,768,256]{2,1,0:T(8,128)(2,1)S(1)}, bf16[2,768,256]{2,1,0:T(8,128)(2,1)S(1)}, u32[]{:S(2)}, u32[]{:S(2)}) collective-permute-start(bf16[2,768,256]{2,1,0:T(8,128)(2,1)S(1)} %slice.32), channel_id=1, source_target_pairs={{0,32},{16,48},{32,0},{48,16},{64,96},{80,112},{96,64},{112,80},{1... | collective-permute-start | bytes 2359304 | tf_op jit(solution)/shard_map/ppermute | solution.py:66
  94.0 4.4 %collective-permute-start.8 = (bf16[256,384]{1,0:T(8,128)(2,1)S(1)}, bf16[256,384]{1,0:T(8,128)(2,1)S(1)}, u32[]{:S(2)}, u32[]{:S(2)}) collective-permute-start(bf16[256,384]{1,0:T(8,128)(2,1)S(1)} %pad_maximum_fusion.1), channel_id=1, source_target_pairs={{0,8},{4,12},{8,0},{12,4},{1,9},{5,13},{9,1},{13,5},{2,10},{6,14},... | collective-permute-start | bytes 589832 | tf_op jit(solution)/shard_map/ppermute | solution.py:66
  99.1 4.5 %collective-permute-done.8 = bf16[256,384]{1,0:T(8,128)(2,1)S(1)} collective-permute-done((bf16[256,384]{1,0:T(8,128)(2,1)S(1)}, bf16[256,384]{1,0:T(8,128)(2,1)S(1)}, u32[]{:S(2)}, u32[]{:S(2)}) %collective-permute-start.8) | collective-permute-done | bytes 196640 | tf_op jit(solution)/shard_map/ppermute | solution.py:66
  110.1 9.4 %collective-permute-done.13.refs_2_ = bf16[1,768,256]{2,1,0:T(8,128)(2,1)S(1)} collective-permute-done((bf16[1,768,256]{2,1,0:T(8,128)(2,1)S(1)}, bf16[1,768,256]{2,1,0:T(8,128)(2,1)S(1)}, u32[]{:S(2)}, u32[]{:S(2)}) %collective-permute-start.13) | collective-permute-done | bytes 393248 | tf_op jit(solution)/shard_map/ppermute | solution.py:66
  120.8 7.7 %collective-permute-start.10 = (s32[8,128]{1,0:T(8,128)S(1)}, s32[8,128]{1,0:T(8,128)S(1)}, u32[]{:S(2)}, u32[]{:S(2)}) collective-permute-start(s32[8,128]{1,0:T(8,128)S(1)} %broadcast_in_dim.34), channel_id=1, source_target_pairs={{0,0},{1,32},{2,48},{3,16},{16,34},{17,2},{18,18},{19,50},{32,1},{... | collective-permute-start | bytes 12296 | tf_op jit(solution)/shard_map/ppermute | solution.py:43
  132.4 11.4 %attend.2 = (bf16[192,256]{1,0:T(8,128)(2,1)}, bf16[192,256]{1,0:T(8,128)(2,1)}, bf16[192,256]{1,0:T(8,128)(2,1)}, bf16[192,256]{1,0:T(8,128)(2,1)}) custom-call(bf16[3,768,128]{2,1,0:T(8,128)(2,1)} %get-tuple-element.38.q_ref, f32[1,3072]{1,0:T(1,128)} %compare_select_fusion.bias_ref, bf16[3,768,256]{2,1,0:T(8,128)(2,1)} %get-tuple-element.39.refs_0_, ...), custom_call_target="tpu_custom_call" | custom-call | tf_op jit(solution)/shard_map/attend/pallas_call | solution.py:181
  143.8 6.9 %attend.3 = (bf16[192,384]{1,0:T(8,128)(2,1)}, bf16[192,384]{1,0:T(8,128)(2,1)}, bf16[192,384]{1,0:T(8,128)(2,1)}, bf16[192,384]{1,0:T(8,128)(2,1)}) custom-call(bf16[3,768,128]{2,1,0:T(8,128)(2,1)} %get-tuple-element.38.q_ref, f32[1,3072]{1,0:T(1,128)} %compare_select_fusion.bias_ref, bf16[3,768,256]{2,1,0:T(8,128)(2,1)} %get-tuple-element.39.refs_0_, ...), custom_call_target="tpu_custom_call" | custom-call | tf_op jit(solution)/shard_map/attend/pallas_call | solution.py:181
  150.6 6.6 %collective-permute-start.16 = (bf16[192,384]{1,0:T(8,128)(2,1)}, bf16[192,384]{1,0:T(8,128)(2,1)S(1)}, u32[]{:S(2)}, u32[]{:S(2)}) collective-permute-start(bf16[192,384]{1,0:T(8,128)(2,1)} %get-tuple-element.45), channel_id=1, source_target_pairs={{0,0},{4,4},{8,8},{12,12},{32,1},{36,5},{40,9},{44,13},{48,2},{52,... | collective-permute-start | bytes 442376 | tf_op jit(solution)/shard_map/ppermute | solution.py:56
  157.4 6.3 %collective-permute-start.18 = (bf16[192,384]{1,0:T(8,128)(2,1)}, bf16[192,384]{1,0:T(8,128)(2,1)S(1)}, u32[]{:S(2)}, u32[]{:S(2)}) collective-permute-start(bf16[192,384]{1,0:T(8,128)(2,1)} %get-tuple-element.47), channel_id=1, source_target_pairs={{0,8},{4,12},{8,0},{12,4},{32,9},{36,13},{40,1},{44,5},{48,10},{52... | collective-permute-start | bytes 442376 | tf_op jit(solution)/shard_map/ppermute | solution.py:56
  166.9 3.0 %collective-permute-done.18.refs_2_ = bf16[192,384]{1,0:T(8,128)(2,1)S(1)} collective-permute-done((bf16[192,384]{1,0:T(8,128)(2,1)}, bf16[192,384]{1,0:T(8,128)(2,1)S(1)}, u32[]{:S(2)}, u32[]{:S(2)}) %collective-permute-start.18) | collective-permute-done | bytes 147488 | tf_op jit(solution)/shard_map/ppermute | solution.py:56
  169.8 4.8 %collective-permute-done.19.refs_3_ = bf16[192,384]{1,0:T(8,128)(2,1)S(1)} collective-permute-done((bf16[192,384]{1,0:T(8,128)(2,1)}, bf16[192,384]{1,0:T(8,128)(2,1)S(1)}, u32[]{:S(2)}, u32[]{:S(2)}) %collective-permute-start.19) | collective-permute-done | bytes 147488 | tf_op jit(solution)/shard_map/ppermute | solution.py:56
  175.3 4.5 %standard.1 = (bf16[192,1536]{1,0:T(8,128)(2,1)}, bf16[192,64]{1,0:T(8,128)(2,1)}, bf16[192,3072]{1,0:T(8,128)(2,1)}, f32[8,128]{1,0:T(8,128)}) custom-call(s32[2]{0:T(128)} %pad_add_fusion.ints_ref, f32[1]{0:T(128)} %bitcast.4.gain_ref, bf16[64,1536]{1,0:T(8,128)(2,1)} %slice.36.down_ref, bf16[64,3072]{1,0:T(8,128)(2,1)} %up_ref.3, ...), custom_call_target="tpu_custom_call" | custom-call | tf_op jit(solution)/shard_map/standard/pallas_call | solution.py:406
  179.8 3.7 %products.1 = (f32[64,1280]{1,0:T(8,128)}, f32[64,1280]{1,0:T(8,128)}, f32[64,1280]{1,0:T(8,128)}, f32[64,1280]{1,0:T(8,128)}) custom-call(s32[1]{0:T(128)} %bitcast.8.ints_ref, bf16[192,64]{1,0:T(8,128)(2,1)} %get-tuple-element.51.narrow_ref, bf16[192,3072]{1,0:T(8,128)(2,1)} %get-tuple-element.52.masked_ref, bf16[64,3072]{1,0:T(8,128)(2,1)} %up_ref.3, ...), custom_call_target="tpu_custom_call" | custom-call | tf_op jit(solution)/shard_map/products/pallas_call | solution.py:421
  183.5 2.6 collective-permute-start.21
  188.0 8.8 %move.1 = bf16[192,3072]{1,0:T(8,128)(2,1)} custom-call(f32[4]{0:T(128)} %pad_maximum_fusion.2.scalars_ref, bf16[192,1536]{1,0:T(8,128)(2,1)} %get-tuple-element.49.own_ref, bf16[3072,1536]{1,0:T(8,128)(2,1)} %all-gather.5.cloned.1.call-done.w_ref, bf16[192,3072]{1,0:T(8,128)(2,1)} %bitcast.23, bf16[192,3072]{1,0:T(8,128)(2,1)} %bitcast.22), custom_call_target="tpu_custom_call" | custom-call | tf_op jit(solution)/shard_map/move/pallas_call | solution.py:440
  198.4 4.4 %collective-permute-start.25 = (f32[16,1280]{1,0:T(8,128)S(1)}, f32[16,1280]{1,0:T(8,128)S(1)}, u32[]{:S(2)}, u32[]{:S(2)}) collective-permute-start(f32[16,1280]{1,0:T(8,128)S(1)} %get-tuple-element.67), channel_id=1, source_target_pairs={{0,3},{1,2},{2,1},{3,0},{4,7},{5,6},{6,5},{7,4},{8,11},{9,10},{10,... | collective-permute-start | bytes 245768 | tf_op jit(solution)/shard_map/ppermute | solution.py:66
  203.5 3.0 %collective-permute-done.24 = f32[16,1280]{1,0:T(8,128)S(1)} collective-permute-done((f32[16,1280]{1,0:T(8,128)S(1)}, f32[16,1280]{1,0:T(8,128)S(1)}, u32[]{:S(2)}, u32[]{:S(2)}) %collective-permute-start.24) | collective-permute-done | bytes 81952 | tf_op jit(solution)/shard_map/ppermute | solution.py:66
  209.3 4.5 %collective-permute-start.27 = (f32[16,1152]{1,0:T(8,128)S(1)}, f32[16,1152]{1,0:T(8,128)S(1)}, u32[]{:S(2)}, u32[]{:S(2)}) collective-permute-start(f32[16,1152]{1,0:T(8,128)S(1)} %slice_multiply_fusion), channel_id=1, source_target_pairs={{0,128},{16,144},{32,160},{48,176},{64,192},{80,208},{96,224},{112... | collective-permute-start | bytes 221192 | tf_op jit(solution)/shard_map/ppermute | solution.py:66
  216.3 2.7 %collective-permute-done.28 = f32[16,1152]{1,0:T(8,128)S(1)} collective-permute-done((f32[16,1152]{1,0:T(8,128)S(1)}, f32[16,1152]{1,0:T(8,128)S(1)}, u32[]{:S(2)}, u32[]{:S(2)}) %collective-permute-start.28) | collective-permute-done | bytes 73760 | tf_op jit(solution)/shard_map/ppermute | solution.py:66
  219.1 2.9 %collective-permute-start.29 = (f32[16,1152]{1,0:T(8,128)S(1)}, f32[16,1152]{1,0:T(8,128)S(1)}, u32[]{:S(2)}, u32[]{:S(2)}) collective-permute-start(f32[16,1152]{1,0:T(8,128)S(1)} %add_add_fusion.2), channel_id=1, source_target_pairs={{0,16},{16,0},{32,48},{48,32},{64,80},{80,64},{96,112},{112,96},{1... | collective-permute-start | bytes 221192 | tf_op jit(solution)/shard_map/ppermute | solution.py:66
  229.7 3.3 %collective-permute-start.33 = (bf16[16,1152]{1,0:T(8,128)(2,1)S(1)}, bf16[16,1152]{1,0:T(8,128)(2,1)S(1)}, u32[]{:S(2)}, u32[]{:S(2)}) collective-permute-start(bf16[16,1152]{1,0:T(8,128)(2,1)S(1)} %add_convert_fusion.refs_0_), channel_id=1, source_target_pairs={{0,2},{1,3},{2,0},{3,1},{4,6},{5,7},{6,4},{7,5},{8,10},{9,11},{10,... | collective-permute-start | bytes 110600 | tf_op jit(solution)/shard_map/ppermute | solution.py:66
  233.5 2.9 %collective-permute-done.33.refs_2_ = bf16[16,1152]{1,0:T(8,128)(2,1)S(1)} collective-permute-done((bf16[16,1152]{1,0:T(8,128)(2,1)S(1)}, bf16[16,1152]{1,0:T(8,128)(2,1)S(1)}, u32[]{:S(2)}, u32[]{:S(2)}) %collective-permute-start.33) | collective-permute-done | bytes 36896 | tf_op jit(solution)/shard_map/ppermute | solution.py:66
  240.0 2.6 collective-permute-start.36
  246.0 2.6 collective-permute-done.37.refs_3_
  (138 shorter events, 53.8 us)
Async XLA Ops:
  7.2 69.9 %all-gather.3.cloned.1.call-start = ((), (), s32[]{:S(2)}) async-start(), calls=%async_computation | async-start | bytes 7520256 | tf_op jit(solution)/shard_map/all_gather | solution.py:336
  9.2 178.8 %all-gather.5.cloned.1.call-start = ((), (), s32[]{:S(2)}) async-start(), calls=%async_computation.1 | async-start | bytes 10027008 | tf_op jit(solution)/shard_map/all_gather | solution.py:383
  9.3 23.0 %collective-permute-start = (bf16[96,3072]{1,0:T(8,128)(2,1)S(1)}, bf16[96,3072]{1,0:T(8,128)(2,1)S(1)}, u32[]{:S(2)}, u32[]{:S(2)}) collective-permute-start(bf16[96,3072]{1,0:T(8,128)(2,1)S(1)} %get-tuple-element.64), channel_id=1, source_target_pairs={{0,0},{1,32},{2,48},{3,16},{16,34},{17,2},{18,18},{19,50},{32,1},{... | collective-permute-start | bytes 1769480 | tf_op jit(solution)/shard_map/ppermute | solution.py:43
  32.3 23.7 %collective-permute-start.1 = (bf16[96,3072]{1,0:T(8,128)(2,1)S(1)}, bf16[96,3072]{1,0:T(8,128)(2,1)S(1)}, u32[]{:S(2)}, u32[]{:S(2)}) collective-permute-start(bf16[96,3072]{1,0:T(8,128)(2,1)S(1)} %get-tuple-element.34), channel_id=1, source_target_pairs={{0,0},{1,32},{2,48},{3,16},{16,34},{17,2},{18,18},{19,50},{32,1},{... | collective-permute-start | bytes 1769480 | tf_op jit(solution)/shard_map/ppermute | solution.py:43
  40.2 16.2 %collective-permute-start.2 = (bf16[96,3072]{1,0:T(8,128)(2,1)S(1)}, bf16[96,3072]{1,0:T(8,128)(2,1)S(1)}, u32[]{:S(2)}, u32[]{:S(2)}) collective-permute-start(bf16[96,3072]{1,0:T(8,128)(2,1)S(1)} %fusion.3.a_ref), channel_id=1, source_target_pairs={{0,4},{4,8},{8,12},{12,0},{1,5},{5,9},{9,13},{13,1},{2,6},{6,10},{... | collective-permute-start | bytes 1769480 | tf_op jit(solution)/shard_map/ppermute | solution.py:61
  41.5 14.9 %collective-permute-start.3 = (bf16[96,3072]{1,0:T(8,128)(2,1)S(1)}, bf16[96,3072]{1,0:T(8,128)(2,1)S(1)}, u32[]{:S(2)}, u32[]{:S(2)}) collective-permute-start(bf16[96,3072]{1,0:T(8,128)(2,1)S(1)} %fusion.3.a_ref), channel_id=1, source_target_pairs={{0,12},{4,0},{8,4},{12,8},{1,13},{5,1},{9,5},{13,9},{2,14},{6,2},{... | collective-permute-start | bytes 1769480 | tf_op jit(solution)/shard_map/ppermute | solution.py:61
  57.7 16.5 %collective-permute-start.4 = (bf16[192,3072]{1,0:T(8,128)(2,1)}, bf16[192,3072]{1,0:T(8,128)(2,1)S(1)}, u32[]{:S(2)}, u32[]{:S(2)}) collective-permute-start(bf16[192,3072]{1,0:T(8,128)(2,1)} %pad_maximum_fusion), channel_id=1, source_target_pairs={{0,4},{4,8},{8,12},{12,0},{1,5},{5,9},{9,13},{13,1},{2,6},{6,10},{... | collective-permute-start | bytes 3538952 | tf_op jit(solution)/shard_map/ppermute | solution.py:61
  59.0 9.1 %collective-permute-start.5 = (bf16[96,3072]{1,0:T(8,128)(2,1)S(1)}, bf16[96,3072]{1,0:T(8,128)(2,1)S(1)}, u32[]{:S(2)}, u32[]{:S(2)}) collective-permute-start(bf16[96,3072]{1,0:T(8,128)(2,1)S(1)} %fusion.1.b_ref), channel_id=1, source_target_pairs={{0,12},{4,0},{8,4},{12,8},{1,13},{5,1},{9,5},{13,9},{2,14},{6,2},{... | collective-permute-start | bytes 1769480 | tf_op jit(solution)/shard_map/ppermute | solution.py:61
  68.1 9.0 %collective-permute-start.6 = (bf16[96,3072]{1,0:T(8,128)(2,1)S(1)}, bf16[96,3072]{1,0:T(8,128)(2,1)}, u32[]{:S(2)}, u32[]{:S(2)}) collective-permute-start(bf16[96,3072]{1,0:T(8,128)(2,1)S(1)} %collective-permute-done.5.right_b_ref), channel_id=1, source_target_pairs={{0,12},{4,0},{8,4},{12,8},{1,13},{5,1},{9,5},{13,9},{2,14},{6,2},{... | collective-permute-start | bytes 1769480 | tf_op jit(solution)/shard_map/ppermute | solution.py:61
  90.9 15.8 %collective-permute-start.12 = (bf16[2,768,256]{2,1,0:T(8,128)(2,1)S(1)}, bf16[2,768,256]{2,1,0:T(8,128)(2,1)S(1)}, u32[]{:S(2)}, u32[]{:S(2)}) collective-permute-start(bf16[2,768,256]{2,1,0:T(8,128)(2,1)S(1)} %slice.32), channel_id=1, source_target_pairs={{0,32},{16,48},{32,0},{48,16},{64,96},{80,112},{96,64},{112,80},{1... | collective-permute-start | bytes 2359304 | tf_op jit(solution)/shard_map/ppermute | solution.py:66
  94.0 9.7 %collective-permute-start.8 = (bf16[256,384]{1,0:T(8,128)(2,1)S(1)}, bf16[256,384]{1,0:T(8,128)(2,1)S(1)}, u32[]{:S(2)}, u32[]{:S(2)}) collective-permute-start(bf16[256,384]{1,0:T(8,128)(2,1)S(1)} %pad_maximum_fusion.1), channel_id=1, source_target_pairs={{0,8},{4,12},{8,0},{12,4},{1,9},{5,13},{9,1},{13,5},{2,10},{6,14},... | collective-permute-start | bytes 589832 | tf_op jit(solution)/shard_map/ppermute | solution.py:66
  98.4 7.3 %collective-permute-start.9 = (bf16[256,384]{1,0:T(8,128)(2,1)S(1)}, bf16[256,384]{1,0:T(8,128)(2,1)S(1)}, u32[]{:S(2)}, u32[]{:S(2)}) collective-permute-start(bf16[256,384]{1,0:T(8,128)(2,1)S(1)} %pad_maximum_fusion.1), channel_id=1, source_target_pairs={{0,12},{4,8},{8,4},{12,0},{1,13},{5,9},{9,5},{13,1},{2,14},{6,10},... | collective-permute-start | bytes 589832 | tf_op jit(solution)/shard_map/ppermute | solution.py:66
  107.6 23.7 %collective-permute-start.11 = (bf16[3,768,256]{2,1,0:T(8,128)(2,1)S(1)}, bf16[3,768,256]{2,1,0:T(8,128)(2,1)S(1)}, u32[]{:S(2)}, u32[]{:S(2)}) collective-permute-start(bf16[3,768,256]{2,1,0:T(8,128)(2,1)S(1)} %copy-done), channel_id=1, source_target_pairs={{0,16},{16,0},{32,48},{48,32},{64,80},{80,64},{96,112},{112,96},{1... | collective-permute-start | bytes 3538952 | tf_op jit(solution)/shard_map/ppermute | solution.py:66
  107.8 23.6 %collective-permute-start.15 = (bf16[2,768,256]{2,1,0:T(8,128)(2,1)}, bf16[2,768,256]{2,1,0:T(8,128)(2,1)}, u32[]{:S(2)}, u32[]{:S(2)}) collective-permute-start(bf16[2,768,256]{2,1,0:T(8,128)(2,1)} %copy-done.7), channel_id=1, source_target_pairs={{0,16},{16,0},{32,48},{48,32},{64,80},{80,64},{96,112},{112,96},{1... | collective-permute-start | bytes 2359304 | tf_op jit(solution)/shard_map/ppermute | solution.py:66
  108.3 11.1 %collective-permute-start.13 = (bf16[1,768,256]{2,1,0:T(8,128)(2,1)S(1)}, bf16[1,768,256]{2,1,0:T(8,128)(2,1)S(1)}, u32[]{:S(2)}, u32[]{:S(2)}) collective-permute-start(bf16[1,768,256]{2,1,0:T(8,128)(2,1)S(1)} %slice.31), channel_id=1, source_target_pairs={{0,32},{16,48},{32,0},{48,16},{64,96},{80,112},{96,64},{112,80},{1... | collective-permute-start | bytes 1179656 | tf_op jit(solution)/shard_map/ppermute | solution.py:66
  119.5 24.3 %collective-permute-start.14 = (bf16[1,768,256]{2,1,0:T(8,128)(2,1)S(1)}, bf16[1,768,256]{2,1,0:T(8,128)(2,1)}, u32[]{:S(2)}, u32[]{:S(2)}) collective-permute-start(bf16[1,768,256]{2,1,0:T(8,128)(2,1)S(1)} %collective-permute-done.13.refs_2_), channel_id=1, source_target_pairs={{0,16},{16,0},{32,48},{48,32},{64,80},{80,64},{96,112},{112,96},{1... | collective-permute-start | bytes 1179656 | tf_op jit(solution)/shard_map/ppermute | solution.py:66
  120.8 8.4 %collective-permute-start.10 = (s32[8,128]{1,0:T(8,128)S(1)}, s32[8,128]{1,0:T(8,128)S(1)}, u32[]{:S(2)}, u32[]{:S(2)}) collective-permute-start(s32[8,128]{1,0:T(8,128)S(1)} %broadcast_in_dim.34), channel_id=1, source_target_pairs={{0,0},{1,32},{2,48},{3,16},{16,34},{17,2},{18,18},{19,50},{32,1},{... | collective-permute-start | bytes 12296 | tf_op jit(solution)/shard_map/ppermute | solution.py:43
  150.6 16.2 %collective-permute-start.16 = (bf16[192,384]{1,0:T(8,128)(2,1)}, bf16[192,384]{1,0:T(8,128)(2,1)S(1)}, u32[]{:S(2)}, u32[]{:S(2)}) collective-permute-start(bf16[192,384]{1,0:T(8,128)(2,1)} %get-tuple-element.45), channel_id=1, source_target_pairs={{0,0},{4,4},{8,8},{12,12},{32,1},{36,5},{40,9},{44,13},{48,2},{52,... | collective-permute-start | bytes 442376 | tf_op jit(solution)/shard_map/ppermute | solution.py:56
  157.3 9.6 %collective-permute-start.17 = (bf16[192,384]{1,0:T(8,128)(2,1)}, bf16[192,384]{1,0:T(8,128)(2,1)S(1)}, u32[]{:S(2)}, u32[]{:S(2)}) collective-permute-start(bf16[192,384]{1,0:T(8,128)(2,1)} %get-tuple-element.46), channel_id=1, source_target_pairs={{0,4},{4,0},{8,12},{12,8},{32,5},{36,1},{40,13},{44,9},{48,6},{52,... | collective-permute-start | bytes 442376 | tf_op jit(solution)/shard_map/ppermute | solution.py:56
  157.4 12.4 %collective-permute-start.18 = (bf16[192,384]{1,0:T(8,128)(2,1)}, bf16[192,384]{1,0:T(8,128)(2,1)S(1)}, u32[]{:S(2)}, u32[]{:S(2)}) collective-permute-start(bf16[192,384]{1,0:T(8,128)(2,1)} %get-tuple-element.47), channel_id=1, source_target_pairs={{0,8},{4,12},{8,0},{12,4},{32,9},{36,13},{40,1},{44,5},{48,10},{52... | collective-permute-start | bytes 442376 | tf_op jit(solution)/shard_map/ppermute | solution.py:56
  163.8 10.9 %collective-permute-start.19 = (bf16[192,384]{1,0:T(8,128)(2,1)}, bf16[192,384]{1,0:T(8,128)(2,1)S(1)}, u32[]{:S(2)}, u32[]{:S(2)}) collective-permute-start(bf16[192,384]{1,0:T(8,128)(2,1)} %get-tuple-element.48), channel_id=1, source_target_pairs={{0,12},{4,8},{8,4},{12,0},{32,13},{36,9},{40,5},{44,1},{48,14},{52... | collective-permute-start | bytes 442376 | tf_op jit(solution)/shard_map/ppermute | solution.py:56
  183.5 13.3 %collective-permute-start.20 = (f32[64,1280]{1,0:T(8,128)}, f32[64,1280]{1,0:T(8,128)S(1)}, u32[]{:S(2)}, u32[]{:S(2)}) collective-permute-start(f32[64,1280]{1,0:T(8,128)} %get-tuple-element.54), channel_id=1, source_target_pairs={{0,4},{4,0},{8,12},{12,8},{1,5},{5,1},{9,13},{13,9},{2,6},{6,2},{1... | collective-permute-start | bytes 983048 | tf_op jit(solution)/shard_map/ppermute | solution.py:66
  183.5 13.3 %collective-permute-start.21 = (f32[64,1280]{1,0:T(8,128)}, f32[64,1280]{1,0:T(8,128)S(1)}, u32[]{:S(2)}, u32[]{:S(2)}) collective-permute-start(f32[64,1280]{1,0:T(8,128)} %get-tuple-element.55), channel_id=1, source_target_pairs={{0,8},{4,12},{8,0},{12,4},{1,9},{5,13},{9,1},{13,5},{2,10},{6,14},... | collective-permute-start | bytes 983048 | tf_op jit(solution)/shard_map/ppermute | solution.py:66
  186.1 10.9 %collective-permute-start.22 = (f32[64,1280]{1,0:T(8,128)}, f32[64,1280]{1,0:T(8,128)S(1)}, u32[]{:S(2)}, u32[]{:S(2)}) collective-permute-start(f32[64,1280]{1,0:T(8,128)} %get-tuple-element.56), channel_id=1, source_target_pairs={{0,12},{4,8},{8,4},{12,0},{1,13},{5,9},{9,5},{13,1},{2,14},{6,10},... | collective-permute-start | bytes 983048 | tf_op jit(solution)/shard_map/ppermute | solution.py:66
  197.0 6.4 %collective-permute-start.23 = (f32[16,1280]{1,0:T(8,128)S(1)}, f32[16,1280]{1,0:T(8,128)S(1)}, u32[]{:S(2)}, u32[]{:S(2)}) collective-permute-start(f32[16,1280]{1,0:T(8,128)S(1)} %get-tuple-element.66), channel_id=1, source_target_pairs={{0,1},{1,0},{2,3},{3,2},{4,5},{5,4},{6,7},{7,6},{8,9},{9,8},{10,11... | collective-permute-start | bytes 245768 | tf_op jit(solution)/shard_map/ppermute | solution.py:66
  198.4 8.1 %collective-permute-start.24 = (f32[16,1280]{1,0:T(8,128)S(1)}, f32[16,1280]{1,0:T(8,128)S(1)}, u32[]{:S(2)}, u32[]{:S(2)}) collective-permute-start(f32[16,1280]{1,0:T(8,128)S(1)} %get-tuple-element.68), channel_id=1, source_target_pairs={{0,2},{1,3},{2,0},{3,1},{4,6},{5,7},{6,4},{7,5},{8,10},{9,11},{10,... | collective-permute-start | bytes 245768 | tf_op jit(solution)/shard_map/ppermute | solution.py:66
  198.4 9.5 %collective-permute-start.25 = (f32[16,1280]{1,0:T(8,128)S(1)}, f32[16,1280]{1,0:T(8,128)S(1)}, u32[]{:S(2)}, u32[]{:S(2)}) collective-permute-start(f32[16,1280]{1,0:T(8,128)S(1)} %get-tuple-element.67), channel_id=1, source_target_pairs={{0,3},{1,2},{2,1},{3,0},{4,7},{5,6},{6,5},{7,4},{8,11},{9,10},{10,... | collective-permute-start | bytes 245768 | tf_op jit(solution)/shard_map/ppermute | solution.py:66
  209.3 7.1 %collective-permute-start.27 = (f32[16,1152]{1,0:T(8,128)S(1)}, f32[16,1152]{1,0:T(8,128)S(1)}, u32[]{:S(2)}, u32[]{:S(2)}) collective-permute-start(f32[16,1152]{1,0:T(8,128)S(1)} %slice_multiply_fusion), channel_id=1, source_target_pairs={{0,128},{16,144},{32,160},{48,176},{64,192},{80,208},{96,224},{112... | collective-permute-start | bytes 221192 | tf_op jit(solution)/shard_map/ppermute | solution.py:66
  227.7 5.7 %collective-permute-start.32 = (bf16[16,1152]{1,0:T(8,128)(2,1)S(1)}, bf16[16,1152]{1,0:T(8,128)(2,1)S(1)}, u32[]{:S(2)}, u32[]{:S(2)}) collective-permute-start(bf16[16,1152]{1,0:T(8,128)(2,1)S(1)} %add_convert_fusion.refs_0_), channel_id=1, source_target_pairs={{0,1},{1,0},{2,3},{3,2},{4,5},{5,4},{6,7},{7,6},{8,9},{9,8},{10,11... | collective-permute-start | bytes 110600 | tf_op jit(solution)/shard_map/ppermute | solution.py:66
  229.7 6.7 %collective-permute-start.33 = (bf16[16,1152]{1,0:T(8,128)(2,1)S(1)}, bf16[16,1152]{1,0:T(8,128)(2,1)S(1)}, u32[]{:S(2)}, u32[]{:S(2)}) collective-permute-start(bf16[16,1152]{1,0:T(8,128)(2,1)S(1)} %add_convert_fusion.refs_0_), channel_id=1, source_target_pairs={{0,2},{1,3},{2,0},{3,1},{4,6},{5,7},{6,4},{7,5},{8,10},{9,11},{10,... | collective-permute-start | bytes 110600 | tf_op jit(solution)/shard_map/ppermute | solution.py:66
  240.0 6.0 %collective-permute-start.36 = (bf16[64,768]{1,0:T(8,128)(2,1)}, bf16[64,768]{1,0:T(8,128)(2,1)S(1)}, u32[]{:S(2)}, u32[]{:S(2)}) collective-permute-start(bf16[64,768]{1,0:T(8,128)(2,1)} %get-tuple-element.63.refs_0_), channel_id=1, source_target_pairs={{0,8},{4,12},{8,0},{12,4},{1,9},{5,13},{9,1},{13,5},{2,10},{6,14},... | collective-permute-start | bytes 294920 | tf_op jit(solution)/shard_map/ppermute | solution.py:66
  242.6 5.9 %collective-permute-start.37 = (bf16[64,768]{1,0:T(8,128)(2,1)}, bf16[64,768]{1,0:T(8,128)(2,1)S(1)}, u32[]{:S(2)}, u32[]{:S(2)}) collective-permute-start(bf16[64,768]{1,0:T(8,128)(2,1)} %get-tuple-element.63.refs_0_), channel_id=1, source_target_pairs={{0,12},{4,8},{8,4},{12,0},{1,13},{5,9},{9,5},{13,1},{2,14},{6,10},... | collective-permute-start | bytes 294920 | tf_op jit(solution)/shard_map/ppermute | solution.py:66
  (33 other events, 202.6 us)
Sparse Core Ops, SparseCore 0:
  9.8 61.8 all-gather.2
  107.7 66.9 all-gather.4

commit v4 on v3

--- a/solution.py
+++ b/solution.py
@@ -168,25 +168,22 @@
         ref[:, :-HEAD_SIZE] = before[...]
 
 
-def attend(query_rows, first_head, heads, blocks, bias, earlier=()):
-    rows = query_rows.shape[1]
+def attend(queries, blocks, bias, earlier=()):
+    heads, rows, _ = queries.shape
     keys = bias.shape[1]
     seg = rows // 4
     columns = heads * HEAD_SIZE + sum(array.shape[1] for array in earlier[:1])
     chunk = 1024
 
-    def spec(array, place):
-        return pl.BlockSpec((None,) + array.shape[1:], lambda i: (i + place, 0, 0))
+    def spec(array):
+        return pl.BlockSpec((None,) + array.shape[1:], lambda i: (i, 0, 0))
 
     return pl.pallas_call(
         attention_body,
         out_shape=[jax.ShapeDtypeStruct((seg, columns), jnp.bfloat16)] * 4,
         grid=(heads,),
-        in_specs=[
-            pl.BlockSpec((None, rows, HEAD_SIZE), lambda i: (i + first_head, 0, 0)),
-            pl.BlockSpec(bias.shape, lambda i: (0, 0)),
-        ]
-        + [spec(array, place) for array, place in blocks]
+        in_specs=[spec(queries), pl.BlockSpec(bias.shape, lambda i: (0, 0))]
+        + [spec(array) for array in blocks]
         + [pl.BlockSpec(array.shape, lambda i: (0, 0)) for array in earlier],
         out_specs=[pl.BlockSpec((seg, columns // heads), lambda i: (0, i))] * 4,
         scratch_shapes=[
@@ -195,7 +192,7 @@
             pltpu.VMEM((rows, HEAD_SIZE), jnp.float32),
         ],
         name="attend",
-    )(query_rows, bias, *[array for array, _ in blocks], *earlier)
+    )(queries, bias, *blocks, *earlier)
 
 
 def standard_body(ints_ref, gain_ref, down_ref, up_ref, noise_ref, *refs):
@@ -231,6 +228,13 @@
 
 
 def products_body(ints_ref, narrow_ref, masked_ref, up_ref, own_ref, log_ref, *outs):
+    log = jnp.broadcast_to(log_ref[:1], (outs[0].shape[0], log_ref.shape[1]))
+    column = lax.broadcasted_iota(jnp.int32, log.shape, 1)
+    high = log.astype(jnp.bfloat16)
+    rest = log - high.astype(jnp.float32)
+    middle = rest.astype(jnp.bfloat16)
+    low = (rest - middle.astype(jnp.float32)).astype(jnp.bfloat16)
+    terms = jnp.where(column == 0, high, jnp.where(column == 1, middle, low))
     width = masked_ref.shape[1]
     count = len(outs)
     columns = width // count
@@ -248,11 +252,11 @@
             masked_ref[:, pl.ds(start, columns)],
             first_axis,
             preferred_element_type=jnp.float32,
-        )
-        out[:, columns : columns + own_columns] = down[:, k * own_columns : (k + 1) * own_columns]
-        out[:, columns + own_columns :] = jnp.broadcast_to(
-            log_ref[:1], (out.shape[0], log_ref.shape[1])
-        )
+        ).astype(jnp.bfloat16)
+        out[:, columns : columns + own_columns] = down[
+            :, k * own_columns : (k + 1) * own_columns
+        ].astype(jnp.bfloat16)
+        out[:, columns + own_columns :] = terms
 
 
 def rows_body(ints_ref, *refs):
@@ -346,21 +350,28 @@
     maps = jnp.concatenate([maps] + [exchange(maps, "uly", k) for k in (1, 2, 3)], 1)
     output_columns, down_full = maps[: output_weight.shape[0]], maps[output_weight.shape[0] :]
 
-    key_values, query_rows = pl.pallas_call(
-        project_body,
-        out_shape=(
-            jax.ShapeDtypeStruct((heads_here, group_rows, pair), jnp.bfloat16),
-            jax.ShapeDtypeStruct((heads_here, group_rows, HEAD_SIZE), jnp.bfloat16),
-        ),
-        grid=(heads_here,),
-        in_specs=[smem] + [vmem] * 7 + [pl.BlockSpec((width, local_columns), lambda h: (0, h))],
-        out_specs=(
-            pl.BlockSpec((None, group_rows, pair), lambda h: (h, 0, 0)),
-            pl.BlockSpec((None, group_rows, HEAD_SIZE), lambda h: (h, 0, 0)),
-        ),
-        scratch_shapes=[pltpu.VMEM((group_rows, width), jnp.bfloat16)],
-        name="project",
-    )(uly_int, normed_a, normed_b, left_a, right_a, up, right_b, far_b, weight_rows)
+    def project(first_head, heads):
+        return pl.pallas_call(
+            project_body,
+            out_shape=(
+                jax.ShapeDtypeStruct((heads, group_rows, pair), jnp.bfloat16),
+                jax.ShapeDtypeStruct((heads, group_rows, HEAD_SIZE), jnp.bfloat16),
+            ),
+            grid=(heads,),
+            in_specs=[smem]
+            + [vmem] * 7
+            + [pl.BlockSpec((width, local_columns), lambda h: (0, h + first_head))],
+            out_specs=(
+                pl.BlockSpec((None, group_rows, pair), lambda h: (h, 0, 0)),
+                pl.BlockSpec((None, group_rows, HEAD_SIZE), lambda h: (h, 0, 0)),
+            ),
+            scratch_shapes=[pltpu.VMEM((group_rows, width), jnp.bfloat16)],
+            name="project",
+        )(uly_int, normed_a, normed_b, left_a, right_a, up, right_b, far_b, weight_rows)
+
+    lead = heads_here - 1
+    lead_pairs, lead_queries = project(0, lead)
+    last_pairs, last_queries = project(lead, 1)
 
     key_index = jnp.arange(blk_count * group_rows, dtype=jnp.int32)
     slot = video_slot ^ (key_index // group_rows)
@@ -374,25 +385,16 @@
     ) * rows + key_index % rows
     bias = jnp.where(key_pos < work_limit, 0.0, -1e30).astype(jnp.float32)[None]
 
-    lead = heads_here - 1
-    core = exchange(key_values, "fsdp", 1)
-    chip_lead = exchange(key_values[:lead], "fsdp", 2)
-    chip_last = exchange(after(key_values[lead:], chip_lead), "fsdp", 2)
+    chip_lead = exchange(lead_pairs, "fsdp", 2)
+    core_lead = exchange(lead_pairs, "fsdp", 1)
+    chip_last = exchange(after(last_pairs, chip_lead), "fsdp", 2)
+    core_last = exchange(last_pairs, "fsdp", 1)
     far_lead = exchange(chip_lead, "fsdp", 1)
     far_last = exchange(chip_last, "fsdp", 1)
     weight_full = lax.all_gather(after(output_columns, chip_lead), "fsdp", axis=0, tiled=True)
 
-    segs = attend(
-        query_rows, 0, lead, ((key_values, 0), (core, 0), (chip_lead, 0), (far_lead, 0)), bias
-    )
-    segs = attend(
-        query_rows,
-        lead,
-        1,
-        ((key_values, lead), (core, lead), (chip_last, 0), (far_last, 0)),
-        bias,
-        segs,
-    )
+    segs = attend(lead_queries, (lead_pairs, core_lead, chip_lead, far_lead), bias)
+    segs = attend(last_queries, (last_pairs, core_last, chip_last, far_last), bias, segs)
     pieces = [return_tokens(segs[k], k) for k in range(uly_count)]
 
     step_float = timestep_index[0].astype(jnp.float32)
@@ -420,13 +422,20 @@
     share_columns = up_columns + local_columns
     shares = pl.pallas_call(
         products_body,
-        out_shape=[jax.ShapeDtypeStruct((rank, share_columns + 128), jnp.float32)] * uly_count,
+        out_shape=[jax.ShapeDtypeStruct((rank, share_columns + 128), jnp.bfloat16)] * uly_count,
         in_specs=[smem] + [vmem] * 5,
         out_specs=[vmem] * uly_count,
         name="products",
     )(uly_int, narrow_projection, masked, adapter_up_map, own_heads, log_tile)
 
-    parts = [exchange(shares[k], "uly", k) for k in (1, 2, 3)]
+    parts = [shares[0]] + [exchange(shares[k], "uly", k) for k in (1, 2, 3)]
+    summed = four_sum([part.astype(jnp.float32) for part in parts])
+    part = rank // blk_count
+
+    def rows_of(k):
+        return lax.dynamic_slice_in_dim(summed, (blk_id ^ k) * part, part, 0)
+
+    parts = [exchange(rows_of(k), "blk", k) for k in (1, 2, 3)]
     tile = 512
     scalars = jnp.stack(
         [
@@ -452,14 +461,9 @@
         name="move",
     )(scalars, own_heads, weight_full, latents[0], sampler_noise[0])
     next_latents, *parts = lax.optimization_barrier((next_latents, *parts))
-    summed = four_sum([shares[0]] + parts)
-    part = rank // blk_count
-
-    def rows_of(k):
-        return lax.dynamic_slice_in_dim(summed, (blk_id ^ k) * part, part, 0)
-
-    summed = four_sum([rows_of(0)] + [exchange(rows_of(k), "blk", k) for k in (1, 2, 3)])
-    log_ratio = summed[0, share_columns] / (2.0 * valid_len * width)
+    summed = four_sum([rows_of(0)] + parts)
+    log_sum = summed[0, share_columns] + summed[0, share_columns + 1] + summed[0, share_columns + 2]
+    log_ratio = log_sum / (2.0 * valid_len * width)
     coef = (
         loss_scale
         * advantage[0]

time: 260 us -> 266 us (1.023)
  Pallas kernels: 53.2 us -> 57.4 us
    pallas_call x1 -> x2, Pallas kernels: 12.6 us -> 16.9 us  [project(): pl.pallas_call(project_body, out_shape=(jax.ShapeDtypeStruct((heads, grou...]
    ppermute x26 -> x27, waiting for transfers between devices: 39.5 us -> 41.7 us  [exchange(): return lax.ppermute(x, axis, [(i, i ^ mask) for i in range(n)])]
    ppermute x26 -> x27, starting transfers between devices: 39 us -> 39.5 us  [exchange(): return lax.ppermute(x, axis, [(i, i ^ mask) for i in range(n)])]
  transfers between devices with their start and end apart: 40 -> 41, of which waited for: 24 -> 25; matrix products, arithmetic and copies ran while one was open for 3% -> 3% of each run, Pallas kernels for 14% -> 16%
where the time goes in v4:
time: 266 us; the launch traced here: 265 us
  waiting for transfers between devices  90.2 us (34%)
  starting transfers between devices  85.8 us (32%)
  Pallas kernels  57.4 us (22%)
  between operations  19.7 us (7%)
  other arithmetic  5.89 us (2%)
  local copies, waits for them, and re-layouts  5.71 us (2%)
    ppermute x27, waiting for transfers between devices, exchange(): return lax.ppermute(x, axis, [(i, i ^ mask) for i in range(n)])  41.7 us
    ppermute x27, starting transfers between devices, exchange(): return lax.ppermute(x, axis, [(i, i ^ mask) for i in range(n)])  39.5 us
    ppermute x3, waiting for transfers between devices, gather_tokens(): return lax.ppermute(x, ('fsdp', 'blk'), pairs)  27.6 us
    ppermute x3, starting transfers between devices, gather_tokens(): return lax.ppermute(x, ('fsdp', 'blk'), pairs)  25.1 us
    pallas_call x2, Pallas kernels, attend(): pl.pallas_call(attention_body, out_shape=[jax.ShapeDtypeStruct((seg, colu...  18.3 us
    pallas_call x2, Pallas kernels, project(): pl.pallas_call(project_body, out_shape=(jax.ShapeDtypeStruct((heads, grou...  16.9 us
    ppermute x5, waiting for transfers between devices, shift(): return lax.ppermute(x, axis, [(i, (i + step) % n) for i in range(n)])  14.6 us
    ppermute x4, starting transfers between devices, return_tokens(): return lax.ppermute(x, ('fsdp', 'uly', 'blk'), pairs)  13.6 us
  transfers between devices with their start and end apart: 41, of which 25 were waited for; matrix products, arithmetic and copies ran while one was open for 3% of the time, Pallas kernels for 16%

profile of v4, /device:TPU:1, one launch (start us, length us, event | category | flops | bytes accessed | tf_op | source)
XLA Modules:
  0.0 264.7 jit_solution(17241956015474074405)
XLA Ops:
  9.3 9.8 %collective-permute-start = (bf16[96,3072]{1,0:T(8,128)(2,1)S(1)}, bf16[96,3072]{1,0:T(8,128)(2,1)S(1)}, u32[]{:S(2)}, u32[]{:S(2)}) collective-permute-start(bf16[96,3072]{1,0:T(8,128)(2,1)S(1)} %get-tuple-element.68), channel_id=1, source_target_pairs={{0,0},{1,32},{2,48},{3,16},{16,34},{17,2},{18,18},{19,50},{32,1},{... | collective-permute-start | bytes 1769480 | tf_op jit(solution)/shard_map/ppermute | solution.py:43
  19.1 13.2 %collective-permute-done = bf16[96,3072]{1,0:T(8,128)(2,1)S(1)} collective-permute-done((bf16[96,3072]{1,0:T(8,128)(2,1)S(1)}, bf16[96,3072]{1,0:T(8,128)(2,1)S(1)}, u32[]{:S(2)}, u32[]{:S(2)}) %collective-permute-start) | collective-permute-done | bytes 589856 | tf_op jit(solution)/shard_map/ppermute | solution.py:43
  32.3 7.5 %collective-permute-start.1 = (bf16[96,3072]{1,0:T(8,128)(2,1)S(1)}, bf16[96,3072]{1,0:T(8,128)(2,1)S(1)}, u32[]{:S(2)}, u32[]{:S(2)}) collective-permute-start(bf16[96,3072]{1,0:T(8,128)(2,1)S(1)} %get-tuple-element.36), channel_id=1, source_target_pairs={{0,0},{1,32},{2,48},{3,16},{16,34},{17,2},{18,18},{19,50},{32,1},{... | collective-permute-start | bytes 1769480 | tf_op jit(solution)/shard_map/ppermute | solution.py:43
  42.9 13.1 %collective-permute-done.1 = bf16[96,3072]{1,0:T(8,128)(2,1)S(1)} collective-permute-done((bf16[96,3072]{1,0:T(8,128)(2,1)S(1)}, bf16[96,3072]{1,0:T(8,128)(2,1)S(1)}, u32[]{:S(2)}, u32[]{:S(2)}) %collective-permute-start.1) | collective-permute-done | bytes 589856 | tf_op jit(solution)/shard_map/ppermute | solution.py:43
  60.3 7.8 %collective-permute-done.5.right_b_ref = bf16[96,3072]{1,0:T(8,128)(2,1)S(1)} collective-permute-done((bf16[96,3072]{1,0:T(8,128)(2,1)S(1)}, bf16[96,3072]{1,0:T(8,128)(2,1)S(1)}, u32[]{:S(2)}, u32[]{:S(2)}) %collective-permute-start.5) | collective-permute-done | bytes 589856 | tf_op jit(solution)/shard_map/ppermute | solution.py:61
  70.3 3.8 %collective-permute-done.4.up_ref = bf16[192,3072]{1,0:T(8,128)(2,1)S(1)} collective-permute-done((bf16[192,3072]{1,0:T(8,128)(2,1)}, bf16[192,3072]{1,0:T(8,128)(2,1)S(1)}, u32[]{:S(2)}, u32[]{:S(2)}) %collective-permute-start.4) | collective-permute-done | bytes 1179680 | tf_op jit(solution)/shard_map/ppermute | solution.py:61
  74.1 3.0 %collective-permute-done.6.far_b_ref = bf16[96,3072]{1,0:T(8,128)(2,1)} collective-permute-done((bf16[96,3072]{1,0:T(8,128)(2,1)S(1)}, bf16[96,3072]{1,0:T(8,128)(2,1)}, u32[]{:S(2)}, u32[]{:S(2)}) %collective-permute-start.6) | collective-permute-done | bytes 589856 | tf_op jit(solution)/shard_map/ppermute | solution.py:61
  77.1 9.8 %project.3 = (bf16[2,768,256]{2,1,0:T(8,128)(2,1)}, bf16[2,768,128]{2,1,0:T(8,128)(2,1)}) custom-call(s32[1]{0:T(128)} %bitcast.8.ints_ref, bf16[96,3072]{1,0:T(8,128)(2,1)} %copy-done.1, bf16[96,3072]{1,0:T(8,128)(2,1)} %copy-done, bf16[96,3072]{1,0:T(8,128)(2,1)} %copy-done.2, bf16[96,3072]{1,0:T(8,128)(2,1)} %copy-done.5, bf16[192,3072]{1,0:T(8,128)(2,1)} %copy-done.3, ...), custom_call_target="tpu_custom_call" | custom-call | tf_op jit(solution)/shard_map/project/pallas_call | solution.py:354
  86.9 3.2 %collective-permute-start.12 = (bf16[2,768,256]{2,1,0:T(8,128)(2,1)}, bf16[2,768,256]{2,1,0:T(8,128)(2,1)S(1)}, u32[]{:S(2)}, u32[]{:S(2)}) collective-permute-start(bf16[2,768,256]{2,1,0:T(8,128)(2,1)} %get-tuple-element.42.refs_0_), channel_id=1, source_target_pairs={{0,32},{16,48},{32,0},{48,16},{64,96},{80,112},{96,64},{112,80},{1... | collective-permute-start | bytes 2359304 | tf_op jit(solution)/shard_map/ppermute | solution.py:66
  90.3 4.4 %collective-permute-start.8 = (bf16[256,384]{1,0:T(8,128)(2,1)S(1)}, bf16[256,384]{1,0:T(8,128)(2,1)S(1)}, u32[]{:S(2)}, u32[]{:S(2)}) collective-permute-start(bf16[256,384]{1,0:T(8,128)(2,1)S(1)} %pad_maximum_fusion.1), channel_id=1, source_target_pairs={{0,8},{4,12},{8,0},{12,4},{1,9},{5,13},{9,1},{13,5},{2,10},{6,14},... | collective-permute-start | bytes 589832 | tf_op jit(solution)/shard_map/ppermute | solution.py:66
  95.1 4.8 %collective-permute-done.8 = bf16[256,384]{1,0:T(8,128)(2,1)S(1)} collective-permute-done((bf16[256,384]{1,0:T(8,128)(2,1)S(1)}, bf16[256,384]{1,0:T(8,128)(2,1)S(1)}, u32[]{:S(2)}, u32[]{:S(2)}) %collective-permute-start.8) | collective-permute-done | bytes 196640 | tf_op jit(solution)/shard_map/ppermute | solution.py:66
  103.1 7.1 %project.2 = (bf16[1,768,256]{2,1,0:T(8,128)(2,1)}, bf16[1,768,128]{2,1,0:T(8,128)(2,1)}) custom-call(s32[1]{0:T(128)} %bitcast.8.ints_ref, bf16[96,3072]{1,0:T(8,128)(2,1)} %copy-done.1, bf16[96,3072]{1,0:T(8,128)(2,1)} %copy-done, bf16[96,3072]{1,0:T(8,128)(2,1)} %copy-done.2, bf16[96,3072]{1,0:T(8,128)(2,1)} %copy-done.5, bf16[192,3072]{1,0:T(8,128)(2,1)} %copy-done.3, ...), custom_call_target="tpu_custom_call" | custom-call | tf_op jit(solution)/shard_map/project/pallas_call | solution.py:354
  112.8 13.6 %collective-permute-done.13.refs_2_ = bf16[1,768,256]{2,1,0:T(8,128)(2,1)S(1)} collective-permute-done((bf16[1,768,256]{2,1,0:T(8,128)(2,1)}, bf16[1,768,256]{2,1,0:T(8,128)(2,1)S(1)}, u32[]{:S(2)}, u32[]{:S(2)}) %collective-permute-start.13) | collective-permute-done | bytes 393248 | tf_op jit(solution)/shard_map/ppermute | solution.py:66
  129.3 7.8 %collective-permute-start.10 = (s32[8,128]{1,0:T(8,128)S(1)}, s32[8,128]{1,0:T(8,128)S(1)}, u32[]{:S(2)}, u32[]{:S(2)}) collective-permute-start(s32[8,128]{1,0:T(8,128)S(1)} %broadcast_in_dim.34), channel_id=1, source_target_pairs={{0,0},{1,32},{2,48},{3,16},{16,34},{17,2},{18,18},{19,50},{32,1},{... | collective-permute-start | bytes 12296 | tf_op jit(solution)/shard_map/ppermute | solution.py:43
  141.5 11.5 %attend.2 = (bf16[192,256]{1,0:T(8,128)(2,1)}, bf16[192,256]{1,0:T(8,128)(2,1)}, bf16[192,256]{1,0:T(8,128)(2,1)}, bf16[192,256]{1,0:T(8,128)(2,1)}) custom-call(bf16[2,768,128]{2,1,0:T(8,128)(2,1)} %get-tuple-element.44.q_ref, f32[1,3072]{1,0:T(1,128)} %compare_select_fusion.bias_ref, bf16[2,768,256]{2,1,0:T(8,128)(2,1)} %get-tuple-element.42.refs_0_, ...), custom_call_target="tpu_custom_call" | custom-call | tf_op jit(solution)/shard_map/attend/pallas_call | solution.py:181
  152.9 6.9 %attend.3 = (bf16[192,384]{1,0:T(8,128)(2,1)}, bf16[192,384]{1,0:T(8,128)(2,1)}, bf16[192,384]{1,0:T(8,128)(2,1)}, bf16[192,384]{1,0:T(8,128)(2,1)}) custom-call(bf16[1,768,128]{2,1,0:T(8,128)(2,1)} %get-tuple-element.40.q_ref, f32[1,3072]{1,0:T(1,128)} %compare_select_fusion.bias_ref, bf16[1,768,256]{2,1,0:T(8,128)(2,1)} %get-tuple-element.43.refs_0_, ...), custom_call_target="tpu_custom_call" | custom-call | tf_op jit(solution)/shard_map/attend/pallas_call | solution.py:181
  159.8 6.5 %collective-permute-start.17 = (bf16[192,384]{1,0:T(8,128)(2,1)}, bf16[192,384]{1,0:T(8,128)(2,1)S(1)}, u32[]{:S(2)}, u32[]{:S(2)}) collective-permute-start(bf16[192,384]{1,0:T(8,128)(2,1)} %get-tuple-element.49), channel_id=1, source_target_pairs={{0,0},{4,4},{8,8},{12,12},{32,1},{36,5},{40,9},{44,13},{48,2},{52,... | collective-permute-start | bytes 442376 | tf_op jit(solution)/shard_map/ppermute | solution.py:56
  166.5 5.2 %collective-permute-start.19 = (bf16[192,384]{1,0:T(8,128)(2,1)}, bf16[192,384]{1,0:T(8,128)(2,1)S(1)}, u32[]{:S(2)}, u32[]{:S(2)}) collective-permute-start(bf16[192,384]{1,0:T(8,128)(2,1)} %get-tuple-element.51), channel_id=1, source_target_pairs={{0,8},{4,12},{8,0},{12,4},{32,9},{36,13},{40,1},{44,5},{48,10},{52... | collective-permute-start | bytes 442376 | tf_op jit(solution)/shard_map/ppermute | solution.py:56
  175.5 2.9 %collective-permute-done.19.refs_2_ = bf16[192,384]{1,0:T(8,128)(2,1)S(1)} collective-permute-done((bf16[192,384]{1,0:T(8,128)(2,1)}, bf16[192,384]{1,0:T(8,128)(2,1)S(1)}, u32[]{:S(2)}, u32[]{:S(2)}) %collective-permute-start.19) | collective-permute-done | bytes 147488 | tf_op jit(solution)/shard_map/ppermute | solution.py:56
  178.5 3.3 %collective-permute-done.20.refs_3_ = bf16[192,384]{1,0:T(8,128)(2,1)S(1)} collective-permute-done((bf16[192,384]{1,0:T(8,128)(2,1)}, bf16[192,384]{1,0:T(8,128)(2,1)S(1)}, u32[]{:S(2)}, u32[]{:S(2)}) %collective-permute-start.20) | collective-permute-done | bytes 147488 | tf_op jit(solution)/shard_map/ppermute | solution.py:56
  182.5 4.5 %standard.1 = (bf16[192,1536]{1,0:T(8,128)(2,1)}, bf16[192,64]{1,0:T(8,128)(2,1)}, bf16[192,3072]{1,0:T(8,128)(2,1)}, f32[8,128]{1,0:T(8,128)}) custom-call(s32[2]{0:T(128)} %pad_add_fusion.ints_ref, f32[1]{0:T(128)} %bitcast.4.gain_ref, bf16[64,1536]{1,0:T(8,128)(2,1)} %slice.36.down_ref, bf16[64,3072]{1,0:T(8,128)(2,1)} %up_ref.3, ...), custom_call_target="tpu_custom_call" | custom-call | tf_op jit(solution)/shard_map/standard/pallas_call | solution.py:408
  186.9 3.6 %products.1 = (bf16[64,1280]{1,0:T(8,128)(2,1)}, bf16[64,1280]{1,0:T(8,128)(2,1)}, bf16[64,1280]{1,0:T(8,128)(2,1)}, bf16[64,1280]{1,0:T(8,128)(2,1)}) custom-call(s32[1]{0:T(128)} %bitcast.8.ints_ref, bf16[192,64]{1,0:T(8,128)(2,1)} %get-tuple-element.55.narrow_ref, bf16[192,3072]{1,0:T(8,128)(2,1)} %get-tuple-element.56.masked_ref, ...), custom_call_target="tpu_custom_call" | custom-call | tf_op jit(solution)/shard_map/products/pallas_call | solution.py:423
  199.5 2.7 %collective-permute-start.24 = (f32[16,1280]{1,0:T(8,128)S(1)}, f32[16,1280]{1,0:T(8,128)S(1)}, u32[]{:S(2)}, u32[]{:S(2)}) collective-permute-start(f32[16,1280]{1,0:T(8,128)S(1)} %get-tuple-element.72), channel_id=1, source_target_pairs={{0,1},{1,0},{2,3},{3,2},{4,5},{5,4},{6,7},{7,6},{8,9},{9,8},{10,11... | collective-permute-start | bytes 245768 | tf_op jit(solution)/shard_map/ppermute | solution.py:66
  202.1 3.4 %collective-permute-start.26 = (f32[16,1280]{1,0:T(8,128)S(1)}, f32[16,1280]{1,0:T(8,128)S(1)}, u32[]{:S(2)}, u32[]{:S(2)}) collective-permute-start(f32[16,1280]{1,0:T(8,128)S(1)} %get-tuple-element.70), channel_id=1, source_target_pairs={{0,3},{1,2},{2,1},{3,0},{4,7},{5,6},{6,5},{7,4},{8,11},{9,10},{10,... | collective-permute-start | bytes 245768 | tf_op jit(solution)/shard_map/ppermute | solution.py:66
  206.1 8.7 %move.1 = bf16[192,3072]{1,0:T(8,128)(2,1)} custom-call(f32[4]{0:T(128)} %pad_maximum_fusion.2.scalars_ref, bf16[192,1536]{1,0:T(8,128)(2,1)} %get-tuple-element.53.own_ref, bf16[3072,1536]{1,0:T(8,128)(2,1)} %all-gather.5.cloned.1.call-done.w_ref, bf16[192,3072]{1,0:T(8,128)(2,1)} %bitcast.23, bf16[192,3072]{1,0:T(8,128)(2,1)} %bitcast.22), custom_call_target="tpu_custom_call" | custom-call | tf_op jit(solution)/shard_map/move/pallas_call | solution.py:449
  217.7 3.2 %collective-permute-start.29 = (f32[16,1152]{1,0:T(8,128)S(1)}, f32[16,1152]{1,0:T(8,128)S(1)}, u32[]{:S(2)}, u32[]{:S(2)}) collective-permute-start(f32[16,1152]{1,0:T(8,128)S(1)} %slice_multiply_fusion), channel_id=1, source_target_pairs={{0,192},{16,208},{32,224},{48,240},{64,128},{80,144},{96,160},{112... | collective-permute-start | bytes 221192 | tf_op jit(solution)/shard_map/ppermute | solution.py:66
  224.4 3.4 %collective-permute-start.31 = (f32[16,1152]{1,0:T(8,128)S(1)}, f32[16,1152]{1,0:T(8,128)S(1)}, u32[]{:S(2)}, u32[]{:S(2)}) collective-permute-start(f32[16,1152]{1,0:T(8,128)S(1)} %add_add_fusion.2), channel_id=1, source_target_pairs={{0,32},{16,48},{32,0},{48,16},{64,96},{80,112},{96,64},{112,80},{1... | collective-permute-start | bytes 221192 | tf_op jit(solution)/shard_map/ppermute | solution.py:66
  229.6 3.1 %collective-permute-done.32 = f32[16,1152]{1,0:T(8,128)S(1)} collective-permute-done((f32[16,1152]{1,0:T(8,128)S(1)}, f32[16,1152]{1,0:T(8,128)S(1)}, u32[]{:S(2)}, u32[]{:S(2)}) %collective-permute-start.32) | collective-permute-done | bytes 73760 | tf_op jit(solution)/shard_map/ppermute | solution.py:66
  234.0 4.0 %collective-permute-start.34 = (bf16[16,1152]{1,0:T(8,128)(2,1)S(1)}, bf16[16,1152]{1,0:T(8,128)(2,1)S(1)}, u32[]{:S(2)}, u32[]{:S(2)}) collective-permute-start(bf16[16,1152]{1,0:T(8,128)(2,1)S(1)} %add_convert_fusion.refs_0_), channel_id=1, source_target_pairs={{0,2},{1,3},{2,0},{3,1},{4,6},{5,7},{6,4},{7,5},{8,10},{9,11},{10,... | collective-permute-start | bytes 110600 | tf_op jit(solution)/shard_map/ppermute | solution.py:66
  245.0 3.2 %collective-permute-start.37 = (bf16[64,768]{1,0:T(8,128)(2,1)}, bf16[64,768]{1,0:T(8,128)(2,1)S(1)}, u32[]{:S(2)}, u32[]{:S(2)}) collective-permute-start(bf16[64,768]{1,0:T(8,128)(2,1)} %get-tuple-element.67.refs_0_), channel_id=1, source_target_pairs={{0,8},{4,12},{8,0},{12,4},{1,9},{5,13},{9,1},{13,5},{2,10},{6,14},... | collective-permute-start | bytes 294920 | tf_op jit(solution)/shard_map/ppermute | solution.py:66
  248.9 2.6 collective-permute-done.37.refs_2_
  251.5 2.7 %collective-permute-done.38.refs_3_ = bf16[64,768]{1,0:T(8,128)(2,1)S(1)} collective-permute-done((bf16[64,768]{1,0:T(8,128)(2,1)}, bf16[64,768]{1,0:T(8,128)(2,1)S(1)}, u32[]{:S(2)}, u32[]{:S(2)}) %collective-permute-start.38) | collective-permute-done | bytes 98336 | tf_op jit(solution)/shard_map/ppermute | solution.py:66
  (137 shorter events, 54.8 us)
Async XLA Ops:
  7.2 69.9 %all-gather.3.cloned.1.call-start = ((), (), s32[]{:S(2)}) async-start(), calls=%async_computation | async-start | bytes 7520256 | tf_op jit(solution)/shard_map/all_gather | solution.py:340
  9.2 197.0 %all-gather.5.cloned.1.call-start = ((), (), s32[]{:S(2)}) async-start(), calls=%async_computation.1 | async-start | bytes 10027008 | tf_op jit(solution)/shard_map/all_gather | solution.py:394
  9.3 22.9 %collective-permute-start = (bf16[96,3072]{1,0:T(8,128)(2,1)S(1)}, bf16[96,3072]{1,0:T(8,128)(2,1)S(1)}, u32[]{:S(2)}, u32[]{:S(2)}) collective-permute-start(bf16[96,3072]{1,0:T(8,128)(2,1)S(1)} %get-tuple-element.68), channel_id=1, source_target_pairs={{0,0},{1,32},{2,48},{3,16},{16,34},{17,2},{18,18},{19,50},{32,1},{... | collective-permute-start | bytes 1769480 | tf_op jit(solution)/shard_map/ppermute | solution.py:43
  32.3 23.7 %collective-permute-start.1 = (bf16[96,3072]{1,0:T(8,128)(2,1)S(1)}, bf16[96,3072]{1,0:T(8,128)(2,1)S(1)}, u32[]{:S(2)}, u32[]{:S(2)}) collective-permute-start(bf16[96,3072]{1,0:T(8,128)(2,1)S(1)} %get-tuple-element.36), channel_id=1, source_target_pairs={{0,0},{1,32},{2,48},{3,16},{16,34},{17,2},{18,18},{19,50},{32,1},{... | collective-permute-start | bytes 1769480 | tf_op jit(solution)/shard_map/ppermute | solution.py:43
  40.1 16.3 %collective-permute-start.2 = (bf16[96,3072]{1,0:T(8,128)(2,1)S(1)}, bf16[96,3072]{1,0:T(8,128)(2,1)S(1)}, u32[]{:S(2)}, u32[]{:S(2)}) collective-permute-start(bf16[96,3072]{1,0:T(8,128)(2,1)S(1)} %fusion.3.a_ref), channel_id=1, source_target_pairs={{0,4},{4,8},{8,12},{12,0},{1,5},{5,9},{9,13},{13,1},{2,6},{6,10},{... | collective-permute-start | bytes 1769480 | tf_op jit(solution)/shard_map/ppermute | solution.py:61
  41.4 15.0 %collective-permute-start.3 = (bf16[96,3072]{1,0:T(8,128)(2,1)S(1)}, bf16[96,3072]{1,0:T(8,128)(2,1)S(1)}, u32[]{:S(2)}, u32[]{:S(2)}) collective-permute-start(bf16[96,3072]{1,0:T(8,128)(2,1)S(1)} %fusion.3.a_ref), channel_id=1, source_target_pairs={{0,12},{4,0},{8,4},{12,8},{1,13},{5,1},{9,5},{13,9},{2,14},{6,2},{... | collective-permute-start | bytes 1769480 | tf_op jit(solution)/shard_map/ppermute | solution.py:61
  57.7 16.5 %collective-permute-start.4 = (bf16[192,3072]{1,0:T(8,128)(2,1)}, bf16[192,3072]{1,0:T(8,128)(2,1)S(1)}, u32[]{:S(2)}, u32[]{:S(2)}) collective-permute-start(bf16[192,3072]{1,0:T(8,128)(2,1)} %pad_maximum_fusion), channel_id=1, source_target_pairs={{0,4},{4,8},{8,12},{12,0},{1,5},{5,9},{9,13},{13,1},{2,6},{6,10},{... | collective-permute-start | bytes 3538952 | tf_op jit(solution)/shard_map/ppermute | solution.py:61
  59.0 9.1 %collective-permute-start.5 = (bf16[96,3072]{1,0:T(8,128)(2,1)S(1)}, bf16[96,3072]{1,0:T(8,128)(2,1)S(1)}, u32[]{:S(2)}, u32[]{:S(2)}) collective-permute-start(bf16[96,3072]{1,0:T(8,128)(2,1)S(1)} %fusion.1.b_ref), channel_id=1, source_target_pairs={{0,12},{4,0},{8,4},{12,8},{1,13},{5,1},{9,5},{13,9},{2,14},{6,2},{... | collective-permute-start | bytes 1769480 | tf_op jit(solution)/shard_map/ppermute | solution.py:61
  68.1 9.0 %collective-permute-start.6 = (bf16[96,3072]{1,0:T(8,128)(2,1)S(1)}, bf16[96,3072]{1,0:T(8,128)(2,1)}, u32[]{:S(2)}, u32[]{:S(2)}) collective-permute-start(bf16[96,3072]{1,0:T(8,128)(2,1)S(1)} %collective-permute-done.5.right_b_ref), channel_id=1, source_target_pairs={{0,12},{4,0},{8,4},{12,8},{1,13},{5,1},{9,5},{13,9},{2,14},{6,2},{... | collective-permute-start | bytes 1769480 | tf_op jit(solution)/shard_map/ppermute | solution.py:61
  86.9 16.1 %collective-permute-start.12 = (bf16[2,768,256]{2,1,0:T(8,128)(2,1)}, bf16[2,768,256]{2,1,0:T(8,128)(2,1)S(1)}, u32[]{:S(2)}, u32[]{:S(2)}) collective-permute-start(bf16[2,768,256]{2,1,0:T(8,128)(2,1)} %get-tuple-element.42.refs_0_), channel_id=1, source_target_pairs={{0,32},{16,48},{32,0},{48,16},{64,96},{80,112},{96,64},{112,80},{1... | collective-permute-start | bytes 2359304 | tf_op jit(solution)/shard_map/ppermute | solution.py:66
  90.3 9.6 %collective-permute-start.8 = (bf16[256,384]{1,0:T(8,128)(2,1)S(1)}, bf16[256,384]{1,0:T(8,128)(2,1)S(1)}, u32[]{:S(2)}, u32[]{:S(2)}) collective-permute-start(bf16[256,384]{1,0:T(8,128)(2,1)S(1)} %pad_maximum_fusion.1), channel_id=1, source_target_pairs={{0,8},{4,12},{8,0},{12,4},{1,9},{5,13},{9,1},{13,5},{2,10},{6,14},... | collective-permute-start | bytes 589832 | tf_op jit(solution)/shard_map/ppermute | solution.py:66
  94.7 7.3 %collective-permute-start.9 = (bf16[256,384]{1,0:T(8,128)(2,1)S(1)}, bf16[256,384]{1,0:T(8,128)(2,1)S(1)}, u32[]{:S(2)}, u32[]{:S(2)}) collective-permute-start(bf16[256,384]{1,0:T(8,128)(2,1)S(1)} %pad_maximum_fusion.1), channel_id=1, source_target_pairs={{0,12},{4,8},{8,4},{12,0},{1,13},{5,9},{9,5},{13,1},{2,14},{6,10},... | collective-permute-start | bytes 589832 | tf_op jit(solution)/shard_map/ppermute | solution.py:66
  103.0 37.5 %collective-permute-start.15 = (bf16[2,768,256]{2,1,0:T(8,128)(2,1)S(1)}, bf16[2,768,256]{2,1,0:T(8,128)(2,1)S(1)}, u32[]{:S(2)}, u32[]{:S(2)}) collective-permute-start(bf16[2,768,256]{2,1,0:T(8,128)(2,1)S(1)} %copy-done.7), channel_id=1, source_target_pairs={{0,16},{16,0},{32,48},{48,32},{64,80},{80,64},{96,112},{112,96},{1... | collective-permute-start | bytes 2359304 | tf_op jit(solution)/shard_map/ppermute | solution.py:66
  110.3 30.3 %collective-permute-start.16 = (bf16[2,768,256]{2,1,0:T(8,128)(2,1)S(1)}, bf16[2,768,256]{2,1,0:T(8,128)(2,1)}, u32[]{:S(2)}, u32[]{:S(2)}) collective-permute-start(bf16[2,768,256]{2,1,0:T(8,128)(2,1)S(1)} %collective-permute-done.12.refs_2_), channel_id=1, source_target_pairs={{0,16},{16,0},{32,48},{48,32},{64,80},{80,64},{96,112},{112,96},{1... | collective-permute-start | bytes 2359304 | tf_op jit(solution)/shard_map/ppermute | solution.py:66
  110.7 15.8 %collective-permute-start.13 = (bf16[1,768,256]{2,1,0:T(8,128)(2,1)}, bf16[1,768,256]{2,1,0:T(8,128)(2,1)S(1)}, u32[]{:S(2)}, u32[]{:S(2)}) collective-permute-start(bf16[1,768,256]{2,1,0:T(8,128)(2,1)} %get-tuple-element.43.refs_0_), channel_id=1, source_target_pairs={{0,32},{16,48},{32,0},{48,16},{64,96},{80,112},{96,64},{112,80},{1... | collective-permute-start | bytes 1179656 | tf_op jit(solution)/shard_map/ppermute | solution.py:66
  112.4 40.5 %collective-permute-start.11 = (bf16[1,768,256]{2,1,0:T(8,128)(2,1)}, bf16[1,768,256]{2,1,0:T(8,128)(2,1)}, u32[]{:S(2)}, u32[]{:S(2)}) collective-permute-start(bf16[1,768,256]{2,1,0:T(8,128)(2,1)} %get-tuple-element.43.refs_0_), channel_id=1, source_target_pairs={{0,16},{16,0},{32,48},{48,32},{64,80},{80,64},{96,112},{112,96},{1... | collective-permute-start | bytes 1179656 | tf_op jit(solution)/shard_map/ppermute | solution.py:66
  126.5 26.5 %collective-permute-start.14 = (bf16[1,768,256]{2,1,0:T(8,128)(2,1)S(1)}, bf16[1,768,256]{2,1,0:T(8,128)(2,1)}, u32[]{:S(2)}, u32[]{:S(2)}) collective-permute-start(bf16[1,768,256]{2,1,0:T(8,128)(2,1)S(1)} %collective-permute-done.13.refs_2_), channel_id=1, source_target_pairs={{0,16},{16,0},{32,48},{48,32},{64,80},{80,64},{96,112},{112,96},{1... | collective-permute-start | bytes 1179656 | tf_op jit(solution)/shard_map/ppermute | solution.py:66
  129.3 9.2 %collective-permute-start.10 = (s32[8,128]{1,0:T(8,128)S(1)}, s32[8,128]{1,0:T(8,128)S(1)}, u32[]{:S(2)}, u32[]{:S(2)}) collective-permute-start(s32[8,128]{1,0:T(8,128)S(1)} %broadcast_in_dim.34), channel_id=1, source_target_pairs={{0,0},{1,32},{2,48},{3,16},{16,34},{17,2},{18,18},{19,50},{32,1},{... | collective-permute-start | bytes 12296 | tf_op jit(solution)/shard_map/ppermute | solution.py:43
  159.8 15.7 %collective-permute-start.17 = (bf16[192,384]{1,0:T(8,128)(2,1)}, bf16[192,384]{1,0:T(8,128)(2,1)S(1)}, u32[]{:S(2)}, u32[]{:S(2)}) collective-permute-start(bf16[192,384]{1,0:T(8,128)(2,1)} %get-tuple-element.49), channel_id=1, source_target_pairs={{0,0},{4,4},{8,8},{12,12},{32,1},{36,5},{40,9},{44,13},{48,2},{52,... | collective-permute-start | bytes 442376 | tf_op jit(solution)/shard_map/ppermute | solution.py:56
  166.4 9.1 %collective-permute-start.18 = (bf16[192,384]{1,0:T(8,128)(2,1)}, bf16[192,384]{1,0:T(8,128)(2,1)S(1)}, u32[]{:S(2)}, u32[]{:S(2)}) collective-permute-start(bf16[192,384]{1,0:T(8,128)(2,1)} %get-tuple-element.50), channel_id=1, source_target_pairs={{0,4},{4,0},{8,12},{12,8},{32,5},{36,1},{40,13},{44,9},{48,6},{52,... | collective-permute-start | bytes 442376 | tf_op jit(solution)/shard_map/ppermute | solution.py:56
  166.5 12.0 %collective-permute-start.19 = (bf16[192,384]{1,0:T(8,128)(2,1)}, bf16[192,384]{1,0:T(8,128)(2,1)S(1)}, u32[]{:S(2)}, u32[]{:S(2)}) collective-permute-start(bf16[192,384]{1,0:T(8,128)(2,1)} %get-tuple-element.51), channel_id=1, source_target_pairs={{0,8},{4,12},{8,0},{12,4},{32,9},{36,13},{40,1},{44,5},{48,10},{52... | collective-permute-start | bytes 442376 | tf_op jit(solution)/shard_map/ppermute | solution.py:56
  171.6 10.2 %collective-permute-start.20 = (bf16[192,384]{1,0:T(8,128)(2,1)}, bf16[192,384]{1,0:T(8,128)(2,1)S(1)}, u32[]{:S(2)}, u32[]{:S(2)}) collective-permute-start(bf16[192,384]{1,0:T(8,128)(2,1)} %get-tuple-element.52), channel_id=1, source_target_pairs={{0,12},{4,8},{8,4},{12,0},{32,13},{36,9},{40,5},{44,1},{48,14},{52... | collective-permute-start | bytes 442376 | tf_op jit(solution)/shard_map/ppermute | solution.py:56
  190.5 6.2 %collective-permute-start.23 = (bf16[64,1280]{1,0:T(8,128)(2,1)}, bf16[64,1280]{1,0:T(8,128)(2,1)S(1)}, u32[]{:S(2)}, u32[]{:S(2)}) collective-permute-start(bf16[64,1280]{1,0:T(8,128)(2,1)} %get-tuple-element.61), channel_id=1, source_target_pairs={{0,12},{4,8},{8,4},{12,0},{1,13},{5,9},{9,5},{13,1},{2,14},{6,10},... | collective-permute-start | bytes 491528 | tf_op jit(solution)/shard_map/ppermute | solution.py:66
  192.3 5.9 %collective-permute-start.22 = (bf16[64,1280]{1,0:T(8,128)(2,1)}, bf16[64,1280]{1,0:T(8,128)(2,1)S(1)}, u32[]{:S(2)}, u32[]{:S(2)}) collective-permute-start(bf16[64,1280]{1,0:T(8,128)(2,1)} %get-tuple-element.60), channel_id=1, source_target_pairs={{0,8},{4,12},{8,0},{12,4},{1,9},{5,13},{9,1},{13,5},{2,10},{6,14},... | collective-permute-start | bytes 491528 | tf_op jit(solution)/shard_map/ppermute | solution.py:66
  192.3 6.1 %collective-permute-start.21 = (bf16[64,1280]{1,0:T(8,128)(2,1)}, bf16[64,1280]{1,0:T(8,128)(2,1)S(1)}, u32[]{:S(2)}, u32[]{:S(2)}) collective-permute-start(bf16[64,1280]{1,0:T(8,128)(2,1)} %get-tuple-element.59), channel_id=1, source_target_pairs={{0,4},{4,0},{8,12},{12,8},{1,5},{5,1},{9,13},{13,9},{2,6},{6,2},{1... | collective-permute-start | bytes 491528 | tf_op jit(solution)/shard_map/ppermute | solution.py:66
  199.5 15.4 %collective-permute-start.24 = (f32[16,1280]{1,0:T(8,128)S(1)}, f32[16,1280]{1,0:T(8,128)S(1)}, u32[]{:S(2)}, u32[]{:S(2)}) collective-permute-start(f32[16,1280]{1,0:T(8,128)S(1)} %get-tuple-element.72), channel_id=1, source_target_pairs={{0,1},{1,0},{2,3},{3,2},{4,5},{5,4},{6,7},{7,6},{8,9},{9,8},{10,11... | collective-permute-start | bytes 245768 | tf_op jit(solution)/shard_map/ppermute | solution.py:66
  202.1 12.7 %collective-permute-start.25 = (f32[16,1280]{1,0:T(8,128)S(1)}, f32[16,1280]{1,0:T(8,128)S(1)}, u32[]{:S(2)}, u32[]{:S(2)}) collective-permute-start(f32[16,1280]{1,0:T(8,128)S(1)} %get-tuple-element.71), channel_id=1, source_target_pairs={{0,2},{1,3},{2,0},{3,1},{4,6},{5,7},{6,4},{7,5},{8,10},{9,11},{10,... | collective-permute-start | bytes 245768 | tf_op jit(solution)/shard_map/ppermute | solution.py:66
  202.1 12.8 %collective-permute-start.26 = (f32[16,1280]{1,0:T(8,128)S(1)}, f32[16,1280]{1,0:T(8,128)S(1)}, u32[]{:S(2)}, u32[]{:S(2)}) collective-permute-start(f32[16,1280]{1,0:T(8,128)S(1)} %get-tuple-element.70), channel_id=1, source_target_pairs={{0,3},{1,2},{2,1},{3,0},{4,7},{5,6},{6,5},{7,4},{8,11},{9,10},{10,... | collective-permute-start | bytes 245768 | tf_op jit(solution)/shard_map/ppermute | solution.py:66
  232.7 5.7 %collective-permute-start.33 = (bf16[16,1152]{1,0:T(8,128)(2,1)S(1)}, bf16[16,1152]{1,0:T(8,128)(2,1)S(1)}, u32[]{:S(2)}, u32[]{:S(2)}) collective-permute-start(bf16[16,1152]{1,0:T(8,128)(2,1)S(1)} %add_convert_fusion.refs_0_), channel_id=1, source_target_pairs={{0,1},{1,0},{2,3},{3,2},{4,5},{5,4},{6,7},{7,6},{8,9},{9,8},{10,11... | collective-permute-start | bytes 110600 | tf_op jit(solution)/shard_map/ppermute | solution.py:66
  234.0 6.7 %collective-permute-start.34 = (bf16[16,1152]{1,0:T(8,128)(2,1)S(1)}, bf16[16,1152]{1,0:T(8,128)(2,1)S(1)}, u32[]{:S(2)}, u32[]{:S(2)}) collective-permute-start(bf16[16,1152]{1,0:T(8,128)(2,1)S(1)} %add_convert_fusion.refs_0_), channel_id=1, source_target_pairs={{0,2},{1,3},{2,0},{3,1},{4,6},{5,7},{6,4},{7,5},{8,10},{9,11},{10,... | collective-permute-start | bytes 110600 | tf_op jit(solution)/shard_map/ppermute | solution.py:66
  245.0 6.5 %collective-permute-start.37 = (bf16[64,768]{1,0:T(8,128)(2,1)}, bf16[64,768]{1,0:T(8,128)(2,1)S(1)}, u32[]{:S(2)}, u32[]{:S(2)}) collective-permute-start(bf16[64,768]{1,0:T(8,128)(2,1)} %get-tuple-element.67.refs_0_), channel_id=1, source_target_pairs={{0,8},{4,12},{8,0},{12,4},{1,9},{5,13},{9,1},{13,5},{2,10},{6,14},... | collective-permute-start | bytes 294920 | tf_op jit(solution)/shard_map/ppermute | solution.py:66
  248.2 5.9 %collective-permute-start.38 = (bf16[64,768]{1,0:T(8,128)(2,1)}, bf16[64,768]{1,0:T(8,128)(2,1)S(1)}, u32[]{:S(2)}, u32[]{:S(2)}) collective-permute-start(bf16[64,768]{1,0:T(8,128)(2,1)} %get-tuple-element.67.refs_0_), channel_id=1, source_target_pairs={{0,12},{4,8},{8,4},{12,0},{1,13},{5,9},{9,5},{13,1},{2,14},{6,10},... | collective-permute-start | bytes 294920 | tf_op jit(solution)/shard_map/ppermute | solution.py:66
  (33 other events, 220.9 us)
Sparse Core Ops, SparseCore 0:
  10.4 61.2 all-gather.2
  103.2 65.2 all-gather.4

commit v5 on v4

--- a/solution.py
+++ b/solution.py
@@ -195,8 +195,8 @@
     )(queries, bias, *blocks, *earlier)
 
 
-def standard_body(ints_ref, gain_ref, down_ref, up_ref, noise_ref, *refs):
-    pieces, own_ref, narrow_ref, masked_ref, log_ref = refs[:-4], *refs[-4:]
+def gradients_body(ints_ref, gain_ref, down_ref, up_ref, noise_ref, *refs):
+    pieces, own_ref, outs, (narrow_ref, masked_ref) = refs[:4], refs[4], refs[5:-2], refs[-2:]
     rows, width = noise_ref.shape
     at = 0
     for ref in pieces:
@@ -224,18 +224,13 @@
         return total
 
     total = lax.fori_loop(0, width // chunk, step, jnp.zeros((rows, 128), jnp.float32))
-    log_ref[...] = jnp.full(log_ref.shape, jnp.sum(total))
-
-
-def products_body(ints_ref, narrow_ref, masked_ref, up_ref, own_ref, log_ref, *outs):
-    log = jnp.broadcast_to(log_ref[:1], (outs[0].shape[0], log_ref.shape[1]))
+    log = jnp.full((outs[0].shape[0], 128), jnp.sum(total))
     column = lax.broadcasted_iota(jnp.int32, log.shape, 1)
     high = log.astype(jnp.bfloat16)
     rest = log - high.astype(jnp.float32)
     middle = rest.astype(jnp.bfloat16)
     low = (rest - middle.astype(jnp.float32)).astype(jnp.bfloat16)
     terms = jnp.where(column == 0, high, jnp.where(column == 1, middle, low))
-    width = masked_ref.shape[1]
     count = len(outs)
     columns = width // count
     own_columns = own_ref.shape[1] // count
@@ -246,7 +241,7 @@
         low_grad, own_ref[...], first_axis, preferred_element_type=jnp.float32
     )
     for k, out in enumerate(outs):
-        start = pl.multiple_of(jnp.bitwise_xor(ints_ref[0], k) * columns, 128)
+        start = pl.multiple_of(jnp.bitwise_xor(ints_ref[2], k) * columns, 128)
         out[:, :columns] = lax.dot_general(
             narrow_ref[...],
             masked_ref[:, pl.ds(start, columns)],
@@ -315,7 +310,7 @@
     half = rows // 2
     video_slot = lax.axis_index("fsdp") % 4
     moved_a = gather_tokens(latents[0, :half])
-    moved_b = gather_tokens(after(latents[0, half:], moved_a))
+    moved_b = gather_tokens(latents[0, half:])
     work_limit = gather_tokens(jnp.full((8, 128), limit, jnp.int32))[0, 0]
 
     def norm(x):
@@ -404,29 +399,21 @@
     drift_gain = 1.0 + noise_level**2 / 2.0
     ratio_gain = jnp.sqrt(step_size) * drift_gain / noise_std
     valid_len = limit.astype(jnp.float32)
-    ints = jnp.stack([(uly_id * blk_count + blk_id) * rows, limit]).astype(jnp.int32)
-    own_heads, narrow_projection, masked, log_tile = pl.pallas_call(
-        standard_body,
-        out_shape=(
-            jax.ShapeDtypeStruct((rows, uly_count * local_columns), jnp.bfloat16),
-            jax.ShapeDtypeStruct((rows, rank), jnp.bfloat16),
-            jax.ShapeDtypeStruct((rows, width), jnp.bfloat16),
-            jax.ShapeDtypeStruct((8, 128), jnp.float32),
-        ),
-        in_specs=[smem, smem] + [vmem] * (3 + len(pieces)),
-        out_specs=(vmem,) * 4,
-        name="standard",
-    )(ints, jnp.reshape(ratio_gain, (1,)), down_full, adapter_up_map, sampler_noise[0], *pieces)
-
+    ints = jnp.stack([(uly_id * blk_count + blk_id) * rows, limit, uly_id]).astype(jnp.int32)
     up_columns = width // uly_count
     share_columns = up_columns + local_columns
-    shares = pl.pallas_call(
-        products_body,
-        out_shape=[jax.ShapeDtypeStruct((rank, share_columns + 128), jnp.bfloat16)] * uly_count,
-        in_specs=[smem] + [vmem] * 5,
-        out_specs=[vmem] * uly_count,
-        name="products",
-    )(uly_int, narrow_projection, masked, adapter_up_map, own_heads, log_tile)
+    own_heads, *shares = pl.pallas_call(
+        gradients_body,
+        out_shape=[jax.ShapeDtypeStruct((rows, uly_count * local_columns), jnp.bfloat16)]
+        + [jax.ShapeDtypeStruct((rank, share_columns + 128), jnp.bfloat16)] * uly_count,
+        in_specs=[smem, smem] + [vmem] * (3 + len(pieces)),
+        out_specs=[vmem] * (1 + uly_count),
+        scratch_shapes=[
+            pltpu.VMEM((rows, rank), jnp.bfloat16),
+            pltpu.VMEM((rows, width), jnp.bfloat16),
+        ],
+        name="gradients",
+    )(ints, jnp.reshape(ratio_gain, (1,)), down_full, adapter_up_map, sampler_noise[0], *pieces)
 
     parts = [shares[0]] + [exchange(shares[k], "uly", k) for k in (1, 2, 3)]
     summed = four_sum([part.astype(jnp.float32) for part in parts])
@@ -472,8 +459,9 @@
         / (fsdp_count * valid_len * width)
     )
     summed = summed[:, :share_columns] * coef
-    for unit in (4, 1):
-        summed = four_sum([summed] + [exchange(summed, "fsdp", unit * k) for k in (1, 2, 3)])
+    summed = four_sum([summed] + [exchange(summed, "fsdp", 4 * k) for k in (1, 2, 3)])
+    summed = summed + exchange(summed, "fsdp", 1)
+    summed = summed + exchange(summed, "fsdp", 2)
 
     summed = summed.astype(jnp.bfloat16)
     parts = [exchange(summed, "blk", k) for k in (1, 2, 3)]

time: 266 us -> 264 us (level); the launches traced: 265 us -> 260 us
  starting transfers between devices: 85.8 us -> 80.7 us
  waiting for transfers between devices: 90.2 us -> 93.3 us
    ppermute x5, waiting for transfers between devices: 14.6 us -> 23 us  [shift(): return lax.ppermute(x, axis, [(i, (i + step) % n) for i in range(n)])]
    ppermute x3, waiting for transfers between devices: 27.6 us -> 21.4 us  [gather_tokens(): return lax.ppermute(x, ('fsdp', 'blk'), pairs)]
    ppermute x3, starting transfers between devices: 25.1 us -> 20.5 us  [gather_tokens(): return lax.ppermute(x, ('fsdp', 'blk'), pairs)]
    pallas_call x2 -> x1, Pallas kernels: 8.02 us -> 5.48 us  [shards(): pl.pallas_call(gradients_body, out_shape=[jax.ShapeDtypeStruct((rows, uly...]
    ppermute x27 -> x26, starting transfers between devices: 39.5 us -> 38.4 us  [exchange(): return lax.ppermute(x, axis, [(i, i ^ mask) for i in range(n)])]
    ppermute x27 -> x26, waiting for transfers between devices: 41.7 us -> 41.2 us  [exchange(): return lax.ppermute(x, axis, [(i, i ^ mask) for i in range(n)])]
  transfers between devices with their start and end apart: 41 -> 40, of which waited for: 25 -> 26; matrix products, arithmetic and copies ran while one was open for 3% -> 3% of each run, Pallas kernels for 16% -> 15%
where the time goes in v5:
time: 264 us; the launch traced here: 260 us
  waiting for transfers between devices  93.3 us (35%)
  starting transfers between devices  80.7 us (31%)
  Pallas kernels  54.8 us (21%)
  between operations  19.7 us (7%)
  other arithmetic  5.86 us (2%)
  local copies, waits for them, and re-layouts  5.7 us (2%)
    ppermute x26, waiting for transfers between devices, exchange(): return lax.ppermute(x, axis, [(i, i ^ mask) for i in range(n)])  41.2 us
    ppermute x26, starting transfers between devices, exchange(): return lax.ppermute(x, axis, [(i, i ^ mask) for i in range(n)])  38.4 us
    ppermute x5, waiting for transfers between devices, shift(): return lax.ppermute(x, axis, [(i, (i + step) % n) for i in range(n)])  23 us
    ppermute x3, waiting for transfers between devices, gather_tokens(): return lax.ppermute(x, ('fsdp', 'blk'), pairs)  21.4 us
    ppermute x3, starting transfers between devices, gather_tokens(): return lax.ppermute(x, ('fsdp', 'blk'), pairs)  20.5 us
    pallas_call x2, Pallas kernels, attend(): pl.pallas_call(attention_body, out_shape=[jax.ShapeDtypeStruct((seg, colu...  18.3 us
    pallas_call x2, Pallas kernels, project(): pl.pallas_call(project_body, out_shape=(jax.ShapeDtypeStruct((heads, grou...  16.9 us
    ppermute x4, starting transfers between devices, return_tokens(): return lax.ppermute(x, ('fsdp', 'uly', 'blk'), pairs)  14.4 us
  transfers between devices with their start and end apart: 40, of which 26 were waited for; matrix products, arithmetic and copies ran while one was open for 3% of the time, Pallas kernels for 15%

profile of v5, /device:TPU:1, one launch (start us, length us, event | category | flops | bytes accessed | tf_op | source)
XLA Modules:
  0.0 260.1 jit_solution(15142196680770957087)
XLA Ops:
  9.3 9.8 %collective-permute-start.1 = (bf16[96,3072]{1,0:T(8,128)(2,1)S(1)}, bf16[96,3072]{1,0:T(8,128)(2,1)S(1)}, u32[]{:S(2)}, u32[]{:S(2)}) collective-permute-start(bf16[96,3072]{1,0:T(8,128)(2,1)S(1)} %get-tuple-element.60), channel_id=1, source_target_pairs={{0,0},{1,32},{2,48},{3,16},{16,34},{17,2},{18,18},{19,50},{32,1},{... | collective-permute-start | bytes 1769480 | tf_op jit(solution)/shard_map/ppermute | solution.py:43
  21.0 15.5 %collective-permute-done.1 = bf16[96,3072]{1,0:T(8,128)(2,1)S(1)} collective-permute-done((bf16[96,3072]{1,0:T(8,128)(2,1)S(1)}, bf16[96,3072]{1,0:T(8,128)(2,1)S(1)}, u32[]{:S(2)}, u32[]{:S(2)}) %collective-permute-start.1) | collective-permute-done | bytes 589856 | tf_op jit(solution)/shard_map/ppermute | solution.py:43
  39.7 5.1 %collective-permute-done = bf16[96,3072]{1,0:T(8,128)(2,1)S(1)} collective-permute-done((bf16[96,3072]{1,0:T(8,128)(2,1)S(1)}, bf16[96,3072]{1,0:T(8,128)(2,1)S(1)}, u32[]{:S(2)}, u32[]{:S(2)}) %collective-permute-start) | collective-permute-done | bytes 589856 | tf_op jit(solution)/shard_map/ppermute | solution.py:43
  45.3 4.7 %collective-permute-done.2.left_a_ref = bf16[96,3072]{1,0:T(8,128)(2,1)S(1)} collective-permute-done((bf16[96,3072]{1,0:T(8,128)(2,1)S(1)}, bf16[96,3072]{1,0:T(8,128)(2,1)S(1)}, u32[]{:S(2)}, u32[]{:S(2)}) %collective-permute-start.2) | collective-permute-done | bytes 589856 | tf_op jit(solution)/shard_map/ppermute | solution.py:61
  50.0 3.3 %collective-permute-done.3.right_a_ref = bf16[96,3072]{1,0:T(8,128)(2,1)S(1)} collective-permute-done((bf16[96,3072]{1,0:T(8,128)(2,1)S(1)}, bf16[96,3072]{1,0:T(8,128)(2,1)S(1)}, u32[]{:S(2)}, u32[]{:S(2)}) %collective-permute-start.3) | collective-permute-done | bytes 589856 | tf_op jit(solution)/shard_map/ppermute | solution.py:61
  57.1 8.0 %collective-permute-done.5.right_b_ref = bf16[96,3072]{1,0:T(8,128)(2,1)S(1)} collective-permute-done((bf16[96,3072]{1,0:T(8,128)(2,1)S(1)}, bf16[96,3072]{1,0:T(8,128)(2,1)S(1)}, u32[]{:S(2)}, u32[]{:S(2)}) %collective-permute-start.5) | collective-permute-done | bytes 589856 | tf_op jit(solution)/shard_map/ppermute | solution.py:61
  67.1 3.8 %collective-permute-done.4.up_ref = bf16[192,3072]{1,0:T(8,128)(2,1)S(1)} collective-permute-done((bf16[192,3072]{1,0:T(8,128)(2,1)}, bf16[192,3072]{1,0:T(8,128)(2,1)S(1)}, u32[]{:S(2)}, u32[]{:S(2)}) %collective-permute-start.4) | collective-permute-done | bytes 1179680 | tf_op jit(solution)/shard_map/ppermute | solution.py:61
  70.9 3.1 %collective-permute-done.6.far_b_ref = bf16[96,3072]{1,0:T(8,128)(2,1)} collective-permute-done((bf16[96,3072]{1,0:T(8,128)(2,1)S(1)}, bf16[96,3072]{1,0:T(8,128)(2,1)}, u32[]{:S(2)}, u32[]{:S(2)}) %collective-permute-start.6) | collective-permute-done | bytes 589856 | tf_op jit(solution)/shard_map/ppermute | solution.py:61
  74.0 9.8 %project.3 = (bf16[2,768,256]{2,1,0:T(8,128)(2,1)}, bf16[2,768,128]{2,1,0:T(8,128)(2,1)}) custom-call(s32[1]{0:T(128)} %bitcast.4.ints_ref, bf16[96,3072]{1,0:T(8,128)(2,1)} %copy-done.1, bf16[96,3072]{1,0:T(8,128)(2,1)} %copy-done, bf16[96,3072]{1,0:T(8,128)(2,1)} %copy-done.2, bf16[96,3072]{1,0:T(8,128)(2,1)} %copy-done.5, bf16[192,3072]{1,0:T(8,128)(2,1)} %copy-done.3, ...), custom_call_target="tpu_custom_call" | custom-call | tf_op jit(solution)/shard_map/project/pallas_call | solution.py:349
  83.8 5.8 %collective-permute-start.12 = (bf16[2,768,256]{2,1,0:T(8,128)(2,1)}, bf16[2,768,256]{2,1,0:T(8,128)(2,1)S(1)}, u32[]{:S(2)}, u32[]{:S(2)}) collective-permute-start(bf16[2,768,256]{2,1,0:T(8,128)(2,1)} %get-tuple-element.37.refs_0_), channel_id=1, source_target_pairs={{0,32},{16,48},{32,0},{48,16},{64,96},{80,112},{96,64},{112,80},{1... | collective-permute-start | bytes 2359304 | tf_op jit(solution)/shard_map/ppermute | solution.py:66
  89.7 4.4 %collective-permute-start.8 = (bf16[256,384]{1,0:T(8,128)(2,1)S(1)}, bf16[256,384]{1,0:T(8,128)(2,1)S(1)}, u32[]{:S(2)}, u32[]{:S(2)}) collective-permute-start(bf16[256,384]{1,0:T(8,128)(2,1)S(1)} %pad_maximum_fusion.1), channel_id=1, source_target_pairs={{0,8},{4,12},{8,0},{12,4},{1,9},{5,13},{9,1},{13,5},{2,10},{6,14},... | collective-permute-start | bytes 589832 | tf_op jit(solution)/shard_map/ppermute | solution.py:66
  95.6 3.8 %collective-permute-done.8 = bf16[256,384]{1,0:T(8,128)(2,1)S(1)} collective-permute-done((bf16[256,384]{1,0:T(8,128)(2,1)S(1)}, bf16[256,384]{1,0:T(8,128)(2,1)S(1)}, u32[]{:S(2)}, u32[]{:S(2)}) %collective-permute-start.8) | collective-permute-done | bytes 196640 | tf_op jit(solution)/shard_map/ppermute | solution.py:66
  103.5 7.1 %project.2 = (bf16[1,768,256]{2,1,0:T(8,128)(2,1)}, bf16[1,768,128]{2,1,0:T(8,128)(2,1)}) custom-call(s32[1]{0:T(128)} %bitcast.4.ints_ref, bf16[96,3072]{1,0:T(8,128)(2,1)} %copy-done.1, bf16[96,3072]{1,0:T(8,128)(2,1)} %copy-done, bf16[96,3072]{1,0:T(8,128)(2,1)} %copy-done.2, bf16[96,3072]{1,0:T(8,128)(2,1)} %copy-done.5, bf16[192,3072]{1,0:T(8,128)(2,1)} %copy-done.3, ...), custom_call_target="tpu_custom_call" | custom-call | tf_op jit(solution)/shard_map/project/pallas_call | solution.py:349
  113.2 12.5 %collective-permute-done.13.refs_2_ = bf16[1,768,256]{2,1,0:T(8,128)(2,1)S(1)} collective-permute-done((bf16[1,768,256]{2,1,0:T(8,128)(2,1)}, bf16[1,768,256]{2,1,0:T(8,128)(2,1)S(1)}, u32[]{:S(2)}, u32[]{:S(2)}) %collective-permute-start.13) | collective-permute-done | bytes 393248 | tf_op jit(solution)/shard_map/ppermute | solution.py:66
  128.5 8.8 %collective-permute-start.10 = (s32[8,128]{1,0:T(8,128)S(1)}, s32[8,128]{1,0:T(8,128)S(1)}, u32[]{:S(2)}, u32[]{:S(2)}) collective-permute-start(s32[8,128]{1,0:T(8,128)S(1)} %broadcast_in_dim.34), channel_id=1, source_target_pairs={{0,0},{1,32},{2,48},{3,16},{16,34},{17,2},{18,18},{19,50},{32,1},{... | collective-permute-start | bytes 12296 | tf_op jit(solution)/shard_map/ppermute | solution.py:43
  141.0 11.4 %attend.2 = (bf16[192,256]{1,0:T(8,128)(2,1)}, bf16[192,256]{1,0:T(8,128)(2,1)}, bf16[192,256]{1,0:T(8,128)(2,1)}, bf16[192,256]{1,0:T(8,128)(2,1)}) custom-call(bf16[2,768,128]{2,1,0:T(8,128)(2,1)} %get-tuple-element.39.q_ref, f32[1,3072]{1,0:T(1,128)} %compare_select_fusion.bias_ref, bf16[2,768,256]{2,1,0:T(8,128)(2,1)} %get-tuple-element.37.refs_0_, ...), custom_call_target="tpu_custom_call" | custom-call | tf_op jit(solution)/shard_map/attend/pallas_call | solution.py:181
  152.4 6.9 %attend.3 = (bf16[192,384]{1,0:T(8,128)(2,1)}, bf16[192,384]{1,0:T(8,128)(2,1)}, bf16[192,384]{1,0:T(8,128)(2,1)}, bf16[192,384]{1,0:T(8,128)(2,1)}) custom-call(bf16[1,768,128]{2,1,0:T(8,128)(2,1)} %get-tuple-element.35.q_ref, f32[1,3072]{1,0:T(1,128)} %compare_select_fusion.bias_ref, bf16[1,768,256]{2,1,0:T(8,128)(2,1)} %get-tuple-element.38.refs_0_, ...), custom_call_target="tpu_custom_call" | custom-call | tf_op jit(solution)/shard_map/attend/pallas_call | solution.py:181
  159.3 6.0 %collective-permute-start.17 = (bf16[192,384]{1,0:T(8,128)(2,1)}, bf16[192,384]{1,0:T(8,128)(2,1)S(1)}, u32[]{:S(2)}, u32[]{:S(2)}) collective-permute-start(bf16[192,384]{1,0:T(8,128)(2,1)} %get-tuple-element.44), channel_id=1, source_target_pairs={{0,0},{4,4},{8,8},{12,12},{32,1},{36,5},{40,9},{44,13},{48,2},{52,... | collective-permute-start | bytes 442376 | tf_op jit(solution)/shard_map/ppermute | solution.py:56
  166.8 6.8 %collective-permute-start.19 = (bf16[192,384]{1,0:T(8,128)(2,1)}, bf16[192,384]{1,0:T(8,128)(2,1)S(1)}, u32[]{:S(2)}, u32[]{:S(2)}) collective-permute-start(bf16[192,384]{1,0:T(8,128)(2,1)} %get-tuple-element.46), channel_id=1, source_target_pairs={{0,8},{4,12},{8,0},{12,4},{32,9},{36,13},{40,1},{44,5},{48,10},{52... | collective-permute-start | bytes 442376 | tf_op jit(solution)/shard_map/ppermute | solution.py:56
  175.8 2.9 %collective-permute-done.19.refs_2_ = bf16[192,384]{1,0:T(8,128)(2,1)S(1)} collective-permute-done((bf16[192,384]{1,0:T(8,128)(2,1)}, bf16[192,384]{1,0:T(8,128)(2,1)S(1)}, u32[]{:S(2)}, u32[]{:S(2)}) %collective-permute-start.19) | collective-permute-done | bytes 147488 | tf_op jit(solution)/shard_map/ppermute | solution.py:56
  178.8 4.8 %collective-permute-done.20.refs_3_ = bf16[192,384]{1,0:T(8,128)(2,1)S(1)} collective-permute-done((bf16[192,384]{1,0:T(8,128)(2,1)}, bf16[192,384]{1,0:T(8,128)(2,1)S(1)}, u32[]{:S(2)}, u32[]{:S(2)}) %collective-permute-start.20) | collective-permute-done | bytes 147488 | tf_op jit(solution)/shard_map/ppermute | solution.py:56
  184.2 5.5 %gradients.1 = (bf16[192,1536]{1,0:T(8,128)(2,1)}, bf16[64,1280]{1,0:T(8,128)(2,1)}, bf16[64,1280]{1,0:T(8,128)(2,1)}, bf16[64,1280]{1,0:T(8,128)(2,1)}, bf16[64,1280]{1,0:T(8,128)(2,1)}) custom-call(s32[3]{0:T(128)} %pad_add_fusion.ints_ref, f32[1]{0:T(128)} %bitcast.5.gain_ref, bf16[64,1536]{1,0:T(8,128)(2,1)} %slice.36.down_ref, bf16[64,3072]{1,0:T(8,128)(2,1)} %up_ref.1, ...), custom_call_target="tpu_custom_call" | custom-call | tf_op jit(solution)/shard_map/gradients/pallas_call | solution.py:405
  190.3 2.6 %collective-permute-start.21 = (bf16[64,1280]{1,0:T(8,128)(2,1)}, bf16[64,1280]{1,0:T(8,128)(2,1)S(1)}, u32[]{:S(2)}, u32[]{:S(2)}) collective-permute-start(bf16[64,1280]{1,0:T(8,128)(2,1)} %get-tuple-element.51), channel_id=1, source_target_pairs={{0,4},{4,0},{8,12},{12,8},{1,5},{5,1},{9,13},{13,9},{2,6},{6,2},{1... | collective-permute-start | bytes 491528 | tf_op jit(solution)/shard_map/ppermute | solution.py:66
  193.6 3.4 %collective-permute-done.23 = bf16[64,1280]{1,0:T(8,128)(2,1)S(1)} collective-permute-done((bf16[64,1280]{1,0:T(8,128)(2,1)}, bf16[64,1280]{1,0:T(8,128)(2,1)S(1)}, u32[]{:S(2)}, u32[]{:S(2)}) %collective-permute-start.23) | collective-permute-done | bytes 163872 | tf_op jit(solution)/shard_map/ppermute | solution.py:66
  198.8 5.5 %collective-permute-start.26 = (f32[16,1280]{1,0:T(8,128)S(1)}, f32[16,1280]{1,0:T(8,128)S(1)}, u32[]{:S(2)}, u32[]{:S(2)}) collective-permute-start(f32[16,1280]{1,0:T(8,128)S(1)} %get-tuple-element.62), channel_id=1, source_target_pairs={{0,3},{1,2},{2,1},{3,0},{4,7},{5,6},{6,5},{7,4},{8,11},{9,10},{10,... | collective-permute-start | bytes 245768 | tf_op jit(solution)/shard_map/ppermute | solution.py:66
  205.0 8.7 %move.1 = bf16[192,3072]{1,0:T(8,128)(2,1)} custom-call(f32[4]{0:T(128)} %pad_maximum_fusion.2.scalars_ref, bf16[192,1536]{1,0:T(8,128)(2,1)} %get-tuple-element.48.own_ref, bf16[3072,1536]{1,0:T(8,128)(2,1)} %all-gather.5.cloned.1.call-done.w_ref, bf16[192,3072]{1,0:T(8,128)(2,1)} %bitcast.23, bf16[192,3072]{1,0:T(8,128)(2,1)} %bitcast.22), custom_call_target="tpu_custom_call" | custom-call | tf_op jit(solution)/shard_map/move/pallas_call | solution.py:436
  216.6 2.7 %collective-permute-start.29 = (f32[16,1152]{1,0:T(8,128)S(1)}, f32[16,1152]{1,0:T(8,128)S(1)}, u32[]{:S(2)}, u32[]{:S(2)}) collective-permute-start(f32[16,1152]{1,0:T(8,128)S(1)} %slice_multiply_fusion), channel_id=1, source_target_pairs={{0,192},{16,208},{32,224},{48,240},{64,128},{80,144},{96,160},{112... | collective-permute-start | bytes 221192 | tf_op jit(solution)/shard_map/ppermute | solution.py:66
  226.2 2.8 %collective-permute-done.31 = f32[16,1152]{1,0:T(8,128)S(1)} collective-permute-done((f32[16,1152]{1,0:T(8,128)S(1)}, f32[16,1152]{1,0:T(8,128)S(1)}, u32[]{:S(2)}, u32[]{:S(2)}) %collective-permute-start.31) | collective-permute-done | bytes 73760 | tf_op jit(solution)/shard_map/ppermute | solution.py:66
  230.6 3.7 %collective-permute-start.33 = (bf16[16,1152]{1,0:T(8,128)(2,1)S(1)}, bf16[16,1152]{1,0:T(8,128)(2,1)S(1)}, u32[]{:S(2)}, u32[]{:S(2)}) collective-permute-start(bf16[16,1152]{1,0:T(8,128)(2,1)S(1)} %add_convert_fusion.refs_0_), channel_id=1, source_target_pairs={{0,2},{1,3},{2,0},{3,1},{4,6},{5,7},{6,4},{7,5},{8,10},{9,11},{10,... | collective-permute-start | bytes 110600 | tf_op jit(solution)/shard_map/ppermute | solution.py:66
  234.7 2.8 %collective-permute-done.33.refs_2_ = bf16[16,1152]{1,0:T(8,128)(2,1)S(1)} collective-permute-done((bf16[16,1152]{1,0:T(8,128)(2,1)S(1)}, bf16[16,1152]{1,0:T(8,128)(2,1)S(1)}, u32[]{:S(2)}, u32[]{:S(2)}) %collective-permute-start.33) | collective-permute-done | bytes 36896 | tf_op jit(solution)/shard_map/ppermute | solution.py:66
  242.0 2.6 collective-permute-start.36
  245.5 2.3 collective-permute-done.36.refs_2_
  (135 shorter events, 53.3 us)
Async XLA Ops:
  7.2 66.8 %all-gather.3.cloned.1.call-start = ((), (), s32[]{:S(2)}) async-start(), calls=%async_computation | async-start | bytes 7520256 | tf_op jit(solution)/shard_map/all_gather | solution.py:335
  9.2 195.9 %all-gather.5.cloned.1.call-start = ((), (), s32[]{:S(2)}) async-start(), calls=%async_computation.1 | async-start | bytes 10027008 | tf_op jit(solution)/shard_map/all_gather | solution.py:389
  9.3 27.2 %collective-permute-start.1 = (bf16[96,3072]{1,0:T(8,128)(2,1)S(1)}, bf16[96,3072]{1,0:T(8,128)(2,1)S(1)}, u32[]{:S(2)}, u32[]{:S(2)}) collective-permute-start(bf16[96,3072]{1,0:T(8,128)(2,1)S(1)} %get-tuple-element.60), channel_id=1, source_target_pairs={{0,0},{1,32},{2,48},{3,16},{16,34},{17,2},{18,18},{19,50},{32,1},{... | collective-permute-start | bytes 1769480 | tf_op jit(solution)/shard_map/ppermute | solution.py:43
  19.1 25.8 %collective-permute-start = (bf16[96,3072]{1,0:T(8,128)(2,1)S(1)}, bf16[96,3072]{1,0:T(8,128)(2,1)S(1)}, u32[]{:S(2)}, u32[]{:S(2)}) collective-permute-start(bf16[96,3072]{1,0:T(8,128)(2,1)S(1)} %get-tuple-element.61), channel_id=1, source_target_pairs={{0,0},{1,32},{2,48},{3,16},{16,34},{17,2},{18,18},{19,50},{32,1},{... | collective-permute-start | bytes 1769480 | tf_op jit(solution)/shard_map/ppermute | solution.py:43
  37.0 13.0 %collective-permute-start.2 = (bf16[96,3072]{1,0:T(8,128)(2,1)S(1)}, bf16[96,3072]{1,0:T(8,128)(2,1)S(1)}, u32[]{:S(2)}, u32[]{:S(2)}) collective-permute-start(bf16[96,3072]{1,0:T(8,128)(2,1)S(1)} %fusion.3.a_ref), channel_id=1, source_target_pairs={{0,4},{4,8},{8,12},{12,0},{1,5},{5,9},{9,13},{13,1},{2,6},{6,10},{... | collective-permute-start | bytes 1769480 | tf_op jit(solution)/shard_map/ppermute | solution.py:61
  38.2 15.1 %collective-permute-start.3 = (bf16[96,3072]{1,0:T(8,128)(2,1)S(1)}, bf16[96,3072]{1,0:T(8,128)(2,1)S(1)}, u32[]{:S(2)}, u32[]{:S(2)}) collective-permute-start(bf16[96,3072]{1,0:T(8,128)(2,1)S(1)} %fusion.3.a_ref), channel_id=1, source_target_pairs={{0,12},{4,0},{8,4},{12,8},{1,13},{5,1},{9,5},{13,9},{2,14},{6,2},{... | collective-permute-start | bytes 1769480 | tf_op jit(solution)/shard_map/ppermute | solution.py:61
  54.5 16.5 %collective-permute-start.4 = (bf16[192,3072]{1,0:T(8,128)(2,1)}, bf16[192,3072]{1,0:T(8,128)(2,1)S(1)}, u32[]{:S(2)}, u32[]{:S(2)}) collective-permute-start(bf16[192,3072]{1,0:T(8,128)(2,1)} %pad_maximum_fusion), channel_id=1, source_target_pairs={{0,4},{4,8},{8,12},{12,0},{1,5},{5,9},{9,13},{13,1},{2,6},{6,10},{... | collective-permute-start | bytes 3538952 | tf_op jit(solution)/shard_map/ppermute | solution.py:61
  56.0 9.1 %collective-permute-start.5 = (bf16[96,3072]{1,0:T(8,128)(2,1)S(1)}, bf16[96,3072]{1,0:T(8,128)(2,1)S(1)}, u32[]{:S(2)}, u32[]{:S(2)}) collective-permute-start(bf16[96,3072]{1,0:T(8,128)(2,1)S(1)} %fusion.1.b_ref), channel_id=1, source_target_pairs={{0,12},{4,0},{8,4},{12,8},{1,13},{5,1},{9,5},{13,9},{2,14},{6,2},{... | collective-permute-start | bytes 1769480 | tf_op jit(solution)/shard_map/ppermute | solution.py:61
  65.2 8.8 %collective-permute-start.6 = (bf16[96,3072]{1,0:T(8,128)(2,1)S(1)}, bf16[96,3072]{1,0:T(8,128)(2,1)}, u32[]{:S(2)}, u32[]{:S(2)}) collective-permute-start(bf16[96,3072]{1,0:T(8,128)(2,1)S(1)} %collective-permute-done.5.right_b_ref), channel_id=1, source_target_pairs={{0,12},{4,0},{8,4},{12,8},{1,13},{5,1},{9,5},{13,9},{2,14},{6,2},{... | collective-permute-start | bytes 1769480 | tf_op jit(solution)/shard_map/ppermute | solution.py:61
  83.8 19.6 %collective-permute-start.12 = (bf16[2,768,256]{2,1,0:T(8,128)(2,1)}, bf16[2,768,256]{2,1,0:T(8,128)(2,1)S(1)}, u32[]{:S(2)}, u32[]{:S(2)}) collective-permute-start(bf16[2,768,256]{2,1,0:T(8,128)(2,1)} %get-tuple-element.37.refs_0_), channel_id=1, source_target_pairs={{0,32},{16,48},{32,0},{48,16},{64,96},{80,112},{96,64},{112,80},{1... | collective-permute-start | bytes 2359304 | tf_op jit(solution)/shard_map/ppermute | solution.py:66
  89.6 5.9 %collective-permute-start.7 = (bf16[256,384]{1,0:T(8,128)(2,1)S(1)}, bf16[256,384]{1,0:T(8,128)(2,1)S(1)}, u32[]{:S(2)}, u32[]{:S(2)}) collective-permute-start(bf16[256,384]{1,0:T(8,128)(2,1)S(1)} %pad_maximum_fusion.1), channel_id=1, source_target_pairs={{0,4},{4,0},{8,12},{12,8},{1,5},{5,1},{9,13},{13,9},{2,6},{6,2},{1... | collective-permute-start | bytes 589832 | tf_op jit(solution)/shard_map/ppermute | solution.py:66
  89.7 9.7 %collective-permute-start.8 = (bf16[256,384]{1,0:T(8,128)(2,1)S(1)}, bf16[256,384]{1,0:T(8,128)(2,1)S(1)}, u32[]{:S(2)}, u32[]{:S(2)}) collective-permute-start(bf16[256,384]{1,0:T(8,128)(2,1)S(1)} %pad_maximum_fusion.1), channel_id=1, source_target_pairs={{0,8},{4,12},{8,0},{12,4},{1,9},{5,13},{9,1},{13,5},{2,10},{6,14},... | collective-permute-start | bytes 589832 | tf_op jit(solution)/shard_map/ppermute | solution.py:66
  94.1 7.3 %collective-permute-start.9 = (bf16[256,384]{1,0:T(8,128)(2,1)S(1)}, bf16[256,384]{1,0:T(8,128)(2,1)S(1)}, u32[]{:S(2)}, u32[]{:S(2)}) collective-permute-start(bf16[256,384]{1,0:T(8,128)(2,1)S(1)} %pad_maximum_fusion.1), channel_id=1, source_target_pairs={{0,12},{4,8},{8,4},{12,0},{1,13},{5,9},{9,5},{13,1},{2,14},{6,10},... | collective-permute-start | bytes 589832 | tf_op jit(solution)/shard_map/ppermute | solution.py:66
  103.4 36.7 %collective-permute-start.15 = (bf16[2,768,256]{2,1,0:T(8,128)(2,1)S(1)}, bf16[2,768,256]{2,1,0:T(8,128)(2,1)S(1)}, u32[]{:S(2)}, u32[]{:S(2)}) collective-permute-start(bf16[2,768,256]{2,1,0:T(8,128)(2,1)S(1)} %copy-done.7), channel_id=1, source_target_pairs={{0,16},{16,0},{32,48},{48,32},{64,80},{80,64},{96,112},{112,96},{1... | collective-permute-start | bytes 2359304 | tf_op jit(solution)/shard_map/ppermute | solution.py:66
  110.7 29.5 %collective-permute-start.16 = (bf16[2,768,256]{2,1,0:T(8,128)(2,1)S(1)}, bf16[2,768,256]{2,1,0:T(8,128)(2,1)}, u32[]{:S(2)}, u32[]{:S(2)}) collective-permute-start(bf16[2,768,256]{2,1,0:T(8,128)(2,1)S(1)} %collective-permute-done.12.refs_2_), channel_id=1, source_target_pairs={{0,16},{16,0},{32,48},{48,32},{64,80},{80,64},{96,112},{112,96},{1... | collective-permute-start | bytes 2359304 | tf_op jit(solution)/shard_map/ppermute | solution.py:66
  111.0 14.6 %collective-permute-start.13 = (bf16[1,768,256]{2,1,0:T(8,128)(2,1)}, bf16[1,768,256]{2,1,0:T(8,128)(2,1)S(1)}, u32[]{:S(2)}, u32[]{:S(2)}) collective-permute-start(bf16[1,768,256]{2,1,0:T(8,128)(2,1)} %get-tuple-element.38.refs_0_), channel_id=1, source_target_pairs={{0,32},{16,48},{32,0},{48,16},{64,96},{80,112},{96,64},{112,80},{1... | collective-permute-start | bytes 1179656 | tf_op jit(solution)/shard_map/ppermute | solution.py:66
  112.8 39.6 %collective-permute-start.11 = (bf16[1,768,256]{2,1,0:T(8,128)(2,1)}, bf16[1,768,256]{2,1,0:T(8,128)(2,1)}, u32[]{:S(2)}, u32[]{:S(2)}) collective-permute-start(bf16[1,768,256]{2,1,0:T(8,128)(2,1)} %get-tuple-element.38.refs_0_), channel_id=1, source_target_pairs={{0,16},{16,0},{32,48},{48,32},{64,80},{80,64},{96,112},{112,96},{1... | collective-permute-start | bytes 1179656 | tf_op jit(solution)/shard_map/ppermute | solution.py:66
  125.7 26.7 %collective-permute-start.14 = (bf16[1,768,256]{2,1,0:T(8,128)(2,1)S(1)}, bf16[1,768,256]{2,1,0:T(8,128)(2,1)}, u32[]{:S(2)}, u32[]{:S(2)}) collective-permute-start(bf16[1,768,256]{2,1,0:T(8,128)(2,1)S(1)} %collective-permute-done.13.refs_2_), channel_id=1, source_target_pairs={{0,16},{16,0},{32,48},{48,32},{64,80},{80,64},{96,112},{112,96},{1... | collective-permute-start | bytes 1179656 | tf_op jit(solution)/shard_map/ppermute | solution.py:66
  128.5 9.5 %collective-permute-start.10 = (s32[8,128]{1,0:T(8,128)S(1)}, s32[8,128]{1,0:T(8,128)S(1)}, u32[]{:S(2)}, u32[]{:S(2)}) collective-permute-start(s32[8,128]{1,0:T(8,128)S(1)} %broadcast_in_dim.34), channel_id=1, source_target_pairs={{0,0},{1,32},{2,48},{3,16},{16,34},{17,2},{18,18},{19,50},{32,1},{... | collective-permute-start | bytes 12296 | tf_op jit(solution)/shard_map/ppermute | solution.py:43
  159.3 16.5 %collective-permute-start.17 = (bf16[192,384]{1,0:T(8,128)(2,1)}, bf16[192,384]{1,0:T(8,128)(2,1)S(1)}, u32[]{:S(2)}, u32[]{:S(2)}) collective-permute-start(bf16[192,384]{1,0:T(8,128)(2,1)} %get-tuple-element.44), channel_id=1, source_target_pairs={{0,0},{4,4},{8,8},{12,12},{32,1},{36,5},{40,9},{44,13},{48,2},{52,... | collective-permute-start | bytes 442376 | tf_op jit(solution)/shard_map/ppermute | solution.py:56
  165.4 10.5 %collective-permute-start.18 = (bf16[192,384]{1,0:T(8,128)(2,1)}, bf16[192,384]{1,0:T(8,128)(2,1)S(1)}, u32[]{:S(2)}, u32[]{:S(2)}) collective-permute-start(bf16[192,384]{1,0:T(8,128)(2,1)} %get-tuple-element.45), channel_id=1, source_target_pairs={{0,4},{4,0},{8,12},{12,8},{32,5},{36,1},{40,13},{44,9},{48,6},{52,... | collective-permute-start | bytes 442376 | tf_op jit(solution)/shard_map/ppermute | solution.py:56
  166.8 11.9 %collective-permute-start.19 = (bf16[192,384]{1,0:T(8,128)(2,1)}, bf16[192,384]{1,0:T(8,128)(2,1)S(1)}, u32[]{:S(2)}, u32[]{:S(2)}) collective-permute-start(bf16[192,384]{1,0:T(8,128)(2,1)} %get-tuple-element.46), channel_id=1, source_target_pairs={{0,8},{4,12},{8,0},{12,4},{32,9},{36,13},{40,1},{44,5},{48,10},{52... | collective-permute-start | bytes 442376 | tf_op jit(solution)/shard_map/ppermute | solution.py:56
  173.7 9.9 %collective-permute-start.20 = (bf16[192,384]{1,0:T(8,128)(2,1)}, bf16[192,384]{1,0:T(8,128)(2,1)S(1)}, u32[]{:S(2)}, u32[]{:S(2)}) collective-permute-start(bf16[192,384]{1,0:T(8,128)(2,1)} %get-tuple-element.47), channel_id=1, source_target_pairs={{0,12},{4,8},{8,4},{12,0},{32,13},{36,9},{40,5},{44,1},{48,14},{52... | collective-permute-start | bytes 442376 | tf_op jit(solution)/shard_map/ppermute | solution.py:56
  189.7 7.3 %collective-permute-start.23 = (bf16[64,1280]{1,0:T(8,128)(2,1)}, bf16[64,1280]{1,0:T(8,128)(2,1)S(1)}, u32[]{:S(2)}, u32[]{:S(2)}) collective-permute-start(bf16[64,1280]{1,0:T(8,128)(2,1)} %get-tuple-element.53), channel_id=1, source_target_pairs={{0,12},{4,8},{8,4},{12,0},{1,13},{5,9},{9,5},{13,1},{2,14},{6,10},... | collective-permute-start | bytes 491528 | tf_op jit(solution)/shard_map/ppermute | solution.py:66
  190.0 7.0 %collective-permute-start.22 = (bf16[64,1280]{1,0:T(8,128)(2,1)}, bf16[64,1280]{1,0:T(8,128)(2,1)S(1)}, u32[]{:S(2)}, u32[]{:S(2)}) collective-permute-start(bf16[64,1280]{1,0:T(8,128)(2,1)} %get-tuple-element.52), channel_id=1, source_target_pairs={{0,8},{4,12},{8,0},{12,4},{1,9},{5,13},{9,1},{13,5},{2,10},{6,14},... | collective-permute-start | bytes 491528 | tf_op jit(solution)/shard_map/ppermute | solution.py:66
  190.3 7.3 %collective-permute-start.21 = (bf16[64,1280]{1,0:T(8,128)(2,1)}, bf16[64,1280]{1,0:T(8,128)(2,1)S(1)}, u32[]{:S(2)}, u32[]{:S(2)}) collective-permute-start(bf16[64,1280]{1,0:T(8,128)(2,1)} %get-tuple-element.51), channel_id=1, source_target_pairs={{0,4},{4,0},{8,12},{12,8},{1,5},{5,1},{9,13},{13,9},{2,6},{6,2},{1... | collective-permute-start | bytes 491528 | tf_op jit(solution)/shard_map/ppermute | solution.py:66
  198.6 15.1 %collective-permute-start.24 = (f32[16,1280]{1,0:T(8,128)S(1)}, f32[16,1280]{1,0:T(8,128)S(1)}, u32[]{:S(2)}, u32[]{:S(2)}) collective-permute-start(f32[16,1280]{1,0:T(8,128)S(1)} %get-tuple-element.64), channel_id=1, source_target_pairs={{0,1},{1,0},{2,3},{3,2},{4,5},{5,4},{6,7},{7,6},{8,9},{9,8},{10,11... | collective-permute-start | bytes 245768 | tf_op jit(solution)/shard_map/ppermute | solution.py:66
  198.7 15.0 %collective-permute-start.25 = (f32[16,1280]{1,0:T(8,128)S(1)}, f32[16,1280]{1,0:T(8,128)S(1)}, u32[]{:S(2)}, u32[]{:S(2)}) collective-permute-start(f32[16,1280]{1,0:T(8,128)S(1)} %get-tuple-element.63), channel_id=1, source_target_pairs={{0,2},{1,3},{2,0},{3,1},{4,6},{5,7},{6,4},{7,5},{8,10},{9,11},{10,... | collective-permute-start | bytes 245768 | tf_op jit(solution)/shard_map/ppermute | solution.py:66
  198.8 14.9 %collective-permute-start.26 = (f32[16,1280]{1,0:T(8,128)S(1)}, f32[16,1280]{1,0:T(8,128)S(1)}, u32[]{:S(2)}, u32[]{:S(2)}) collective-permute-start(f32[16,1280]{1,0:T(8,128)S(1)} %get-tuple-element.62), channel_id=1, source_target_pairs={{0,3},{1,2},{2,1},{3,0},{4,7},{5,6},{6,5},{7,4},{8,11},{9,10},{10,... | collective-permute-start | bytes 245768 | tf_op jit(solution)/shard_map/ppermute | solution.py:66
  216.6 6.9 %collective-permute-start.29 = (f32[16,1152]{1,0:T(8,128)S(1)}, f32[16,1152]{1,0:T(8,128)S(1)}, u32[]{:S(2)}, u32[]{:S(2)}) collective-permute-start(f32[16,1152]{1,0:T(8,128)S(1)} %slice_multiply_fusion), channel_id=1, source_target_pairs={{0,192},{16,208},{32,224},{48,240},{64,128},{80,144},{96,160},{112... | collective-permute-start | bytes 221192 | tf_op jit(solution)/shard_map/ppermute | solution.py:66
  230.6 6.9 %collective-permute-start.33 = (bf16[16,1152]{1,0:T(8,128)(2,1)S(1)}, bf16[16,1152]{1,0:T(8,128)(2,1)S(1)}, u32[]{:S(2)}, u32[]{:S(2)}) collective-permute-start(bf16[16,1152]{1,0:T(8,128)(2,1)S(1)} %add_convert_fusion.refs_0_), channel_id=1, source_target_pairs={{0,2},{1,3},{2,0},{3,1},{4,6},{5,7},{6,4},{7,5},{8,10},{9,11},{10,... | collective-permute-start | bytes 110600 | tf_op jit(solution)/shard_map/ppermute | solution.py:66
  242.0 5.8 %collective-permute-start.36 = (bf16[64,768]{1,0:T(8,128)(2,1)}, bf16[64,768]{1,0:T(8,128)(2,1)S(1)}, u32[]{:S(2)}, u32[]{:S(2)}) collective-permute-start(bf16[64,768]{1,0:T(8,128)(2,1)} %get-tuple-element.59.refs_0_), channel_id=1, source_target_pairs={{0,8},{4,12},{8,0},{12,4},{1,9},{5,13},{9,1},{13,5},{2,10},{6,14},... | collective-permute-start | bytes 294920 | tf_op jit(solution)/shard_map/ppermute | solution.py:66
  (32 other events, 234.2 us)
Sparse Core Ops, SparseCore 0:
  10.4 62.0 all-gather.2
  103.5 65.9 all-gather.4

commit v6 on v5

--- a/solution.py
+++ b/solution.py
@@ -342,8 +342,10 @@
     far_b = shift(right_b, "uly", -1)
 
     maps = after(jnp.concatenate((output_weight, adapter_down_map), 0), up, far_b)
-    maps = jnp.concatenate([maps] + [exchange(maps, "uly", k) for k in (1, 2, 3)], 1)
-    output_columns, down_full = maps[: output_weight.shape[0]], maps[output_weight.shape[0] :]
+    maps = [maps] + [exchange(maps, "uly", k) for k in (1, 2, 3)]
+    mine = output_weight.shape[0]
+    output_columns = jnp.concatenate([m[:mine] for m in maps], 1)
+    down_full = jnp.concatenate([m[mine:] for m in maps], 1)
 
     def project(first_head, heads):
         return pl.pallas_call(
@@ -423,7 +425,7 @@
         return lax.dynamic_slice_in_dim(summed, (blk_id ^ k) * part, part, 0)
 
     parts = [exchange(rows_of(k), "blk", k) for k in (1, 2, 3)]
-    tile = 512
+    tile = 768
     scalars = jnp.stack(
         [
             jnp.float32(step_size),

time: 264 us -> 252 us (0.955)
  waiting for transfers between devices: 93.3 us -> 77 us
  starting transfers between devices: 80.7 us -> 85.3 us
    ppermute x26, waiting for transfers between devices: 41.2 us -> 27.4 us  [exchange(): return lax.ppermute(x, axis, [(i, i ^ mask) for i in range(n)])]
    ppermute x4, starting transfers between devices: 14.4 us -> 18.7 us  [return_tokens(): return lax.ppermute(x, ('fsdp', 'uly', 'blk'), pairs)]
  transfers between devices with their start and end apart: 40 -> 40, of which waited for: 26 -> 24; matrix products, arithmetic and copies ran while one was open for 3% -> 3% of each run, Pallas kernels for 15% -> 16%
where the time goes in v6:
time: 252 us; the launch traced here: 249 us
  starting transfers between devices  85.3 us (34%)
  waiting for transfers between devices  77 us (31%)
  Pallas kernels  54.1 us (21%)
  between operations  19.7 us (8%)
  other arithmetic  7.38 us (3%)
  local copies, waits for them, and re-layouts  5.63 us (2%)
    ppermute x26, starting transfers between devices, exchange(): return lax.ppermute(x, axis, [(i, i ^ mask) for i in range(n)])  40.7 us
    ppermute x26, waiting for transfers between devices, exchange(): return lax.ppermute(x, axis, [(i, i ^ mask) for i in range(n)])  27.4 us
    ppermute x5, waiting for transfers between devices, shift(): return lax.ppermute(x, axis, [(i, (i + step) % n) for i in range(n)])  23 us
    ppermute x3, waiting for transfers between devices, gather_tokens(): return lax.ppermute(x, ('fsdp', 'blk'), pairs)  20.7 us
    ppermute x4, starting transfers between devices, return_tokens(): return lax.ppermute(x, ('fsdp', 'uly', 'blk'), pairs)  18.7 us
    ppermute x3, starting transfers between devices, gather_tokens(): return lax.ppermute(x, ('fsdp', 'blk'), pairs)  18.6 us
    pallas_call x2, Pallas kernels, attend(): pl.pallas_call(attention_body, out_shape=[jax.ShapeDtypeStruct((seg, colu...  18.4 us
    pallas_call x2, Pallas kernels, project(): pl.pallas_call(project_body, out_shape=(jax.ShapeDtypeStruct((heads, grou...  17 us
  transfers between devices with their start and end apart: 40, of which 24 were waited for; matrix products, arithmetic and copies ran while one was open for 3% of the time, Pallas kernels for 16%

profile of v6, /device:TPU:1, one launch (start us, length us, event | category | flops | bytes accessed | tf_op | source)
XLA Modules:
  0.0 249.1 jit_solution(18362865368784244362)
XLA Ops:
  9.3 9.8 %collective-permute-start.1 = (bf16[96,3072]{1,0:T(8,128)(2,1)S(1)}, bf16[96,3072]{1,0:T(8,128)(2,1)S(1)}, u32[]{:S(2)}, u32[]{:S(2)}) collective-permute-start(bf16[96,3072]{1,0:T(8,128)(2,1)S(1)} %get-tuple-element.60), channel_id=1, source_target_pairs={{0,0},{1,32},{2,48},{3,16},{16,34},{17,2},{18,18},{19,50},{32,1},{... | collective-permute-start | bytes 1769480 | tf_op jit(solution)/shard_map/ppermute | solution.py:43
  21.0 15.5 %collective-permute-done.1 = bf16[96,3072]{1,0:T(8,128)(2,1)S(1)} collective-permute-done((bf16[96,3072]{1,0:T(8,128)(2,1)S(1)}, bf16[96,3072]{1,0:T(8,128)(2,1)S(1)}, u32[]{:S(2)}, u32[]{:S(2)}) %collective-permute-start.1) | collective-permute-done | bytes 589856 | tf_op jit(solution)/shard_map/ppermute | solution.py:43
  39.7 5.1 %collective-permute-done = bf16[96,3072]{1,0:T(8,128)(2,1)S(1)} collective-permute-done((bf16[96,3072]{1,0:T(8,128)(2,1)S(1)}, bf16[96,3072]{1,0:T(8,128)(2,1)S(1)}, u32[]{:S(2)}, u32[]{:S(2)}) %collective-permute-start) | collective-permute-done | bytes 589856 | tf_op jit(solution)/shard_map/ppermute | solution.py:43
  45.3 4.7 %collective-permute-done.2.left_a_ref = bf16[96,3072]{1,0:T(8,128)(2,1)S(1)} collective-permute-done((bf16[96,3072]{1,0:T(8,128)(2,1)S(1)}, bf16[96,3072]{1,0:T(8,128)(2,1)S(1)}, u32[]{:S(2)}, u32[]{:S(2)}) %collective-permute-start.2) | collective-permute-done | bytes 589856 | tf_op jit(solution)/shard_map/ppermute | solution.py:61
  50.0 3.3 %collective-permute-done.3.right_a_ref = bf16[96,3072]{1,0:T(8,128)(2,1)S(1)} collective-permute-done((bf16[96,3072]{1,0:T(8,128)(2,1)S(1)}, bf16[96,3072]{1,0:T(8,128)(2,1)S(1)}, u32[]{:S(2)}, u32[]{:S(2)}) %collective-permute-start.3) | collective-permute-done | bytes 589856 | tf_op jit(solution)/shard_map/ppermute | solution.py:61
  57.1 8.0 %collective-permute-done.5.right_b_ref = bf16[96,3072]{1,0:T(8,128)(2,1)S(1)} collective-permute-done((bf16[96,3072]{1,0:T(8,128)(2,1)S(1)}, bf16[96,3072]{1,0:T(8,128)(2,1)S(1)}, u32[]{:S(2)}, u32[]{:S(2)}) %collective-permute-start.5) | collective-permute-done | bytes 589856 | tf_op jit(solution)/shard_map/ppermute | solution.py:61
  67.1 3.8 %collective-permute-done.4.up_ref = bf16[192,3072]{1,0:T(8,128)(2,1)S(1)} collective-permute-done((bf16[192,3072]{1,0:T(8,128)(2,1)}, bf16[192,3072]{1,0:T(8,128)(2,1)S(1)}, u32[]{:S(2)}, u32[]{:S(2)}) %collective-permute-start.4) | collective-permute-done | bytes 1179680 | tf_op jit(solution)/shard_map/ppermute | solution.py:61
  70.9 3.1 %collective-permute-done.6.far_b_ref = bf16[96,3072]{1,0:T(8,128)(2,1)} collective-permute-done((bf16[96,3072]{1,0:T(8,128)(2,1)S(1)}, bf16[96,3072]{1,0:T(8,128)(2,1)}, u32[]{:S(2)}, u32[]{:S(2)}) %collective-permute-start.6) | collective-permute-done | bytes 589856 | tf_op jit(solution)/shard_map/ppermute | solution.py:61
  74.0 9.8 %project.3 = (bf16[2,768,256]{2,1,0:T(8,128)(2,1)}, bf16[2,768,128]{2,1,0:T(8,128)(2,1)}) custom-call(s32[1]{0:T(128)} %bitcast.4.ints_ref, bf16[96,3072]{1,0:T(8,128)(2,1)} %copy-done.1, bf16[96,3072]{1,0:T(8,128)(2,1)} %copy-done, bf16[96,3072]{1,0:T(8,128)(2,1)} %copy-done.2, bf16[96,3072]{1,0:T(8,128)(2,1)} %copy-done.5, bf16[192,3072]{1,0:T(8,128)(2,1)} %copy-done.3, ...), custom_call_target="tpu_custom_call" | custom-call | tf_op jit(solution)/shard_map/project/pallas_call | solution.py:351
  83.8 5.8 %collective-permute-start.12 = (bf16[2,768,256]{2,1,0:T(8,128)(2,1)}, bf16[2,768,256]{2,1,0:T(8,128)(2,1)S(1)}, u32[]{:S(2)}, u32[]{:S(2)}) collective-permute-start(bf16[2,768,256]{2,1,0:T(8,128)(2,1)} %get-tuple-element.37.refs_0_), channel_id=1, source_target_pairs={{0,32},{16,48},{32,0},{48,16},{64,96},{80,112},{96,64},{112,80},{1... | collective-permute-start | bytes 2359304 | tf_op jit(solution)/shard_map/ppermute | solution.py:66
  89.6 3.3 %collective-permute-start.9 = (bf16[256,384]{1,0:T(8,128)(2,1)S(1)}, bf16[256,384]{1,0:T(8,128)(2,1)S(1)}, u32[]{:S(2)}, u32[]{:S(2)}) collective-permute-start(bf16[256,384]{1,0:T(8,128)(2,1)S(1)} %pad_maximum_fusion.2), channel_id=1, source_target_pairs={{0,12},{4,8},{8,4},{12,0},{1,13},{5,9},{9,5},{13,1},{2,14},{6,10},... | collective-permute-start | bytes 589832 | tf_op jit(solution)/shard_map/ppermute | solution.py:66
  93.7 4.0 %collective-permute-done.9 = bf16[256,384]{1,0:T(8,128)(2,1)S(1)} collective-permute-done((bf16[256,384]{1,0:T(8,128)(2,1)S(1)}, bf16[256,384]{1,0:T(8,128)(2,1)S(1)}, u32[]{:S(2)}, u32[]{:S(2)}) %collective-permute-start.9) | collective-permute-done | bytes 196640 | tf_op jit(solution)/shard_map/ppermute | solution.py:66
  103.4 7.3 %project.2 = (bf16[1,768,256]{2,1,0:T(8,128)(2,1)}, bf16[1,768,128]{2,1,0:T(8,128)(2,1)}) custom-call(s32[1]{0:T(128)} %bitcast.4.ints_ref, bf16[96,3072]{1,0:T(8,128)(2,1)} %copy-done.1, bf16[96,3072]{1,0:T(8,128)(2,1)} %copy-done, bf16[96,3072]{1,0:T(8,128)(2,1)} %copy-done.2, bf16[96,3072]{1,0:T(8,128)(2,1)} %copy-done.5, bf16[192,3072]{1,0:T(8,128)(2,1)} %copy-done.3, ...), custom_call_target="tpu_custom_call" | custom-call | tf_op jit(solution)/shard_map/project/pallas_call | solution.py:351
  113.6 6.9 %collective-permute-start.10 = (s32[8,128]{1,0:T(8,128)S(1)}, s32[8,128]{1,0:T(8,128)S(1)}, u32[]{:S(2)}, u32[]{:S(2)}) collective-permute-start(s32[8,128]{1,0:T(8,128)S(1)} %broadcast_in_dim.34), channel_id=1, source_target_pairs={{0,0},{1,32},{2,48},{3,16},{16,34},{17,2},{18,18},{19,50},{32,1},{... | collective-permute-start | bytes 12296 | tf_op jit(solution)/shard_map/ppermute | solution.py:43
  127.0 11.4 %attend.2 = (bf16[192,256]{1,0:T(8,128)(2,1)}, bf16[192,256]{1,0:T(8,128)(2,1)}, bf16[192,256]{1,0:T(8,128)(2,1)}, bf16[192,256]{1,0:T(8,128)(2,1)}) custom-call(bf16[2,768,128]{2,1,0:T(8,128)(2,1)} %get-tuple-element.39.q_ref, f32[1,3072]{1,0:T(1,128)} %compare_select_fusion.bias_ref, bf16[2,768,256]{2,1,0:T(8,128)(2,1)} %get-tuple-element.37.refs_0_, ...), custom_call_target="tpu_custom_call" | custom-call | tf_op jit(solution)/shard_map/attend/pallas_call | solution.py:181
  138.5 7.0 %attend.3 = (bf16[192,384]{1,0:T(8,128)(2,1)}, bf16[192,384]{1,0:T(8,128)(2,1)}, bf16[192,384]{1,0:T(8,128)(2,1)}, bf16[192,384]{1,0:T(8,128)(2,1)}) custom-call(bf16[1,768,128]{2,1,0:T(8,128)(2,1)} %get-tuple-element.35.q_ref, f32[1,3072]{1,0:T(1,128)} %compare_select_fusion.bias_ref, bf16[1,768,256]{2,1,0:T(8,128)(2,1)} %get-tuple-element.38.refs_0_, ...), custom_call_target="tpu_custom_call" | custom-call | tf_op jit(solution)/shard_map/attend/pallas_call | solution.py:181
  145.5 6.1 %collective-permute-start.17 = (bf16[192,384]{1,0:T(8,128)(2,1)}, bf16[192,384]{1,0:T(8,128)(2,1)S(1)}, u32[]{:S(2)}, u32[]{:S(2)}) collective-permute-start(bf16[192,384]{1,0:T(8,128)(2,1)} %get-tuple-element.44), channel_id=1, source_target_pairs={{0,0},{4,4},{8,8},{12,12},{32,1},{36,5},{40,9},{44,13},{48,2},{52,... | collective-permute-start | bytes 442376 | tf_op jit(solution)/shard_map/ppermute | solution.py:56
  151.6 6.9 %collective-permute-start.18 = (bf16[192,384]{1,0:T(8,128)(2,1)}, bf16[192,384]{1,0:T(8,128)(2,1)S(1)}, u32[]{:S(2)}, u32[]{:S(2)}) collective-permute-start(bf16[192,384]{1,0:T(8,128)(2,1)} %get-tuple-element.45), channel_id=1, source_target_pairs={{0,4},{4,0},{8,12},{12,8},{32,5},{36,1},{40,13},{44,9},{48,6},{52,... | collective-permute-start | bytes 442376 | tf_op jit(solution)/shard_map/ppermute | solution.py:56
  159.7 4.4 %collective-permute-start.20 = (bf16[192,384]{1,0:T(8,128)(2,1)}, bf16[192,384]{1,0:T(8,128)(2,1)S(1)}, u32[]{:S(2)}, u32[]{:S(2)}) collective-permute-start(bf16[192,384]{1,0:T(8,128)(2,1)} %get-tuple-element.47), channel_id=1, source_target_pairs={{0,12},{4,8},{8,4},{12,0},{32,13},{36,9},{40,5},{44,1},{48,14},{52... | collective-permute-start | bytes 442376 | tf_op jit(solution)/shard_map/ppermute | solution.py:56
  165.8 5.0 %collective-permute-done.19.refs_2_ = bf16[192,384]{1,0:T(8,128)(2,1)S(1)} collective-permute-done((bf16[192,384]{1,0:T(8,128)(2,1)}, bf16[192,384]{1,0:T(8,128)(2,1)S(1)}, u32[]{:S(2)}, u32[]{:S(2)}) %collective-permute-start.19) | collective-permute-done | bytes 147488 | tf_op jit(solution)/shard_map/ppermute | solution.py:56
  171.5 5.5 %gradients.1 = (bf16[192,1536]{1,0:T(8,128)(2,1)}, bf16[64,1280]{1,0:T(8,128)(2,1)}, bf16[64,1280]{1,0:T(8,128)(2,1)}, bf16[64,1280]{1,0:T(8,128)(2,1)}, bf16[64,1280]{1,0:T(8,128)(2,1)}) custom-call(s32[3]{0:T(128)} %pad_add_fusion.ints_ref, f32[1]{0:T(128)} %bitcast.5.gain_ref, bf16[64,1536]{1,0:T(8,128)(2,1)} %pad_maximum_fusion.3.down_ref, ...), custom_call_target="tpu_custom_call" | custom-call | tf_op jit(solution)/shard_map/gradients/pallas_call | solution.py:407
  178.1 2.4 collective-permute-start.22
  181.1 3.2 %collective-permute-done.23 = bf16[64,1280]{1,0:T(8,128)(2,1)S(1)} collective-permute-done((bf16[64,1280]{1,0:T(8,128)(2,1)}, bf16[64,1280]{1,0:T(8,128)(2,1)S(1)}, u32[]{:S(2)}, u32[]{:S(2)}) %collective-permute-start.23) | collective-permute-done | bytes 163872 | tf_op jit(solution)/shard_map/ppermute | solution.py:66
  185.9 5.0 %collective-permute-start.24 = (f32[16,1280]{1,0:T(8,128)S(1)}, f32[16,1280]{1,0:T(8,128)S(1)}, u32[]{:S(2)}, u32[]{:S(2)}) collective-permute-start(f32[16,1280]{1,0:T(8,128)S(1)} %get-tuple-element.64), channel_id=1, source_target_pairs={{0,1},{1,0},{2,3},{3,2},{4,5},{5,4},{6,7},{7,6},{8,9},{9,8},{10,11... | collective-permute-start | bytes 245768 | tf_op jit(solution)/shard_map/ppermute | solution.py:66
  190.9 3.4 %collective-permute-start.26 = (f32[16,1280]{1,0:T(8,128)S(1)}, f32[16,1280]{1,0:T(8,128)S(1)}, u32[]{:S(2)}, u32[]{:S(2)}) collective-permute-start(f32[16,1280]{1,0:T(8,128)S(1)} %get-tuple-element.62), channel_id=1, source_target_pairs={{0,3},{1,2},{2,1},{3,0},{4,7},{5,6},{6,5},{7,4},{8,11},{9,10},{10,... | collective-permute-start | bytes 245768 | tf_op jit(solution)/shard_map/ppermute | solution.py:66
  194.9 7.8 %move.1 = bf16[192,3072]{1,0:T(8,128)(2,1)} custom-call(f32[4]{0:T(128)} %pad_maximum_fusion.4.scalars_ref, bf16[192,1536]{1,0:T(8,128)(2,1)} %get-tuple-element.48.own_ref, bf16[3072,1536]{1,0:T(8,128)(2,1)} %all-gather.5.cloned.1.call-done.w_ref, bf16[192,3072]{1,0:T(8,128)(2,1)} %bitcast.23, bf16[192,3072]{1,0:T(8,128)(2,1)} %bitcast.22), custom_call_target="tpu_custom_call" | custom-call | tf_op jit(solution)/shard_map/move/pallas_call | solution.py:438
  214.1 2.8 %collective-permute-start.31 = (f32[16,1152]{1,0:T(8,128)S(1)}, f32[16,1152]{1,0:T(8,128)S(1)}, u32[]{:S(2)}, u32[]{:S(2)}) collective-permute-start(f32[16,1152]{1,0:T(8,128)S(1)} %add.162), channel_id=1, source_target_pairs={{0,32},{16,48},{32,0},{48,16},{64,96},{80,112},{96,64},{112,80},{1... | collective-permute-start | bytes 221192 | tf_op jit(solution)/shard_map/ppermute | solution.py:66
  217.0 2.3 collective-permute-done.31
  219.8 2.9 %collective-permute-start.33 = (bf16[16,1152]{1,0:T(8,128)(2,1)S(1)}, bf16[16,1152]{1,0:T(8,128)(2,1)S(1)}, u32[]{:S(2)}, u32[]{:S(2)}) collective-permute-start(bf16[16,1152]{1,0:T(8,128)(2,1)S(1)} %add_convert_fusion.refs_0_), channel_id=1, source_target_pairs={{0,2},{1,3},{2,0},{3,1},{4,6},{5,7},{6,4},{7,5},{8,10},{9,11},{10,... | collective-permute-start | bytes 110600 | tf_op jit(solution)/shard_map/ppermute | solution.py:66
  222.7 2.4 collective-permute-start.34
  231.2 2.4 collective-permute-start.36
  233.7 3.3 %collective-permute-done.36.refs_2_ = bf16[64,768]{1,0:T(8,128)(2,1)S(1)} collective-permute-done((bf16[64,768]{1,0:T(8,128)(2,1)}, bf16[64,768]{1,0:T(8,128)(2,1)S(1)}, u32[]{:S(2)}, u32[]{:S(2)}) %collective-permute-start.36) | collective-permute-done | bytes 98336 | tf_op jit(solution)/shard_map/ppermute | solution.py:66
  (148 shorter events, 54.9 us)
Async XLA Ops:
  7.2 66.8 %all-gather.3.cloned.1.call-start = ((), (), s32[]{:S(2)}) async-start(), calls=%async_computation | async-start | bytes 7520256 | tf_op jit(solution)/shard_map/all_gather | solution.py:335
  9.2 185.7 %all-gather.5.cloned.1.call-start = ((), (), s32[]{:S(2)}) async-start(), calls=%async_computation.1 | async-start | bytes 10027008 | tf_op jit(solution)/shard_map/all_gather | solution.py:391
  9.3 27.2 %collective-permute-start.1 = (bf16[96,3072]{1,0:T(8,128)(2,1)S(1)}, bf16[96,3072]{1,0:T(8,128)(2,1)S(1)}, u32[]{:S(2)}, u32[]{:S(2)}) collective-permute-start(bf16[96,3072]{1,0:T(8,128)(2,1)S(1)} %get-tuple-element.60), channel_id=1, source_target_pairs={{0,0},{1,32},{2,48},{3,16},{16,34},{17,2},{18,18},{19,50},{32,1},{... | collective-permute-start | bytes 1769480 | tf_op jit(solution)/shard_map/ppermute | solution.py:43
  19.1 25.8 %collective-permute-start = (bf16[96,3072]{1,0:T(8,128)(2,1)S(1)}, bf16[96,3072]{1,0:T(8,128)(2,1)S(1)}, u32[]{:S(2)}, u32[]{:S(2)}) collective-permute-start(bf16[96,3072]{1,0:T(8,128)(2,1)S(1)} %get-tuple-element.61), channel_id=1, source_target_pairs={{0,0},{1,32},{2,48},{3,16},{16,34},{17,2},{18,18},{19,50},{32,1},{... | collective-permute-start | bytes 1769480 | tf_op jit(solution)/shard_map/ppermute | solution.py:43
  37.0 13.0 %collective-permute-start.2 = (bf16[96,3072]{1,0:T(8,128)(2,1)S(1)}, bf16[96,3072]{1,0:T(8,128)(2,1)S(1)}, u32[]{:S(2)}, u32[]{:S(2)}) collective-permute-start(bf16[96,3072]{1,0:T(8,128)(2,1)S(1)} %fusion.3.a_ref), channel_id=1, source_target_pairs={{0,4},{4,8},{8,12},{12,0},{1,5},{5,9},{9,13},{13,1},{2,6},{6,10},{... | collective-permute-start | bytes 1769480 | tf_op jit(solution)/shard_map/ppermute | solution.py:61
  38.2 15.1 %collective-permute-start.3 = (bf16[96,3072]{1,0:T(8,128)(2,1)S(1)}, bf16[96,3072]{1,0:T(8,128)(2,1)S(1)}, u32[]{:S(2)}, u32[]{:S(2)}) collective-permute-start(bf16[96,3072]{1,0:T(8,128)(2,1)S(1)} %fusion.3.a_ref), channel_id=1, source_target_pairs={{0,12},{4,0},{8,4},{12,8},{1,13},{5,1},{9,5},{13,9},{2,14},{6,2},{... | collective-permute-start | bytes 1769480 | tf_op jit(solution)/shard_map/ppermute | solution.py:61
  54.5 16.5 %collective-permute-start.4 = (bf16[192,3072]{1,0:T(8,128)(2,1)}, bf16[192,3072]{1,0:T(8,128)(2,1)S(1)}, u32[]{:S(2)}, u32[]{:S(2)}) collective-permute-start(bf16[192,3072]{1,0:T(8,128)(2,1)} %pad_maximum_fusion), channel_id=1, source_target_pairs={{0,4},{4,8},{8,12},{12,0},{1,5},{5,9},{9,13},{13,1},{2,6},{6,10},{... | collective-permute-start | bytes 3538952 | tf_op jit(solution)/shard_map/ppermute | solution.py:61
  56.0 9.1 %collective-permute-start.5 = (bf16[96,3072]{1,0:T(8,128)(2,1)S(1)}, bf16[96,3072]{1,0:T(8,128)(2,1)S(1)}, u32[]{:S(2)}, u32[]{:S(2)}) collective-permute-start(bf16[96,3072]{1,0:T(8,128)(2,1)S(1)} %fusion.1.b_ref), channel_id=1, source_target_pairs={{0,12},{4,0},{8,4},{12,8},{1,13},{5,1},{9,5},{13,9},{2,14},{6,2},{... | collective-permute-start | bytes 1769480 | tf_op jit(solution)/shard_map/ppermute | solution.py:61
  65.2 8.8 %collective-permute-start.6 = (bf16[96,3072]{1,0:T(8,128)(2,1)S(1)}, bf16[96,3072]{1,0:T(8,128)(2,1)}, u32[]{:S(2)}, u32[]{:S(2)}) collective-permute-start(bf16[96,3072]{1,0:T(8,128)(2,1)S(1)} %collective-permute-done.5.right_b_ref), channel_id=1, source_target_pairs={{0,12},{4,0},{8,4},{12,8},{1,13},{5,1},{9,5},{13,9},{2,14},{6,2},{... | collective-permute-start | bytes 1769480 | tf_op jit(solution)/shard_map/ppermute | solution.py:61
  83.8 19.6 %collective-permute-start.12 = (bf16[2,768,256]{2,1,0:T(8,128)(2,1)}, bf16[2,768,256]{2,1,0:T(8,128)(2,1)S(1)}, u32[]{:S(2)}, u32[]{:S(2)}) collective-permute-start(bf16[2,768,256]{2,1,0:T(8,128)(2,1)} %get-tuple-element.37.refs_0_), channel_id=1, source_target_pairs={{0,32},{16,48},{32,0},{48,16},{64,96},{80,112},{96,64},{112,80},{1... | collective-permute-start | bytes 2359304 | tf_op jit(solution)/shard_map/ppermute | solution.py:66
  89.6 8.0 %collective-permute-start.9 = (bf16[256,384]{1,0:T(8,128)(2,1)S(1)}, bf16[256,384]{1,0:T(8,128)(2,1)S(1)}, u32[]{:S(2)}, u32[]{:S(2)}) collective-permute-start(bf16[256,384]{1,0:T(8,128)(2,1)S(1)} %pad_maximum_fusion.2), channel_id=1, source_target_pairs={{0,12},{4,8},{8,4},{12,0},{1,13},{5,9},{9,5},{13,1},{2,14},{6,10},... | collective-permute-start | bytes 589832 | tf_op jit(solution)/shard_map/ppermute | solution.py:66
  93.0 6.2 %collective-permute-start.8 = (bf16[256,384]{1,0:T(8,128)(2,1)S(1)}, bf16[256,384]{1,0:T(8,128)(2,1)S(1)}, u32[]{:S(2)}, u32[]{:S(2)}) collective-permute-start(bf16[256,384]{1,0:T(8,128)(2,1)S(1)} %pad_maximum_fusion.2), channel_id=1, source_target_pairs={{0,8},{4,12},{8,0},{12,4},{1,9},{5,13},{9,1},{13,5},{2,10},{6,14},... | collective-permute-start | bytes 589832 | tf_op jit(solution)/shard_map/ppermute | solution.py:66
  93.0 6.4 %collective-permute-start.7 = (bf16[256,384]{1,0:T(8,128)(2,1)S(1)}, bf16[256,384]{1,0:T(8,128)(2,1)S(1)}, u32[]{:S(2)}, u32[]{:S(2)}) collective-permute-start(bf16[256,384]{1,0:T(8,128)(2,1)S(1)} %pad_maximum_fusion.2), channel_id=1, source_target_pairs={{0,4},{4,0},{8,12},{12,8},{1,5},{5,1},{9,13},{13,9},{2,6},{6,2},{1... | collective-permute-start | bytes 589832 | tf_op jit(solution)/shard_map/ppermute | solution.py:66
  110.7 11.7 %collective-permute-start.13 = (bf16[1,768,256]{2,1,0:T(8,128)(2,1)}, bf16[1,768,256]{2,1,0:T(8,128)(2,1)}, u32[]{:S(2)}, u32[]{:S(2)}) collective-permute-start(bf16[1,768,256]{2,1,0:T(8,128)(2,1)} %get-tuple-element.38.refs_0_), channel_id=1, source_target_pairs={{0,32},{16,48},{32,0},{48,16},{64,96},{80,112},{96,64},{112,80},{1... | collective-permute-start | bytes 1179656 | tf_op jit(solution)/shard_map/ppermute | solution.py:66
  112.5 13.4 %collective-permute-start.15 = (bf16[2,768,256]{2,1,0:T(8,128)(2,1)S(1)}, bf16[2,768,256]{2,1,0:T(8,128)(2,1)S(1)}, u32[]{:S(2)}, u32[]{:S(2)}) collective-permute-start(bf16[2,768,256]{2,1,0:T(8,128)(2,1)S(1)} %copy-done.7), channel_id=1, source_target_pairs={{0,16},{16,0},{32,48},{48,32},{64,80},{80,64},{96,112},{112,96},{1... | collective-permute-start | bytes 2359304 | tf_op jit(solution)/shard_map/ppermute | solution.py:66
  112.5 13.4 %collective-permute-start.16 = (bf16[2,768,256]{2,1,0:T(8,128)(2,1)S(1)}, bf16[2,768,256]{2,1,0:T(8,128)(2,1)S(1)}, u32[]{:S(2)}, u32[]{:S(2)}) collective-permute-start(bf16[2,768,256]{2,1,0:T(8,128)(2,1)S(1)} %collective-permute-done.12.refs_2_), channel_id=1, source_target_pairs={{0,16},{16,0},{32,48},{48,32},{64,80},{80,64},{96,112},{112,96},{1... | collective-permute-start | bytes 2359304 | tf_op jit(solution)/shard_map/ppermute | solution.py:66
  113.6 10.1 %collective-permute-start.10 = (s32[8,128]{1,0:T(8,128)S(1)}, s32[8,128]{1,0:T(8,128)S(1)}, u32[]{:S(2)}, u32[]{:S(2)}) collective-permute-start(s32[8,128]{1,0:T(8,128)S(1)} %broadcast_in_dim.34), channel_id=1, source_target_pairs={{0,0},{1,32},{2,48},{3,16},{16,34},{17,2},{18,18},{19,50},{32,1},{... | collective-permute-start | bytes 12296 | tf_op jit(solution)/shard_map/ppermute | solution.py:43
  120.6 17.9 %collective-permute-start.11 = (bf16[1,768,256]{2,1,0:T(8,128)(2,1)}, bf16[1,768,256]{2,1,0:T(8,128)(2,1)}, u32[]{:S(2)}, u32[]{:S(2)}) collective-permute-start(bf16[1,768,256]{2,1,0:T(8,128)(2,1)} %get-tuple-element.38.refs_0_), channel_id=1, source_target_pairs={{0,16},{16,0},{32,48},{48,32},{64,80},{80,64},{96,112},{112,96},{1... | collective-permute-start | bytes 1179656 | tf_op jit(solution)/shard_map/ppermute | solution.py:66
  122.4 16.1 %collective-permute-start.14 = (bf16[1,768,256]{2,1,0:T(8,128)(2,1)}, bf16[1,768,256]{2,1,0:T(8,128)(2,1)}, u32[]{:S(2)}, u32[]{:S(2)}) collective-permute-start(bf16[1,768,256]{2,1,0:T(8,128)(2,1)} %collective-permute-done.13.refs_2_), channel_id=1, source_target_pairs={{0,16},{16,0},{32,48},{48,32},{64,80},{80,64},{96,112},{112,96},{1... | collective-permute-start | bytes 1179656 | tf_op jit(solution)/shard_map/ppermute | solution.py:66
  145.5 19.4 %collective-permute-start.17 = (bf16[192,384]{1,0:T(8,128)(2,1)}, bf16[192,384]{1,0:T(8,128)(2,1)S(1)}, u32[]{:S(2)}, u32[]{:S(2)}) collective-permute-start(bf16[192,384]{1,0:T(8,128)(2,1)} %get-tuple-element.44), channel_id=1, source_target_pairs={{0,0},{4,4},{8,8},{12,12},{32,1},{36,5},{40,9},{44,13},{48,2},{52,... | collective-permute-start | bytes 442376 | tf_op jit(solution)/shard_map/ppermute | solution.py:56
  151.6 14.2 %collective-permute-start.18 = (bf16[192,384]{1,0:T(8,128)(2,1)}, bf16[192,384]{1,0:T(8,128)(2,1)S(1)}, u32[]{:S(2)}, u32[]{:S(2)}) collective-permute-start(bf16[192,384]{1,0:T(8,128)(2,1)} %get-tuple-element.45), channel_id=1, source_target_pairs={{0,4},{4,0},{8,12},{12,8},{32,5},{36,1},{40,13},{44,9},{48,6},{52,... | collective-permute-start | bytes 442376 | tf_op jit(solution)/shard_map/ppermute | solution.py:56
  158.5 12.3 %collective-permute-start.19 = (bf16[192,384]{1,0:T(8,128)(2,1)}, bf16[192,384]{1,0:T(8,128)(2,1)S(1)}, u32[]{:S(2)}, u32[]{:S(2)}) collective-permute-start(bf16[192,384]{1,0:T(8,128)(2,1)} %get-tuple-element.46), channel_id=1, source_target_pairs={{0,8},{4,12},{8,0},{12,4},{32,9},{36,13},{40,1},{44,5},{48,10},{52... | collective-permute-start | bytes 442376 | tf_op jit(solution)/shard_map/ppermute | solution.py:56
  159.7 11.1 %collective-permute-start.20 = (bf16[192,384]{1,0:T(8,128)(2,1)}, bf16[192,384]{1,0:T(8,128)(2,1)S(1)}, u32[]{:S(2)}, u32[]{:S(2)}) collective-permute-start(bf16[192,384]{1,0:T(8,128)(2,1)} %get-tuple-element.47), channel_id=1, source_target_pairs={{0,12},{4,8},{8,4},{12,0},{32,13},{36,9},{40,5},{44,1},{48,14},{52... | collective-permute-start | bytes 442376 | tf_op jit(solution)/shard_map/ppermute | solution.py:56
  177.0 7.3 %collective-permute-start.23 = (bf16[64,1280]{1,0:T(8,128)(2,1)}, bf16[64,1280]{1,0:T(8,128)(2,1)S(1)}, u32[]{:S(2)}, u32[]{:S(2)}) collective-permute-start(bf16[64,1280]{1,0:T(8,128)(2,1)} %get-tuple-element.53), channel_id=1, source_target_pairs={{0,12},{4,8},{8,4},{12,0},{1,13},{5,9},{9,5},{13,1},{2,14},{6,10},... | collective-permute-start | bytes 491528 | tf_op jit(solution)/shard_map/ppermute | solution.py:66
  178.1 6.2 %collective-permute-start.22 = (bf16[64,1280]{1,0:T(8,128)(2,1)}, bf16[64,1280]{1,0:T(8,128)(2,1)S(1)}, u32[]{:S(2)}, u32[]{:S(2)}) collective-permute-start(bf16[64,1280]{1,0:T(8,128)(2,1)} %get-tuple-element.52), channel_id=1, source_target_pairs={{0,8},{4,12},{8,0},{12,4},{1,9},{5,13},{9,1},{13,5},{2,10},{6,14},... | collective-permute-start | bytes 491528 | tf_op jit(solution)/shard_map/ppermute | solution.py:66
  185.9 16.7 %collective-permute-start.24 = (f32[16,1280]{1,0:T(8,128)S(1)}, f32[16,1280]{1,0:T(8,128)S(1)}, u32[]{:S(2)}, u32[]{:S(2)}) collective-permute-start(f32[16,1280]{1,0:T(8,128)S(1)} %get-tuple-element.64), channel_id=1, source_target_pairs={{0,1},{1,0},{2,3},{3,2},{4,5},{5,4},{6,7},{7,6},{8,9},{9,8},{10,11... | collective-permute-start | bytes 245768 | tf_op jit(solution)/shard_map/ppermute | solution.py:66
  190.9 11.8 %collective-permute-start.25 = (f32[16,1280]{1,0:T(8,128)S(1)}, f32[16,1280]{1,0:T(8,128)S(1)}, u32[]{:S(2)}, u32[]{:S(2)}) collective-permute-start(f32[16,1280]{1,0:T(8,128)S(1)} %get-tuple-element.63), channel_id=1, source_target_pairs={{0,2},{1,3},{2,0},{3,1},{4,6},{5,7},{6,4},{7,5},{8,10},{9,11},{10,... | collective-permute-start | bytes 245768 | tf_op jit(solution)/shard_map/ppermute | solution.py:66
  190.9 11.8 %collective-permute-start.26 = (f32[16,1280]{1,0:T(8,128)S(1)}, f32[16,1280]{1,0:T(8,128)S(1)}, u32[]{:S(2)}, u32[]{:S(2)}) collective-permute-start(f32[16,1280]{1,0:T(8,128)S(1)} %get-tuple-element.62), channel_id=1, source_target_pairs={{0,3},{1,2},{2,1},{3,0},{4,7},{5,6},{6,5},{7,4},{8,11},{9,10},{10,... | collective-permute-start | bytes 245768 | tf_op jit(solution)/shard_map/ppermute | solution.py:66
  205.5 6.4 %collective-permute-start.29 = (f32[16,1152]{1,0:T(8,128)S(1)}, f32[16,1152]{1,0:T(8,128)S(1)}, u32[]{:S(2)}, u32[]{:S(2)}) collective-permute-start(f32[16,1152]{1,0:T(8,128)S(1)} %slice_multiply_fusion), channel_id=1, source_target_pairs={{0,192},{16,208},{32,224},{48,240},{64,128},{80,144},{96,160},{112... | collective-permute-start | bytes 221192 | tf_op jit(solution)/shard_map/ppermute | solution.py:66
  219.3 5.7 %collective-permute-start.32 = (bf16[16,1152]{1,0:T(8,128)(2,1)S(1)}, bf16[16,1152]{1,0:T(8,128)(2,1)S(1)}, u32[]{:S(2)}, u32[]{:S(2)}) collective-permute-start(bf16[16,1152]{1,0:T(8,128)(2,1)S(1)} %add_convert_fusion.refs_0_), channel_id=1, source_target_pairs={{0,1},{1,0},{2,3},{3,2},{4,5},{5,4},{6,7},{7,6},{8,9},{9,8},{10,11... | collective-permute-start | bytes 110600 | tf_op jit(solution)/shard_map/ppermute | solution.py:66
  219.8 6.8 %collective-permute-start.33 = (bf16[16,1152]{1,0:T(8,128)(2,1)S(1)}, bf16[16,1152]{1,0:T(8,128)(2,1)S(1)}, u32[]{:S(2)}, u32[]{:S(2)}) collective-permute-start(bf16[16,1152]{1,0:T(8,128)(2,1)S(1)} %add_convert_fusion.refs_0_), channel_id=1, source_target_pairs={{0,2},{1,3},{2,0},{3,1},{4,6},{5,7},{6,4},{7,5},{8,10},{9,11},{10,... | collective-permute-start | bytes 110600 | tf_op jit(solution)/shard_map/ppermute | solution.py:66
  231.2 5.7 %collective-permute-start.36 = (bf16[64,768]{1,0:T(8,128)(2,1)}, bf16[64,768]{1,0:T(8,128)(2,1)S(1)}, u32[]{:S(2)}, u32[]{:S(2)}) collective-permute-start(bf16[64,768]{1,0:T(8,128)(2,1)} %get-tuple-element.59.refs_0_), channel_id=1, source_target_pairs={{0,8},{4,12},{8,0},{12,4},{1,9},{5,13},{9,1},{13,5},{2,10},{6,14},... | collective-permute-start | bytes 294920 | tf_op jit(solution)/shard_map/ppermute | solution.py:66
  (38 other events, 282.8 us)
Sparse Core Ops, SparseCore 0:
  10.4 62.0 all-gather.2
  103.5 68.0 all-gather.4
